TPU v7x, 32 devices: a whole 2x2x4 slice. The times are simulated.
32 devices in a mesh: occ: 4 (over z), va: 2 (over x), vb: 4 (over y, core).
Axes of the slice: x: 2, y: 2, z: 4, core: 2. Of those that a mesh axis runs over, the one named last changes fastest.
Arguments:
- aux_factors: bfloat16 [4, 1024, 2048], P('occ', ('vb', 'va')), may hold values from -0.59765625 to 0.59765625
- occ_energy: float32 [4], replicated, may hold values from -2 to -0.5
- vir_energy: float32 [1024], replicated, may hold values from 0.5 to 3
- occ_index: int32 [4], replicated, may hold values from 0 to 3, each once
- vir_index: int32 [1024], replicated, may hold values from 0 to 1023, each once
Outputs:
- gamma_aux: float32 [4, 1024, 2048], P('occ', ('vb', 'va'))
Inputs may be any that keep to these rules, and one draw needn't show every extreme that they name: `occ_index`: each occupied table row appears exactly once. `vir_index`: each virtual table row appears exactly once.
All inputs are finite; a program needn't handle non-finite values.
Results may differ from a plain program's by a relative error of at most 0.0017.
Values may be sent and summed in bfloat16 or wider, within the bound.
No kernel may reach another device: no remote copies, remote signals or barrier semaphores. Data moves between devices by JAX's collectives and lax.ppermute only.
A program may use at most 64 MiB of HBM per device.

v0:
```python
import functools

import jax
import jax.numpy as jnp
from jax import lax
from jax.experimental import pallas as pl
from jax.experimental.pallas import tpu as pltpu
from jax.sharding import PartitionSpec as P


STEPS = 4
CORES = 2

NT = (((1,), (1,)), ((), ()))


def prepare(sizes, partner, index_ref, vir_ref, occ_index_ref, occ_ref, pair_ref, row_ref, col_ref):
    va_count, chip_count, occ_count = sizes
    va, vb, occ = lax.axis_index("va"), lax.axis_index("vb"), lax.axis_index("occ")
    core, chip = lax.rem(vb, CORES), vb // CORES
    index = index_ref[...]
    width = index.shape[1]

    def step(k, found):
        return found + jnp.where(index == k, vir_ref[k], 0.0)

    energy = lax.fori_loop(
        0, vir_ref.shape[0], step, jnp.zeros(index.shape, jnp.float32), unroll=16
    )

    def block(dx, dy, flip):
        other = lax.rem(chip - dy + chip_count, chip_count) * CORES + lax.rem(core + flip, CORES)
        mine = other * va_count + lax.rem(va - dx + va_count, va_count)
        picked = lax.broadcasted_iota(jnp.int32, index.shape, 0) == mine
        return jnp.sum(jnp.where(picked, energy, 0.0), axis=0, keepdims=True)

    for flip in range(CORES):
        spread = jnp.broadcast_to(block(0, 0, flip), (width, width))
        row_ref[flip * width : (flip + 1) * width, :] = jnp.transpose(spread)
    for dx in range(va_count):
        for dy in range(chip_count):
            p = dx * chip_count + dy
            col_ref[p : p + 1, :] = block(dx, dy, 0)
    for d in range(STEPS):
        far = partner(occ, d, occ_count)
        pair_ref[d] = occ_ref[occ_index_ref[occ]] + occ_ref[occ_index_ref[far]]


def contract(blocks, first, *refs):
    refs = list(refs)
    pair_energy, row_energy, col_energy = (refs.pop(0) for _ in range(3))
    rows = [refs.pop(0), refs.pop(0)]
    near = {p: refs.pop(0) for p in sorted({p for d, ps in blocks for p in ps if d > 0})}
    far_rows = {d: [refs.pop(0), refs.pop(0)] for d, _ in blocks if d > 0}
    far = {(d, p): refs.pop(0) for d, ps in blocks for p in ps}
    sums_in = None if first else [refs.pop(0), refs.pop(0)]
    sums_out = refs
    count = rows[0].shape[0]

    def stack(parts):
        return jnp.concatenate([r[...] for r in parts], axis=0)

    own = stack(rows)
    weights = []
    for d, ps in blocks:
        direct = lax.dot_general(
            own, stack([far[d, p] for p in ps]), NT, preferred_element_type=jnp.float32
        )
        if d > 0:
            swapped = lax.dot_general(
                stack(far_rows[d]), stack([near[p] for p in ps]), NT,
                preferred_element_type=jnp.float32,
            )
        else:
            swapped = direct
        for k, p in enumerate(ps):
            cut = slice(k * count, (k + 1) * count)
            gap = pair_energy[d] - row_energy[...] - col_energy[p : p + 1, :]
            weights.append(((2.0 * direct[:, cut] - swapped[:, cut]) / gap).astype(jnp.bfloat16))
    weights = jnp.concatenate(weights, axis=1)
    columns = stack([far[d, p] for d, ps in blocks for p in ps])
    for half in range(CORES):
        part = jnp.dot(
            weights[half * count : (half + 1) * count], columns, preferred_element_type=jnp.float32
        )
        sums_out[half][...] = part if first else sums_in[half][...] + part


def per_device(aux_factors, occ_energy, vir_energy, occ_index, vir_index):
    va_count = lax.axis_size("va")
    vb_count = lax.axis_size("vb")
    occ_count = lax.axis_size("occ")
    chip_count = vb_count // CORES
    occ_rows, width, aux_width = aux_factors.shape
    assert occ_rows == 1 and vb_count % CORES == 0
    paired = occ_count == STEPS and STEPS & (STEPS - 1) == 0

    def partner(i, step, count):
        return i ^ step if paired else (i + count - step) % count

    def from_va(block, step):
        return lax.ppermute(block, "va", [((i - step) % va_count, i) for i in range(va_count)])

    def from_vb(block, step):
        move = step * CORES
        return lax.ppermute(block, "vb", [((i - move) % vb_count, i) for i in range(vb_count)])

    def from_core(block):
        return lax.ppermute(block, "vb", [(i ^ 1, i) for i in range(vb_count)])

    def from_occ(block, step):
        return lax.ppermute(
            block, "occ", [(partner(i, step, occ_count), i) for i in range(occ_count)]
        )

    own = aux_factors[0]
    line = {0: own}
    for d in range(1, STEPS):
        low = d & -d
        line[d] = from_occ(line[d - low], low)
    other = {d: from_core(line[d]) for d in range(STEPS)}
    plane_of = {(dx, dy): dx * chip_count + dy for dx in range(va_count) for dy in range(chip_count)}
    held = {}
    for d in range(STEPS):
        for (dx, dy), p in plane_of.items():
            if dx == 0 and dy == 0:
                held[d, p] = line[d]
            elif dy == 0:
                held[d, p] = from_va(line[d], dx)
            elif dx == 0:
                held[d, p] = from_vb(line[d], dy)
    for d in range(STEPS):
        for (dx, dy), p in plane_of.items():
            if dx > 0 and dy > 0:
                if d % 2 == 1:
                    held[d, p] = from_occ(held[d - 1, p], 1)
                elif d == 0:
                    held[d, p] = from_va(held[d, plane_of[0, dy]], dx)
                else:
                    held[d, p] = from_vb(held[d, plane_of[dx, 0]], dy)

    whole = pl.BlockSpec(memory_space=pltpu.VMEM)
    scalar = pl.BlockSpec(memory_space=pltpu.SMEM)
    f32 = jnp.float32

    def energies():
        return pl.pallas_call(
            functools.partial(prepare, (va_count, chip_count, occ_count), partner),
            out_shape=(
                jax.ShapeDtypeStruct((STEPS,), f32),
                jax.ShapeDtypeStruct((CORES * width, width), f32),
                jax.ShapeDtypeStruct((len(plane_of), width), f32),
            ),
            in_specs=[whole, scalar, scalar, scalar],
            out_specs=(scalar, whole, whole),
            cost_estimate=pl.CostEstimate(
                flops=3 * vir_index.shape[0] ** 2, bytes_accessed=1 << 18, transcendentals=0
            ),
        )(vir_index.reshape(-1, width), vir_energy, occ_index, occ_energy)

    tables = energies()
    total = jax.ShapeDtypeStruct((width, aux_width), f32)

    def add(blocks, sums):
        operands = [*tables, own, other[0]]
        operands += [held[0, p] for p in sorted({p for d, ps in blocks for p in ps if d > 0})]
        for d, _ in blocks:
            operands += [line[d], other[d]] if d > 0 else []
        operands += [held[d, p] for d, ps in blocks for p in ps]
        aliases = {}
        if sums is not None:
            aliases = {len(operands) + k: k for k in range(CORES)}
            operands += list(sums)
        count = sum(len(ps) for _, ps in blocks)
        return pl.pallas_call(
            functools.partial(contract, blocks, sums is None),
            out_shape=(total, total),
            in_specs=[scalar] + [whole] * (len(operands) - 1),
            out_specs=(whole, whole),
            input_output_aliases=aliases,
            cost_estimate=pl.CostEstimate(
                flops=2 * 3 * count * CORES * width * width * aux_width,
                bytes_accessed=count * width * aux_width * 4,
                transcendentals=0,
            ),
            compiler_params=pltpu.CompilerParams(vmem_limit_bytes=24 << 20),
        )(*operands)

    here = [plane_of[0, 0]]
    xs = [p for (dx, dy), p in plane_of.items() if dx > 0 and dy == 0]
    ys = [p for (dx, dy), p in plane_of.items() if dx == 0 and dy > 0]
    cs = [p for (dx, dy), p in plane_of.items() if dx > 0 and dy > 0]
    groups = (
        ((0, here + xs + ys + cs),),
        ((1, here + ys), (2, here + xs + ys)),
        ((1, xs + cs), (2, cs), (3, here)),
        ((3, xs + ys + cs),),
    )
    sums = None
    for blocks in groups:
        sums = add(blocks, sums)
    return (sums[0] + from_core(sums[1]))[None]


def solution(mesh):
    return jax.shard_map(
        per_device,
        mesh=mesh,
        in_specs=(P("occ", ("vb", "va"), None), P(), P(), P(), P()),
        out_specs=P("occ", ("vb", "va"), None),
        check_vma=False,
    )
```

profile of v0, /device:TPU:0, one launch (start us, length us, event | category | flops | bytes accessed | tf_op | source)
XLA Modules:
  0.0 95.0 jit_solution(3907008341726156224)
XLA Ops:
  0.0 3.0 %collective-permute-start.1 = (bf16[128,2048]{1,0:T(8,128)(2,1)}, bf16[128,2048]{1,0:T(8,128)(2,1)S(1)}, u32[]{:S(2)}, u32[]{:S(2)}) collective-permute-start(bf16[128,2048]{1,0:T(8,128)(2,1)} %bitcast.4), channel_id=1, source_target_pairs={{2,0},{3,1},{0,2},{1,3},{6,4},{7,5},{4,6},{5,7},{10,8},{11,9},{8,1... | collective-permute-start | bytes 1572872 | tf_op jit(solution)/shard_map/ppermute | solution.py:106
  3.0 2.6 %collective-permute-start.4 = (bf16[128,2048]{1,0:T(8,128)(2,1)}, bf16[128,2048]{1,0:T(8,128)(2,1)S(1)}, u32[]{:S(2)}, u32[]{:S(2)}) collective-permute-start(bf16[128,2048]{1,0:T(8,128)(2,1)} %bitcast.5), channel_id=1, source_target_pairs={{16,0},{24,8},{0,16},{8,24},{17,1},{25,9},{1,17},{9,25},{18,2},{26... | collective-permute-start | bytes 1572872 | tf_op jit(solution)/shard_map/ppermute | solution.py:112
  5.6 1.6 %collective-permute-start.12 = (bf16[128,2048]{1,0:T(8,128)(2,1)}, bf16[128,2048]{1,0:T(8,128)(2,1)S(1)}, u32[]{:S(2)}, u32[]{:S(2)}) collective-permute-start(bf16[128,2048]{1,0:T(8,128)(2,1)} %bitcast.7), channel_id=1, source_target_pairs={{8,0},{0,8},{24,16},{16,24},{9,1},{1,9},{25,17},{17,25},{10,2},{2,... | collective-permute-start | bytes 1572872 | tf_op jit(solution)/shard_map/ppermute | solution.py:112
  7.2 1.5 %collective-permute-start.2 = (bf16[128,2048]{1,0:T(8,128)(2,1)}, bf16[128,2048]{1,0:T(8,128)(2,1)S(1)}, u32[]{:S(2)}, u32[]{:S(2)}) collective-permute-start(bf16[128,2048]{1,0:T(8,128)(2,1)} %bitcast.8), channel_id=1, source_target_pairs={{4,0},{0,4},{5,1},{1,5},{6,2},{2,6},{7,3},{3,7},{12,8},{8,12},{13,... | collective-permute-start | bytes 1572872 | tf_op jit(solution)/shard_map/ppermute | solution.py:102
  8.7 6.5 %collective-permute-done.1.refs_7_.refs_6_.refs_5_ = bf16[128,2048]{1,0:T(8,128)(2,1)S(1)} collective-permute-done((bf16[128,2048]{1,0:T(8,128)(2,1)}, bf16[128,2048]{1,0:T(8,128)(2,1)S(1)}, u32[]{:S(2)}, u32[]{:S(2)}) %collective-permute-start.1) | collective-permute-done | bytes 524320 | tf_op jit(solution)/shard_map/ppermute | solution.py:106
  15.1 1.7 %collective-permute-start.3 = (bf16[128,2048]{1,0:T(8,128)(2,1)S(1)}, bf16[128,2048]{1,0:T(8,128)(2,1)S(1)}, u32[]{:S(2)}, u32[]{:S(2)}) collective-permute-start(bf16[128,2048]{1,0:T(8,128)(2,1)S(1)} %collective-permute-done.1.refs_7_.refs_6_.refs_5_), channel_id=1, source_target_pairs={{4,0},{0,4},{5,1},{1,5},{6,2},{2,6},{7,3},{3,7},{12,8},{8,12},{13,... | collective-permute-start | bytes 1572872 | tf_op jit(solution)/shard_map/ppermute | solution.py:102
  16.8 0.8 copy-done.1
  17.6 11.2 %collective-permute-done.4.refs_10_.refs_14_ = bf16[128,2048]{1,0:T(8,128)(2,1)S(1)} collective-permute-done((bf16[128,2048]{1,0:T(8,128)(2,1)}, bf16[128,2048]{1,0:T(8,128)(2,1)S(1)}, u32[]{:S(2)}, u32[]{:S(2)}) %collective-permute-start.4) | collective-permute-done | bytes 524320 | tf_op jit(solution)/shard_map/ppermute | solution.py:112
  28.8 1.5 %collective-permute-start.9 = (bf16[128,2048]{1,0:T(8,128)(2,1)S(1)}, bf16[128,2048]{1,0:T(8,128)(2,1)S(1)}, u32[]{:S(2)}, u32[]{:S(2)}) collective-permute-start(bf16[128,2048]{1,0:T(8,128)(2,1)S(1)} %collective-permute-done.4.refs_10_.refs_14_), channel_id=1, source_target_pairs={{4,0},{0,4},{5,1},{1,5},{6,2},{2,6},{7,3},{3,7},{12,8},{8,12},{13,... | collective-permute-start | bytes 1572872 | tf_op jit(solution)/shard_map/ppermute | solution.py:102
  31.3 2.1 %collective-permute-done.3.refs_8_.refs_7_ = bf16[128,2048]{1,0:T(8,128)(2,1)S(1)} collective-permute-done((bf16[128,2048]{1,0:T(8,128)(2,1)S(1)}, bf16[128,2048]{1,0:T(8,128)(2,1)S(1)}, u32[]{:S(2)}, u32[]{:S(2)}) %collective-permute-start.3) | collective-permute-done | bytes 524320 | tf_op jit(solution)/shard_map/ppermute | solution.py:102
  33.9 0.8 copy-done.3
  34.7 1.5 %collective-permute-start.17 = (bf16[128,2048]{1,0:T(8,128)(2,1)S(1)}, bf16[128,2048]{1,0:T(8,128)(2,1)S(1)}, u32[]{:S(2)}, u32[]{:S(2)}) collective-permute-start(bf16[128,2048]{1,0:T(8,128)(2,1)S(1)} %collective-permute-done.12.refs_8_.refs_12_), channel_id=1, source_target_pairs={{2,0},{3,1},{0,2},{1,3},{6,4},{7,5},{4,6},{5,7},{10,8},{11,9},{8,1... | collective-permute-start | bytes 1572872 | tf_op jit(solution)/shard_map/ppermute | solution.py:106
  36.2 7.7 %collective-permute-done.9.refs_15_ = bf16[128,2048]{1,0:T(8,128)(2,1)S(1)} collective-permute-done((bf16[128,2048]{1,0:T(8,128)(2,1)S(1)}, bf16[128,2048]{1,0:T(8,128)(2,1)S(1)}, u32[]{:S(2)}, u32[]{:S(2)}) %collective-permute-start.9) | collective-permute-done | bytes 524320 | tf_op jit(solution)/shard_map/ppermute | solution.py:102
  43.9 1.5 %collective-permute-start.15 = (bf16[128,2048]{1,0:T(8,128)(2,1)S(1)}, bf16[128,2048]{1,0:T(8,128)(2,1)S(1)}, u32[]{:S(2)}, u32[]{:S(2)}) collective-permute-start(bf16[128,2048]{1,0:T(8,128)(2,1)S(1)} %collective-permute-done.12.refs_8_.refs_12_), channel_id=1, source_target_pairs={{4,0},{0,4},{5,1},{1,5},{6,2},{2,6},{7,3},{3,7},{12,8},{8,12},{13,... | collective-permute-start | bytes 1572872 | tf_op jit(solution)/shard_map/ppermute | solution.py:102
  45.4 0.8 copy-done.5
  46.7 0.8 copy-done.10
  48.2 0.8 copy-done.12
  49.2 10.2 %collective-permute-done.17.refs_13_ = bf16[128,2048]{1,0:T(8,128)(2,1)S(1)} collective-permute-done((bf16[128,2048]{1,0:T(8,128)(2,1)S(1)}, bf16[128,2048]{1,0:T(8,128)(2,1)S(1)}, u32[]{:S(2)}, u32[]{:S(2)}) %collective-permute-start.17) | collective-permute-done | bytes 524320 | tf_op jit(solution)/shard_map/ppermute | solution.py:106
  59.4 0.8 copy-done.14
  60.2 1.5 %collective-permute-start.7 = (bf16[128,2048]{1,0:T(8,128)(2,1)S(1)}, bf16[128,2048]{1,0:T(8,128)(2,1)}, u32[]{:S(2)}, u32[]{:S(2)}) collective-permute-start(bf16[128,2048]{1,0:T(8,128)(2,1)S(1)} %collective-permute-done.5.refs_12_.refs_17_.refs_8_), channel_id=1, source_target_pairs={{4,0},{0,4},{5,1},{1,5},{6,2},{2,6},{7,3},{3,7},{12,8},{8,12},{13,... | collective-permute-start | bytes 1572872 | tf_op jit(solution)/shard_map/ppermute | solution.py:102
  61.7 0.8 copy-done.8
  63.0 7.7 %collective-permute-done.10.refs_16_ = bf16[128,2048]{1,0:T(8,128)(2,1)} collective-permute-done((bf16[128,2048]{1,0:T(8,128)(2,1)S(1)}, bf16[128,2048]{1,0:T(8,128)(2,1)}, u32[]{:S(2)}, u32[]{:S(2)}) %collective-permute-start.10) | collective-permute-done | bytes 524320 | tf_op jit(solution)/shard_map/ppermute | solution.py:106
  71.0 3.1 %shard_map.55 = (f32[4]{0:T(128)}, f32[256,128]{1,0:T(8,128)}, f32[4,128]{1,0:T(4,128)}) custom-call(s32[8,128]{1,0:T(8,128)} %bitcast.16, f32[1024]{0:T(1024)} %vir_ref.1, s32[4]{0:T(128)} %occ_index_ref.1, f32[4]{0:T(128)} %occ_ref.1), custom_call_target="tpu_custom_call" | custom-call | flops 3145728 | bytes 262144 | tf_op jit(solution)/shard_map/pallas_call | solution.py:147
  74.7 1.0 %copy-done = bf16[1,128,2048]{2,1,0:T(8,128)(2,1)S(1)} copy-done((bf16[1,128,2048]{2,1,0:T(8,128)(2,1)S(1)}, bf16[1,128,2048]{2,1,0:T(8,128)(2,1)}, u32[]{:S(2)}) %copy-start) | copy-done | bytes 524312
  75.8 1.0 %copy-done.2 = bf16[128,2048]{1,0:T(8,128)(2,1)S(1)} copy-done((bf16[128,2048]{1,0:T(8,128)(2,1)S(1)}, bf16[128,2048]{1,0:T(8,128)(2,1)}, u32[]{:S(2)}) %copy-start.2) | copy-done | bytes 524312
  76.8 0.9 copy-done.7
  77.7 1.9 %shard_map.56 = (f32[128,2048]{1,0:T(8,128)S(1)}, f32[128,2048]{1,0:T(8,128)S(1)}) custom-call(f32[4]{0:T(128)S(1)} %copy-done.17, f32[256,128]{1,0:T(8,128)S(1)} %copy-done.7, f32[4,128]{1,0:T(4,128)S(1)} %copy-done.16, bf16[128,2048]{1,0:T(8,128)(2,1)S(1)} %bitcast.9, bf16[128,2048]{1,0:T(8,128)(2,1)S(1)} %collective-permute-done.refs_4_, ...), custom_call_target="tpu_custom_call" | custom-call | flops 1610612736 | bytes 4194304 | tf_op jit(solution)/shard_map/pallas_call | solution.py:175
  79.7 3.6 %shard_map.57 = (f32[128,2048]{1,0:T(8,128)S(1)}, f32[128,2048]{1,0:T(8,128)S(1)}) custom-call(f32[4]{0:T(128)S(1)} %copy-done.17, f32[256,128]{1,0:T(8,128)S(1)} %copy-done.7, f32[4,128]{1,0:T(4,128)S(1)} %copy-done.16, bf16[128,2048]{1,0:T(8,128)(2,1)S(1)} %bitcast.11, ...), custom_call_target="tpu_custom_call", output_to_operand_aliasing={{0}: (17, {}), {1}: (18, {})} | custom-call | flops 2013265920 | bytes 5242880 | tf_op jit(solution)/shard_map/pallas_call | solution.py:175
  83.4 4.0 %shard_map.58 = (f32[128,2048]{1,0:T(8,128)S(1)}, f32[128,2048]{1,0:T(8,128)S(1)}) custom-call(f32[4]{0:T(128)S(1)} %copy-done.17, f32[256,128]{1,0:T(8,128)S(1)} %copy-done.7, f32[4,128]{1,0:T(4,128)S(1)} %copy-done.16, bf16[128,2048]{1,0:T(8,128)(2,1)S(1)} %bitcast.13, ...), custom_call_target="tpu_custom_call", output_to_operand_aliasing={{0}: (18, {}), {1}: (19, {})} | custom-call | flops 1610612736 | bytes 4194304 | tf_op jit(solution)/shard_map/pallas_call | solution.py:175
  87.4 3.7 %shard_map.59 = (f32[128,2048]{1,0:T(8,128)S(1)}, f32[128,2048]{1,0:T(8,128)S(1)}) custom-call(f32[4]{0:T(128)S(1)} %copy-done.17, f32[256,128]{1,0:T(8,128)S(1)} %copy-done.7, f32[4,128]{1,0:T(4,128)S(1)} %copy-done.16, bf16[128,2048]{1,0:T(8,128)(2,1)S(1)} %bitcast.15, ...), custom_call_target="tpu_custom_call", output_to_operand_aliasing={{0}: (13, {}), {1}: (14, {})} | custom-call | flops 1207959552 | bytes 3145728 | tf_op jit(solution)/shard_map/pallas_call | solution.py:175
  91.2 2.6 %collective-permute-done.19 = f32[128,2048]{1,0:T(8,128)S(1)} collective-permute-done((f32[128,2048]{1,0:T(8,128)S(1)}, f32[128,2048]{1,0:T(8,128)S(1)}, u32[]{:S(2)}, u32[]{:S(2)}) %collective-permute-start.19) | collective-permute-done | bytes 1048608 | tf_op jit(solution)/shard_map/ppermute | solution.py:109
  93.9 1.1 %add_bitcast_fusion = f32[1,128,2048]{2,1,0:T(8,128)} fusion(f32[128,2048]{1,0:T(8,128)S(1)} %get-tuple-element.25, f32[128,2048]{1,0:T(8,128)S(1)} %collective-permute-done.19), kind=kLoop, calls=%fused_computation | loop fusion | flops 262144 | bytes 3145728 | tf_op jit(solution)/shard_map/broadcast_in_dim | solution.py:202
  (50 shorter events, 4.4 us)
Async XLA Ops:
  0.0 15.1 %collective-permute-start.1 = (bf16[128,2048]{1,0:T(8,128)(2,1)}, bf16[128,2048]{1,0:T(8,128)(2,1)S(1)}, u32[]{:S(2)}, u32[]{:S(2)}) collective-permute-start(bf16[128,2048]{1,0:T(8,128)(2,1)} %bitcast.4), channel_id=1, source_target_pairs={{2,0},{3,1},{0,2},{1,3},{6,4},{7,5},{4,6},{5,7},{10,8},{11,9},{8,1... | collective-permute-start | bytes 1572872 | tf_op jit(solution)/shard_map/ppermute | solution.py:106
  3.0 25.8 %collective-permute-start.4 = (bf16[128,2048]{1,0:T(8,128)(2,1)}, bf16[128,2048]{1,0:T(8,128)(2,1)S(1)}, u32[]{:S(2)}, u32[]{:S(2)}) collective-permute-start(bf16[128,2048]{1,0:T(8,128)(2,1)} %bitcast.5), channel_id=1, source_target_pairs={{16,0},{24,8},{0,16},{8,24},{17,1},{25,9},{1,17},{9,25},{18,2},{26... | collective-permute-start | bytes 1572872 | tf_op jit(solution)/shard_map/ppermute | solution.py:112
  5.6 23.3 %collective-permute-start = (bf16[128,2048]{1,0:T(8,128)(2,1)}, bf16[128,2048]{1,0:T(8,128)(2,1)S(1)}, u32[]{:S(2)}, u32[]{:S(2)}) collective-permute-start(bf16[128,2048]{1,0:T(8,128)(2,1)} %bitcast.6), channel_id=1, source_target_pairs={{1,0},{0,1},{3,2},{2,3},{5,4},{4,5},{7,6},{6,7},{9,8},{8,9},{11,10... | collective-permute-start | bytes 1572872 | tf_op jit(solution)/shard_map/ppermute | solution.py:109
  5.6 24.8 %collective-permute-start.12 = (bf16[128,2048]{1,0:T(8,128)(2,1)}, bf16[128,2048]{1,0:T(8,128)(2,1)S(1)}, u32[]{:S(2)}, u32[]{:S(2)}) collective-permute-start(bf16[128,2048]{1,0:T(8,128)(2,1)} %bitcast.7), channel_id=1, source_target_pairs={{8,0},{0,8},{24,16},{16,24},{9,1},{1,9},{25,17},{17,25},{10,2},{2,... | collective-permute-start | bytes 1572872 | tf_op jit(solution)/shard_map/ppermute | solution.py:112
  7.2 23.4 %collective-permute-start.2 = (bf16[128,2048]{1,0:T(8,128)(2,1)}, bf16[128,2048]{1,0:T(8,128)(2,1)S(1)}, u32[]{:S(2)}, u32[]{:S(2)}) collective-permute-start(bf16[128,2048]{1,0:T(8,128)(2,1)} %bitcast.8), channel_id=1, source_target_pairs={{4,0},{0,4},{5,1},{1,5},{6,2},{2,6},{7,3},{3,7},{12,8},{8,12},{13,... | collective-permute-start | bytes 1572872 | tf_op jit(solution)/shard_map/ppermute | solution.py:102
  15.1 18.3 %collective-permute-start.3 = (bf16[128,2048]{1,0:T(8,128)(2,1)S(1)}, bf16[128,2048]{1,0:T(8,128)(2,1)S(1)}, u32[]{:S(2)}, u32[]{:S(2)}) collective-permute-start(bf16[128,2048]{1,0:T(8,128)(2,1)S(1)} %collective-permute-done.1.refs_7_.refs_6_.refs_5_), channel_id=1, source_target_pairs={{4,0},{0,4},{5,1},{1,5},{6,2},{2,6},{7,3},{3,7},{12,8},{8,12},{13,... | collective-permute-start | bytes 1572872 | tf_op jit(solution)/shard_map/ppermute | solution.py:102
  28.8 5.1 %collective-permute-start.14 = (bf16[128,2048]{1,0:T(8,128)(2,1)S(1)}, bf16[128,2048]{1,0:T(8,128)(2,1)S(1)}, u32[]{:S(2)}, u32[]{:S(2)}) collective-permute-start(bf16[128,2048]{1,0:T(8,128)(2,1)S(1)} %collective-permute-done.4.refs_10_.refs_14_), channel_id=1, source_target_pairs={{1,0},{0,1},{3,2},{2,3},{5,4},{4,5},{7,6},{6,7},{9,8},{8,9},{11,10... | collective-permute-start | bytes 1572872 | tf_op jit(solution)/shard_map/ppermute | solution.py:109
  28.8 15.1 %collective-permute-start.9 = (bf16[128,2048]{1,0:T(8,128)(2,1)S(1)}, bf16[128,2048]{1,0:T(8,128)(2,1)S(1)}, u32[]{:S(2)}, u32[]{:S(2)}) collective-permute-start(bf16[128,2048]{1,0:T(8,128)(2,1)S(1)} %collective-permute-done.4.refs_10_.refs_14_), channel_id=1, source_target_pairs={{4,0},{0,4},{5,1},{1,5},{6,2},{2,6},{7,3},{3,7},{12,8},{8,12},{13,... | collective-permute-start | bytes 1572872 | tf_op jit(solution)/shard_map/ppermute | solution.py:102
  30.3 15.1 %collective-permute-start.13 = (bf16[128,2048]{1,0:T(8,128)(2,1)S(1)}, bf16[128,2048]{1,0:T(8,128)(2,1)S(1)}, u32[]{:S(2)}, u32[]{:S(2)}) collective-permute-start(bf16[128,2048]{1,0:T(8,128)(2,1)S(1)} %collective-permute-done.12.refs_8_.refs_12_), channel_id=1, source_target_pairs={{1,0},{0,1},{3,2},{2,3},{5,4},{4,5},{7,6},{6,7},{9,8},{8,9},{11,10... | collective-permute-start | bytes 1572872 | tf_op jit(solution)/shard_map/ppermute | solution.py:109
  30.6 16.9 %collective-permute-start.5 = (bf16[128,2048]{1,0:T(8,128)(2,1)S(1)}, bf16[128,2048]{1,0:T(8,128)(2,1)S(1)}, u32[]{:S(2)}, u32[]{:S(2)}) collective-permute-start(bf16[128,2048]{1,0:T(8,128)(2,1)S(1)} %collective-permute-done.4.refs_10_.refs_14_), channel_id=1, source_target_pairs={{8,0},{0,8},{24,16},{16,24},{9,1},{1,9},{25,17},{17,25},{10,2},{2,... | collective-permute-start | bytes 1572872 | tf_op jit(solution)/shard_map/ppermute | solution.py:112
  33.4 14.8 %collective-permute-start.18 = (bf16[128,2048]{1,0:T(8,128)(2,1)S(1)}, bf16[128,2048]{1,0:T(8,128)(2,1)S(1)}, u32[]{:S(2)}, u32[]{:S(2)}) collective-permute-start(bf16[128,2048]{1,0:T(8,128)(2,1)S(1)} %collective-permute-done.4.refs_10_.refs_14_), channel_id=1, source_target_pairs={{2,0},{3,1},{0,2},{1,3},{6,4},{7,5},{4,6},{5,7},{10,8},{11,9},{8,1... | collective-permute-start | bytes 1572872 | tf_op jit(solution)/shard_map/ppermute | solution.py:106
  34.7 24.7 %collective-permute-start.17 = (bf16[128,2048]{1,0:T(8,128)(2,1)S(1)}, bf16[128,2048]{1,0:T(8,128)(2,1)S(1)}, u32[]{:S(2)}, u32[]{:S(2)}) collective-permute-start(bf16[128,2048]{1,0:T(8,128)(2,1)S(1)} %collective-permute-done.12.refs_8_.refs_12_), channel_id=1, source_target_pairs={{2,0},{3,1},{0,2},{1,3},{6,4},{7,5},{4,6},{5,7},{10,8},{11,9},{8,1... | collective-permute-start | bytes 1572872 | tf_op jit(solution)/shard_map/ppermute | solution.py:106
  43.9 17.8 %collective-permute-start.15 = (bf16[128,2048]{1,0:T(8,128)(2,1)S(1)}, bf16[128,2048]{1,0:T(8,128)(2,1)S(1)}, u32[]{:S(2)}, u32[]{:S(2)}) collective-permute-start(bf16[128,2048]{1,0:T(8,128)(2,1)S(1)} %collective-permute-done.12.refs_8_.refs_12_), channel_id=1, source_target_pairs={{4,0},{0,4},{5,1},{1,5},{6,2},{2,6},{7,3},{3,7},{12,8},{8,12},{13,... | collective-permute-start | bytes 1572872 | tf_op jit(solution)/shard_map/ppermute | solution.py:102
  45.4 0.8 copy-start.5
  46.2 24.5 %collective-permute-start.10 = (bf16[128,2048]{1,0:T(8,128)(2,1)S(1)}, bf16[128,2048]{1,0:T(8,128)(2,1)}, u32[]{:S(2)}, u32[]{:S(2)}) collective-permute-start(bf16[128,2048]{1,0:T(8,128)(2,1)S(1)} %collective-permute-done.9.refs_15_), channel_id=1, source_target_pairs={{2,0},{3,1},{0,2},{1,3},{6,4},{7,5},{4,6},{5,7},{10,8},{11,9},{8,1... | collective-permute-start | bytes 1572872 | tf_op jit(solution)/shard_map/ppermute | solution.py:106
  47.5 35.8 %collective-permute-start.6 = (bf16[128,2048]{1,0:T(8,128)(2,1)S(1)}, bf16[128,2048]{1,0:T(8,128)(2,1)}, u32[]{:S(2)}, u32[]{:S(2)}) collective-permute-start(bf16[128,2048]{1,0:T(8,128)(2,1)S(1)} %collective-permute-done.5.refs_12_.refs_17_.refs_8_), channel_id=1, source_target_pairs={{1,0},{0,1},{3,2},{2,3},{5,4},{4,5},{7,6},{6,7},{9,8},{8,9},{11,10... | collective-permute-start | bytes 1572872 | tf_op jit(solution)/shard_map/ppermute | solution.py:109
  48.2 0.8 copy-start.12
  49.0 34.3 %collective-permute-start.16 = (bf16[128,2048]{1,0:T(8,128)(2,1)S(1)}, bf16[128,2048]{1,0:T(8,128)(2,1)}, u32[]{:S(2)}, u32[]{:S(2)}) collective-permute-start(bf16[128,2048]{1,0:T(8,128)(2,1)S(1)} %collective-permute-done.3.refs_8_.refs_7_), channel_id=1, source_target_pairs={{8,0},{0,8},{24,16},{16,24},{9,1},{1,9},{25,17},{17,25},{10,2},{2,... | collective-permute-start | bytes 1572872 | tf_op jit(solution)/shard_map/ppermute | solution.py:112
  60.2 27.2 %collective-permute-start.7 = (bf16[128,2048]{1,0:T(8,128)(2,1)S(1)}, bf16[128,2048]{1,0:T(8,128)(2,1)}, u32[]{:S(2)}, u32[]{:S(2)}) collective-permute-start(bf16[128,2048]{1,0:T(8,128)(2,1)S(1)} %collective-permute-done.5.refs_12_.refs_17_.refs_8_), channel_id=1, source_target_pairs={{4,0},{0,4},{5,1},{1,5},{6,2},{2,6},{7,3},{3,7},{12,8},{8,12},{13,... | collective-permute-start | bytes 1572872 | tf_op jit(solution)/shard_map/ppermute | solution.py:102
  61.7 0.8 copy-start.8
  62.5 24.9 %collective-permute-start.8 = (bf16[128,2048]{1,0:T(8,128)(2,1)S(1)}, bf16[128,2048]{1,0:T(8,128)(2,1)}, u32[]{:S(2)}, u32[]{:S(2)}) collective-permute-start(bf16[128,2048]{1,0:T(8,128)(2,1)S(1)} %collective-permute-done.5.refs_12_.refs_17_.refs_8_), channel_id=1, source_target_pairs={{2,0},{3,1},{0,2},{1,3},{6,4},{7,5},{4,6},{5,7},{10,8},{11,9},{8,1... | collective-permute-start | bytes 1572872 | tf_op jit(solution)/shard_map/ppermute | solution.py:106
  70.8 16.7 %collective-permute-start.11 = (bf16[128,2048]{1,0:T(8,128)(2,1)}, bf16[128,2048]{1,0:T(8,128)(2,1)}, u32[]{:S(2)}, u32[]{:S(2)}) collective-permute-start(bf16[128,2048]{1,0:T(8,128)(2,1)} %collective-permute-done.10.refs_16_), channel_id=1, source_target_pairs={{8,0},{0,8},{24,16},{16,24},{9,1},{1,9},{25,17},{17,25},{10,2},{2,... | collective-permute-start | bytes 1572872 | tf_op jit(solution)/shard_map/ppermute | solution.py:112
  74.7 1.0 %copy-start = (bf16[1,128,2048]{2,1,0:T(8,128)(2,1)S(1)}, bf16[1,128,2048]{2,1,0:T(8,128)(2,1)}, u32[]{:S(2)}) copy-start(bf16[1,128,2048]{2,1,0:T(8,128)(2,1)} %param.5) | copy-start | bytes 1572868
  75.8 1.0 %copy-start.2 = (bf16[128,2048]{1,0:T(8,128)(2,1)S(1)}, bf16[128,2048]{1,0:T(8,128)(2,1)}, u32[]{:S(2)}) copy-start(bf16[128,2048]{1,0:T(8,128)(2,1)} %copy-done.1) | copy-start | bytes 1572868
  76.8 0.9 copy-start.7
  77.7 2.0 %copy-start.4 = (bf16[128,2048]{1,0:T(8,128)(2,1)S(1)}, bf16[128,2048]{1,0:T(8,128)(2,1)}, u32[]{:S(2)}) copy-start(bf16[128,2048]{1,0:T(8,128)(2,1)} %copy-done.3) | copy-start | bytes 1572868
  77.7 2.0 %copy-start.6 = (bf16[128,2048]{1,0:T(8,128)(2,1)S(1)}, bf16[128,2048]{1,0:T(8,128)(2,1)}, u32[]{:S(2)}) copy-start(bf16[128,2048]{1,0:T(8,128)(2,1)} %copy-done.5) | copy-start | bytes 1572868
  77.7 2.0 %copy-start.11 = (bf16[128,2048]{1,0:T(8,128)(2,1)S(1)}, bf16[128,2048]{1,0:T(8,128)(2,1)}, u32[]{:S(2)}) copy-start(bf16[128,2048]{1,0:T(8,128)(2,1)} %copy-done.10) | copy-start | bytes 1572868
  77.7 2.0 %copy-start.13 = (bf16[128,2048]{1,0:T(8,128)(2,1)S(1)}, bf16[128,2048]{1,0:T(8,128)(2,1)}, u32[]{:S(2)}) copy-start(bf16[128,2048]{1,0:T(8,128)(2,1)} %copy-done.12) | copy-start | bytes 1572868
  77.7 2.0 %copy-start.15 = (bf16[128,2048]{1,0:T(8,128)(2,1)S(1)}, bf16[128,2048]{1,0:T(8,128)(2,1)}, u32[]{:S(2)}) copy-start(bf16[128,2048]{1,0:T(8,128)(2,1)} %copy-done.14) | copy-start | bytes 1572868
  79.7 3.6 %copy-start.9 = (bf16[128,2048]{1,0:T(8,128)(2,1)S(1)}, bf16[128,2048]{1,0:T(8,128)(2,1)}, u32[]{:S(2)}) copy-start(bf16[128,2048]{1,0:T(8,128)(2,1)} %copy-done.8) | copy-start | bytes 1572868
  91.1 2.7 %collective-permute-start.19 = (f32[128,2048]{1,0:T(8,128)S(1)}, f32[128,2048]{1,0:T(8,128)S(1)}, u32[]{:S(2)}, u32[]{:S(2)}) collective-permute-start(f32[128,2048]{1,0:T(8,128)S(1)} %get-tuple-element.26), channel_id=1, source_target_pairs={{1,0},{0,1},{3,2},{2,3},{5,4},{4,5},{7,6},{6,7},{9,8},{8,9},{11,10... | collective-permute-start | bytes 3145736 | tf_op jit(solution)/shard_map/ppermute | solution.py:109
  (6 other events, 4.5 us)
where the time goes:
time: 95.3 us; the launch traced here: 95 us
  waiting for transfers between devices  48.7 us (51%)
  starting transfers between devices  19.3 us (20%)
  Pallas kernels  16.3 us (17%)
  local copies, waits for them, and re-layouts  9.31 us (10%)
  other arithmetic  1.11 us (1%)
    ppermute x5, waiting for transfers between devices, from_vb(): lax.ppermute(block, 'vb', [((i - move) % vb_count, i) for i in range(vb_c...  25.1 us
    pallas_call x4, Pallas kernels, add(): pl.pallas_call(functools.partial(contract, blocks, sums is None), out_sha...  13.2 us
    ppermute x5, waiting for transfers between devices, from_occ(): lax.ppermute(block, 'occ', [(partner(i, step, occ_count), i) for i in ran...  11.2 us
    ppermute x5, waiting for transfers between devices, from_va(): lax.ppermute(block, 'va', [((i - step) % va_count, i) for i in range(va_c...  9.81 us
    unnamed x36, local copies, waits for them, and re-layouts  9.31 us
    ppermute x5, starting transfers between devices, from_va(): lax.ppermute(block, 'va', [((i - step) % va_count, i) for i in range(va_c...  7.68 us
    ppermute x5, starting transfers between devices, from_vb(): lax.ppermute(block, 'vb', [((i - move) % vb_count, i) for i in range(vb_c...  6.03 us
    ppermute x5, starting transfers between devices, from_occ(): lax.ppermute(block, 'occ', [(partner(i, step, occ_count), i) for i in ran...  5.27 us
  transfers between devices with their start and end apart: 20, of which 8 were waited for; matrix products, arithmetic and copies ran while one was open for 0% of the time, Pallas kernels for 13%

commit v1 on v0

--- a/solution.py
+++ b/solution.py
@@ -21,12 +21,18 @@
     index = index_ref[...]
     width = index.shape[1]
 
+    lanes = 8
+    share = vir_ref.shape[0] // lanes
+
     def step(k, found):
-        return found + jnp.where(index == k, vir_ref[k], 0.0)
-
-    energy = lax.fori_loop(
-        0, vir_ref.shape[0], step, jnp.zeros(index.shape, jnp.float32), unroll=16
-    )
+        return tuple(
+            f + jnp.where(index == n * share + k, vir_ref[n * share + k], 0.0)
+            for n, f in enumerate(found)
+        )
+
+    zero = jnp.zeros(index.shape, jnp.float32)
+    found = lax.fori_loop(0, share, step, (zero,) * lanes, unroll=4)
+    energy = sum(found[1:], found[0])
 
     def block(dx, dy, flip):
         other = lax.rem(chip - dy + chip_count, chip_count) * CORES + lax.rem(core + flip, CORES)
@@ -39,20 +45,25 @@
         row_ref[flip * width : (flip + 1) * width, :] = jnp.transpose(spread)
     for dx in range(va_count):
         for dy in range(chip_count):
-            p = dx * chip_count + dy
-            col_ref[p : p + 1, :] = block(dx, dy, 0)
+            for flip in range(CORES):
+                p = (flip * va_count + dx) * chip_count + dy
+                col_ref[p : p + 1, :] = block(dx, dy, flip)
     for d in range(STEPS):
         far = partner(occ, d, occ_count)
         pair_ref[d] = occ_ref[occ_index_ref[occ]] + occ_ref[occ_index_ref[far]]
 
 
-def contract(blocks, first, *refs):
+def needed(blocks):
+    return sorted({p for d, ps in blocks for p in ps if d > 0})
+
+
+def contract(blocks, parts, first, *refs):
     refs = list(refs)
     pair_energy, row_energy, col_energy = (refs.pop(0) for _ in range(3))
     rows = [refs.pop(0), refs.pop(0)]
-    near = {p: refs.pop(0) for p in sorted({p for d, ps in blocks for p in ps if d > 0})}
+    near = {p: [refs.pop(0) for _ in range(parts[0, p])] for p in needed(blocks)}
     far_rows = {d: [refs.pop(0), refs.pop(0)] for d, _ in blocks if d > 0}
-    far = {(d, p): refs.pop(0) for d, ps in blocks for p in ps}
+    far = {(d, p): [refs.pop(0) for _ in range(parts[d, p])] for d, ps in blocks for p in ps}
     sums_in = None if first else [refs.pop(0), refs.pop(0)]
     sums_out = refs
     count = rows[0].shape[0]
@@ -64,11 +75,11 @@
     weights = []
     for d, ps in blocks:
         direct = lax.dot_general(
-            own, stack([far[d, p] for p in ps]), NT, preferred_element_type=jnp.float32
+            own, stack([r for p in ps for r in far[d, p]]), NT, preferred_element_type=jnp.float32
         )
         if d > 0:
             swapped = lax.dot_general(
-                stack(far_rows[d]), stack([near[p] for p in ps]), NT,
+                stack(far_rows[d]), stack([r for p in ps for r in near[p]]), NT,
                 preferred_element_type=jnp.float32,
             )
         else:
@@ -78,12 +89,45 @@
             gap = pair_energy[d] - row_energy[...] - col_energy[p : p + 1, :]
             weights.append(((2.0 * direct[:, cut] - swapped[:, cut]) / gap).astype(jnp.bfloat16))
     weights = jnp.concatenate(weights, axis=1)
-    columns = stack([far[d, p] for d, ps in blocks for p in ps])
+    columns = stack([r for d, ps in blocks for p in ps for r in far[d, p]])
     for half in range(CORES):
         part = jnp.dot(
             weights[half * count : (half + 1) * count], columns, preferred_element_type=jnp.float32
         )
         sums_out[half][...] = part if first else sums_in[half][...] + part
+
+
+def finish(label, cuts, final, *refs):
+    refs = list(refs)
+    pair_energy, row_energy, col_energy, own, there = (refs.pop(0) for _ in range(5))
+    near = [refs.pop(0) for _ in cuts]
+    far = [refs.pop(0) for _ in cuts]
+    count = own.shape[0]
+    columns = jnp.concatenate([r[...] for r in far], axis=0)
+    direct = lax.dot_general(own[...], columns, NT, preferred_element_type=jnp.float32)
+    swapped = lax.dot_general(
+        there[...], jnp.concatenate([r[...] for r in near], axis=0), NT,
+        preferred_element_type=jnp.float32,
+    )
+    table = jnp.concatenate([col_energy[p : p + 1, cut] for p, cut in cuts], axis=1)
+    row = jnp.concatenate([row_energy[:count, cut] for _, cut in cuts], axis=1)
+    gap = pair_energy[label] - row - table
+    weights = ((2.0 * direct - swapped) / gap).astype(jnp.bfloat16)
+    if not final:
+        sums, out = refs
+        out[...] = sums[...] + jnp.dot(weights, columns, preferred_element_type=jnp.float32)
+        return
+    *sums, out, buffer, sems = refs
+    depth = out.shape[1] // sems.shape[0]
+    copies = []
+    for k in range(sems.shape[0]):
+        cut = slice(k * depth, (k + 1) * depth)
+        part = jnp.dot(weights, columns[:, cut], preferred_element_type=jnp.float32)
+        buffer[:, cut] = (sums[0][:, cut] + sums[1][:, cut]) + part
+        copies.append(pltpu.make_async_copy(buffer.at[:, cut], out.at[:, cut], sems.at[k]))
+        copies[-1].start()
+    for copy in copies:
+        copy.wait()
 
 
 def per_device(aux_factors, occ_energy, vir_energy, occ_index, vir_index):
@@ -129,15 +173,16 @@
                 held[d, p] = from_va(line[d], dx)
             elif dx == 0:
                 held[d, p] = from_vb(line[d], dy)
+    held = {key: [block] for key, block in held.items()}
     for d in range(STEPS):
         for (dx, dy), p in plane_of.items():
-            if dx > 0 and dy > 0:
-                if d % 2 == 1:
-                    held[d, p] = from_occ(held[d - 1, p], 1)
-                elif d == 0:
-                    held[d, p] = from_va(held[d, plane_of[0, dy]], dx)
-                else:
-                    held[d, p] = from_vb(held[d, plane_of[dx, 0]], dy)
+            if dx > 0 and dy > 0 and d % 2 == 1:
+                first, second = held[d - 1, p]
+                held[d, p] = [from_occ(first, 1), from_occ(second, 1)]
+            elif dx > 0 and dy > 0:
+                first = held[d, plane_of[0, dy]][0][: width // 2]
+                second = held[d, plane_of[dx, 0]][0][width // 2 :]
+                held[d, p] = [from_va(first, dx), from_vb(second, dy)]
 
     whole = pl.BlockSpec(memory_space=pltpu.VMEM)
     scalar = pl.BlockSpec(memory_space=pltpu.SMEM)
@@ -149,7 +194,7 @@
             out_shape=(
                 jax.ShapeDtypeStruct((STEPS,), f32),
                 jax.ShapeDtypeStruct((CORES * width, width), f32),
-                jax.ShapeDtypeStruct((len(plane_of), width), f32),
+                jax.ShapeDtypeStruct((CORES * len(plane_of), width), f32),
             ),
             in_specs=[whole, scalar, scalar, scalar],
             out_specs=(scalar, whole, whole),
@@ -158,22 +203,23 @@
             ),
         )(vir_index.reshape(-1, width), vir_energy, occ_index, occ_energy)
 
+    parts = {key: len(pieces) for key, pieces in held.items()}
     tables = energies()
     total = jax.ShapeDtypeStruct((width, aux_width), f32)
 
     def add(blocks, sums):
         operands = [*tables, own, other[0]]
-        operands += [held[0, p] for p in sorted({p for d, ps in blocks for p in ps if d > 0})]
+        operands += [part for p in needed(blocks) for part in held[0, p]]
         for d, _ in blocks:
             operands += [line[d], other[d]] if d > 0 else []
-        operands += [held[d, p] for d, ps in blocks for p in ps]
+        operands += [part for d, ps in blocks for p in ps for part in held[d, p]]
         aliases = {}
         if sums is not None:
             aliases = {len(operands) + k: k for k in range(CORES)}
             operands += list(sums)
         count = sum(len(ps) for _, ps in blocks)
         return pl.pallas_call(
-            functools.partial(contract, blocks, sums is None),
+            functools.partial(contract, blocks, parts, sums is None),
             out_shape=(total, total),
             in_specs=[scalar] + [whole] * (len(operands) - 1),
             out_specs=(whole, whole),
@@ -192,14 +238,52 @@
     cs = [p for (dx, dy), p in plane_of.items() if dx > 0 and dy > 0]
     groups = (
         ((0, here + xs + ys + cs),),
-        ((1, here + ys), (2, here + xs + ys)),
-        ((1, xs + cs), (2, cs), (3, here)),
-        ((3, xs + ys + cs),),
+        ((1, here + xs + ys),),
+        ((2, here + xs + ys),),
+        ((1, cs), (2, cs), (3, here)),
+        ((3, xs + ys),),
     )
     sums = None
     for blocks in groups:
         sums = add(blocks, sums)
-    return (sums[0] + from_core(sums[1]))[None]
+    sums = [sums[0], from_core(sums[1])]
+
+    pieces = parts[0, cs[0]]
+    swapped = {
+        (d, p, k): from_core(held[d, p][k])
+        for d in (0, 3)
+        for p in cs
+        for k in range(pieces)
+    }
+
+    def late(k, final, *sums):
+        size = width // pieces
+        cut = slice(k * size, (k + 1) * size)
+        operands = [*tables, own, line[3]]
+        for d in (0, 3):
+            operands += [held[d, p][k] for p in cs] + [swapped[d, p, k] for p in cs]
+        operands += sums
+        rows = [core * len(plane_of) + p for core in range(CORES) for p in cs]
+        return pl.pallas_call(
+            functools.partial(finish, 3, [(row, cut) for row in rows], final),
+            out_shape=total,
+            in_specs=[scalar] + [whole] * (len(operands) - 1),
+            out_specs=pl.BlockSpec(memory_space=pl.ANY) if final else whole,
+            scratch_shapes=[pltpu.VMEM(total.shape, f32), pltpu.SemaphoreType.DMA((4,))]
+            if final
+            else [],
+            cost_estimate=pl.CostEstimate(
+                flops=2 * 3 * len(rows) * width * size * aux_width,
+                bytes_accessed=width * aux_width * 4,
+                transcendentals=0,
+            ),
+            compiler_params=pltpu.CompilerParams(vmem_limit_bytes=16 << 20),
+        )(*operands)
+
+    mine = sums[0]
+    for k in range(pieces - 1):
+        mine = late(k, False, mine)
+    return late(pieces - 1, True, mine, sums[1])[None]
 
 
 def solution(mesh):

time: 95.3 us -> 108 us (1.13)
  starting transfers between devices: 19.3 us -> 26 us
  waiting for transfers between devices: 48.7 us -> 54.2 us
  Pallas kernels: 16.3 us -> 21.3 us
  local copies, waits for them, and re-layouts: 9.31 us -> 5.85 us
  other arithmetic: 1.11 us -> 0 us
    ppermute x5 -> x7, waiting for transfers between devices: 11.2 us -> 35.5 us  [from_occ(): lax.ppermute(block, 'occ', [(partner(i, step, occ_count), i) for i in ran...]
    ppermute x5 -> x6, waiting for transfers between devices: 25.1 us -> 7.41 us  [from_vb(): lax.ppermute(block, 'vb', [((i - move) % vb_count, i) for i in range(vb_c...]
    pallas_call x4 -> x7, Pallas kernels: 13.2 us -> 18.8 us  [the longest x5 15.1 us: add(): pl.pallas_call(functools.partial(contract, blocks, parts, sums is None),...]
    unnamed x36 -> x24, local copies, waits for them, and re-layouts: 9.31 us -> 3.79 us
    ppermute x5 -> x7, starting transfers between devices: 5.27 us -> 9.76 us  [from_occ(): lax.ppermute(block, 'occ', [(partner(i, step, occ_count), i) for i in ran...]
    ppermute x5 -> x9, waiting for transfers between devices: 2.66 us -> 0.02 us  [from_core(): return lax.ppermute(block, 'vb', [(i ^ 1, i) for i in range(vb_count)])]
    slice x0 -> x4, local copies, waits for them, and re-layouts: none -> 2.07 us  [the longest x2 1.04 us: per_device(): first = held[d, plane_of[0, dy]][0][:width // 2]]
    ppermute x5 -> x6, waiting for transfers between devices: 9.81 us -> 11.2 us  [from_va(): lax.ppermute(block, 'va', [((i - step) % va_count, i) for i in range(va_c...]
  transfers between devices with their start and end apart: 20 -> 28, of which waited for: 8 -> 10; matrix products, arithmetic and copies ran while one was open for 0% -> 2% of each run, Pallas kernels for 13% -> 15%
where the time goes in v1:
time: 108 us
  waiting for transfers between devices  54.2 us (50%)
  starting transfers between devices  26 us (24%)
  Pallas kernels  21.3 us (20%)
  local copies, waits for them, and re-layouts  5.85 us (5%)
    ppermute x7, waiting for transfers between devices, from_occ(): lax.ppermute(block, 'occ', [(partner(i, step, occ_count), i) for i in ran...  35.5 us
    pallas_call x5, Pallas kernels, add(): pl.pallas_call(functools.partial(contract, blocks, parts, sums is None),...  15.1 us
    ppermute x6, waiting for transfers between devices, from_va(): lax.ppermute(block, 'va', [((i - step) % va_count, i) for i in range(va_c...  11.2 us
    ppermute x7, starting transfers between devices, from_occ(): lax.ppermute(block, 'occ', [(partner(i, step, occ_count), i) for i in ran...  9.76 us
    ppermute x6, starting transfers between devices, from_va(): lax.ppermute(block, 'va', [((i - step) % va_count, i) for i in range(va_c...  8.22 us
    ppermute x6, starting transfers between devices, from_vb(): lax.ppermute(block, 'vb', [((i - move) % vb_count, i) for i in range(vb_c...  7.45 us
    ppermute x6, waiting for transfers between devices, from_vb(): lax.ppermute(block, 'vb', [((i - move) % vb_count, i) for i in range(vb_c...  7.41 us
    unnamed x24, local copies, waits for them, and re-layouts  3.79 us
  transfers between devices with their start and end apart: 28, of which 10 were waited for; matrix products, arithmetic and copies ran while one was open for 2% of the time, Pallas kernels for 15%

profile of v1, /device:TPU:0, one launch (start us, length us, event | category | flops | bytes accessed | tf_op | source)
XLA Modules:
  0.0 107.6 jit_solution(3102112306262847179)
XLA Ops:
  0.0 3.1 %collective-permute-start.20 = (bf16[128,2048]{1,0:T(8,128)(2,1)}, bf16[128,2048]{1,0:T(8,128)(2,1)S(1)}, u32[]{:S(2)}, u32[]{:S(2)}) collective-permute-start(bf16[128,2048]{1,0:T(8,128)(2,1)} %bitcast.3), channel_id=1, source_target_pairs={{8,0},{0,8},{24,16},{16,24},{9,1},{1,9},{25,17},{17,25},{10,2},{2,... | collective-permute-start | bytes 1572872 | tf_op jit(solution)/shard_map/ppermute | solution.py:156
  3.1 1.5 %collective-permute-start.9 = (bf16[128,2048]{1,0:T(8,128)(2,1)}, bf16[128,2048]{1,0:T(8,128)(2,1)S(1)}, u32[]{:S(2)}, u32[]{:S(2)}) collective-permute-start(bf16[128,2048]{1,0:T(8,128)(2,1)} %bitcast.4), channel_id=1, source_target_pairs={{2,0},{3,1},{0,2},{1,3},{6,4},{7,5},{4,6},{5,7},{10,8},{11,9},{8,1... | collective-permute-start | bytes 1572872 | tf_op jit(solution)/shard_map/ppermute | solution.py:150
  4.6 1.5 %collective-permute-start.2 = (bf16[128,2048]{1,0:T(8,128)(2,1)}, bf16[128,2048]{1,0:T(8,128)(2,1)S(1)}, u32[]{:S(2)}, u32[]{:S(2)}) collective-permute-start(bf16[128,2048]{1,0:T(8,128)(2,1)} %bitcast.5), channel_id=1, source_target_pairs={{4,0},{0,4},{5,1},{1,5},{6,2},{2,6},{7,3},{3,7},{12,8},{8,12},{13,... | collective-permute-start | bytes 1572872 | tf_op jit(solution)/shard_map/ppermute | solution.py:146
  6.1 2.6 %collective-permute-start = (bf16[128,2048]{1,0:T(8,128)(2,1)}, bf16[128,2048]{1,0:T(8,128)(2,1)S(1)}, u32[]{:S(2)}, u32[]{:S(2)}) collective-permute-start(bf16[128,2048]{1,0:T(8,128)(2,1)} %bitcast.7), channel_id=1, source_target_pairs={{16,0},{24,8},{0,16},{8,24},{17,1},{25,9},{1,17},{9,25},{18,2},{26... | collective-permute-start | bytes 1572872 | tf_op jit(solution)/shard_map/ppermute | solution.py:156
  8.7 13.7 %collective-permute-done.20.refs_8_.refs_10_ = bf16[128,2048]{1,0:T(8,128)(2,1)S(1)} collective-permute-done((bf16[128,2048]{1,0:T(8,128)(2,1)}, bf16[128,2048]{1,0:T(8,128)(2,1)S(1)}, u32[]{:S(2)}, u32[]{:S(2)}) %collective-permute-start.20) | collective-permute-done | bytes 524320 | tf_op jit(solution)/shard_map/ppermute | solution.py:156
  22.3 2.6 %collective-permute-start.25 = (bf16[128,2048]{1,0:T(8,128)(2,1)S(1)}, bf16[128,2048]{1,0:T(8,128)(2,1)S(1)}, u32[]{:S(2)}, u32[]{:S(2)}) collective-permute-start(bf16[128,2048]{1,0:T(8,128)(2,1)S(1)} %collective-permute-done.20.refs_8_.refs_10_), channel_id=1, source_target_pairs={{4,0},{0,4},{5,1},{1,5},{6,2},{2,6},{7,3},{3,7},{12,8},{8,12},{13,... | collective-permute-start | bytes 1572872 | tf_op jit(solution)/shard_map/ppermute | solution.py:146
  25.1 2.6 %collective-permute-start.3 = (bf16[64,2048]{1,0:T(8,128)(2,1)S(1)}, bf16[64,2048]{1,0:T(8,128)(2,1)S(1)}, u32[]{:S(2)}, u32[]{:S(2)}) collective-permute-start(bf16[64,2048]{1,0:T(8,128)(2,1)S(1)} %slice.16), channel_id=1, source_target_pairs={{2,0},{3,1},{0,2},{1,3},{6,4},{7,5},{4,6},{5,7},{10,8},{11,9},{8,1... | collective-permute-start | bytes 786440 | tf_op jit(solution)/shard_map/ppermute | solution.py:150
  27.7 5.1 %collective-permute-done.refs_8_.refs_10_ = bf16[128,2048]{1,0:T(8,128)(2,1)S(1)} collective-permute-done((bf16[128,2048]{1,0:T(8,128)(2,1)}, bf16[128,2048]{1,0:T(8,128)(2,1)S(1)}, u32[]{:S(2)}, u32[]{:S(2)}) %collective-permute-start) | collective-permute-done | bytes 524320 | tf_op jit(solution)/shard_map/ppermute | solution.py:156
  33.3 10.0 %collective-permute-done.10.refs_8_.refs_6_.refs_5_ = bf16[64,2048]{1,0:T(8,128)(2,1)} collective-permute-done((bf16[64,2048]{1,0:T(8,128)(2,1)S(1)}, bf16[64,2048]{1,0:T(8,128)(2,1)}, u32[]{:S(2)}, u32[]{:S(2)}) %collective-permute-start.10) | collective-permute-done | bytes 262176 | tf_op jit(solution)/shard_map/ppermute | solution.py:146
  43.3 2.5 %collective-permute-start.12 = (bf16[128,2048]{1,0:T(8,128)(2,1)S(1)}, bf16[128,2048]{1,0:T(8,128)(2,1)}, u32[]{:S(2)}, u32[]{:S(2)}) collective-permute-start(bf16[128,2048]{1,0:T(8,128)(2,1)S(1)} %collective-permute-done.refs_8_.refs_10_), channel_id=1, source_target_pairs={{2,0},{3,1},{0,2},{1,3},{6,4},{7,5},{4,6},{5,7},{10,8},{11,9},{8,1... | collective-permute-start | bytes 1572872 | tf_op jit(solution)/shard_map/ppermute | solution.py:150
  46.6 0.8 copy-done.6
  47.4 1.7 %collective-permute-start.5 = (bf16[128,2048]{1,0:T(8,128)(2,1)S(1)}, bf16[128,2048]{1,0:T(8,128)(2,1)}, u32[]{:S(2)}, u32[]{:S(2)}) collective-permute-start(bf16[128,2048]{1,0:T(8,128)(2,1)S(1)} %collective-permute-done.refs_8_.refs_10_), channel_id=1, source_target_pairs={{4,0},{0,4},{5,1},{1,5},{6,2},{2,6},{7,3},{3,7},{12,8},{8,12},{13,... | collective-permute-start | bytes 1572872 | tf_op jit(solution)/shard_map/ppermute | solution.py:146
  50.0 2.0 %collective-permute-start.23 = (bf16[64,2048]{1,0:T(8,128)(2,1)}, bf16[64,2048]{1,0:T(8,128)(2,1)}, u32[]{:S(2)}, u32[]{:S(2)}) collective-permute-start(bf16[64,2048]{1,0:T(8,128)(2,1)} %collective-permute-done.10.refs_8_.refs_6_.refs_5_), channel_id=1, source_target_pairs={{8,0},{0,8},{24,16},{16,24},{9,1},{1,9},{25,17},{17,25},{10,2},{2,... | collective-permute-start | bytes 786440 | tf_op jit(solution)/shard_map/ppermute | solution.py:156
  52.0 5.9 %collective-permute-done.12.refs_12_ = bf16[128,2048]{1,0:T(8,128)(2,1)} collective-permute-done((bf16[128,2048]{1,0:T(8,128)(2,1)S(1)}, bf16[128,2048]{1,0:T(8,128)(2,1)}, u32[]{:S(2)}, u32[]{:S(2)}) %collective-permute-start.12) | collective-permute-done | bytes 524320 | tf_op jit(solution)/shard_map/ppermute | solution.py:150
  57.9 2.7 %collective-permute-done.1.refs_12_.refs_18_.refs_7_.refs_4_ = bf16[128,2048]{1,0:T(8,128)(2,1)S(1)} collective-permute-done((bf16[128,2048]{1,0:T(8,128)(2,1)S(1)}, bf16[128,2048]{1,0:T(8,128)(2,1)S(1)}, u32[]{:S(2)}, u32[]{:S(2)}) %collective-permute-start.1) | collective-permute-done | bytes 524320 | tf_op jit(solution)/shard_map/ppermute | solution.py:156
  61.4 1.7 %collective-permute-start.18 = (bf16[128,2048]{1,0:T(8,128)(2,1)S(1)}, bf16[128,2048]{1,0:T(8,128)(2,1)}, u32[]{:S(2)}, u32[]{:S(2)}) collective-permute-start(bf16[128,2048]{1,0:T(8,128)(2,1)S(1)} %collective-permute-done.1.refs_12_.refs_18_.refs_7_.refs_4_), channel_id=1, source_target_pairs={{4,0},{0,4},{5,1},{1,5},{6,2},{2,6},{7,3},{3,7},{12,8},{8,12},{13,... | collective-permute-start | bytes 1572872 | tf_op jit(solution)/shard_map/ppermute | solution.py:146
  63.2 2.5 %shard_map.55 = (f32[4]{0:T(128)}, f32[256,128]{1,0:T(8,128)}, f32[8,128]{1,0:T(8,128)}) custom-call(s32[8,128]{1,0:T(8,128)} %bitcast.19, f32[1024]{0:T(1024)} %vir_ref.1, s32[4]{0:T(128)} %occ_index_ref.1, f32[4]{0:T(128)} %occ_ref.1), custom_call_target="tpu_custom_call" | custom-call | flops 3145728 | bytes 262144 | tf_op jit(solution)/shard_map/pallas_call | solution.py:192
  65.6 1.0 slice.19
  66.7 1.0 slice.17
  68.3 2.4 %collective-permute-done.24.refs_15_ = bf16[64,2048]{1,0:T(8,128)(2,1)} collective-permute-done((bf16[64,2048]{1,0:T(8,128)(2,1)S(1)}, bf16[64,2048]{1,0:T(8,128)(2,1)}, u32[]{:S(2)}, u32[]{:S(2)}) %collective-permute-start.24) | collective-permute-done | bytes 262176 | tf_op jit(solution)/shard_map/ppermute | solution.py:156
  71.5 2.5 %shard_map.56 = (f32[128,2048]{1,0:T(8,128)S(1)}, f32[128,2048]{1,0:T(8,128)S(1)}) custom-call(f32[4]{0:T(128)S(1)} %copy-done.11, f32[256,128]{1,0:T(8,128)S(1)} %copy-done.1, f32[8,128]{1,0:T(8,128)S(1)} %copy-done.10, bf16[128,2048]{1,0:T(8,128)(2,1)S(1)} %bitcast.8, bf16[128,2048]{1,0:T(8,128)(2,1)S(1)} %collective-permute-done.16.refs_4_, ...), custom_call_target="tpu_custom_call" | custom-call | flops 1610612736 | bytes 4194304 | tf_op jit(solution)/shard_map/pallas_call | solution.py:221
  74.0 2.7 %shard_map.57 = (f32[128,2048]{1,0:T(8,128)S(1)}, f32[128,2048]{1,0:T(8,128)S(1)}) custom-call(f32[4]{0:T(128)S(1)} %copy-done.11, f32[256,128]{1,0:T(8,128)S(1)} %copy-done.1, f32[8,128]{1,0:T(8,128)S(1)} %copy-done.10, bf16[128,2048]{1,0:T(8,128)(2,1)S(1)} %bitcast.10, ...), custom_call_target="tpu_custom_call", output_to_operand_aliasing={{0}: (13, {}), {1}: (14, {})} | custom-call | flops 1207959552 | bytes 3145728 | tf_op jit(solution)/shard_map/pallas_call | solution.py:221
  76.7 3.4 %shard_map.58 = (f32[128,2048]{1,0:T(8,128)S(1)}, f32[128,2048]{1,0:T(8,128)S(1)}) custom-call(f32[4]{0:T(128)S(1)} %copy-done.11, f32[256,128]{1,0:T(8,128)S(1)} %copy-done.1, f32[8,128]{1,0:T(8,128)S(1)} %copy-done.10, bf16[128,2048]{1,0:T(8,128)(2,1)S(1)} %bitcast.12, ...), custom_call_target="tpu_custom_call", output_to_operand_aliasing={{0}: (13, {}), {1}: (14, {})} | custom-call | flops 1207959552 | bytes 3145728 | tf_op jit(solution)/shard_map/pallas_call | solution.py:221
  80.1 1.3 %collective-permute-done.13.refs_16_ = bf16[64,2048]{1,0:T(8,128)(2,1)S(1)} collective-permute-done((bf16[64,2048]{1,0:T(8,128)(2,1)S(1)}, bf16[64,2048]{1,0:T(8,128)(2,1)S(1)}, u32[]{:S(2)}, u32[]{:S(2)}) %collective-permute-start.13) | collective-permute-done | bytes 262176 | tf_op jit(solution)/shard_map/ppermute | solution.py:146
  81.4 1.5 %collective-permute-done.6.refs_17_ = bf16[64,2048]{1,0:T(8,128)(2,1)S(1)} collective-permute-done((bf16[64,2048]{1,0:T(8,128)(2,1)S(1)}, bf16[64,2048]{1,0:T(8,128)(2,1)S(1)}, u32[]{:S(2)}, u32[]{:S(2)}) %collective-permute-start.6) | collective-permute-done | bytes 262176 | tf_op jit(solution)/shard_map/ppermute | solution.py:150
  82.8 3.9 %shard_map.59 = (f32[128,2048]{1,0:T(8,128)S(1)}, f32[128,2048]{1,0:T(8,128)S(1)}) custom-call(f32[4]{0:T(128)S(1)} %copy-done.11, f32[256,128]{1,0:T(8,128)S(1)} %copy-done.1, f32[8,128]{1,0:T(8,128)S(1)} %copy-done.10, bf16[128,2048]{1,0:T(8,128)(2,1)S(1)} %bitcast.14, ...), custom_call_target="tpu_custom_call", output_to_operand_aliasing={{0}: (19, {}), {1}: (20, {})} | custom-call | flops 1207959552 | bytes 3145728 | tf_op jit(solution)/shard_map/pallas_call | solution.py:221
  86.8 2.6 %shard_map.60 = (f32[128,2048]{1,0:T(8,128)S(1)}, f32[128,2048]{1,0:T(8,128)S(1)}) custom-call(f32[4]{0:T(128)S(1)} %copy-done.11, f32[256,128]{1,0:T(8,128)S(1)} %copy-done.1, f32[8,128]{1,0:T(8,128)S(1)} %copy-done.10, bf16[128,2048]{1,0:T(8,128)(2,1)S(1)} %bitcast.16, ...), custom_call_target="tpu_custom_call", output_to_operand_aliasing={{0}: (11, {}), {1}: (12, {})} | custom-call | flops 805306368 | bytes 2097152 | tf_op jit(solution)/shard_map/pallas_call | solution.py:221
  89.7 1.9 %collective-permute-start.7 = (bf16[64,2048]{1,0:T(8,128)(2,1)S(1)}, bf16[64,2048]{1,0:T(8,128)(2,1)S(1)}, u32[]{:S(2)}, u32[]{:S(2)}) collective-permute-start(bf16[64,2048]{1,0:T(8,128)(2,1)S(1)} %collective-permute-done.6.refs_17_), channel_id=1, source_target_pairs={{8,0},{0,8},{24,16},{16,24},{9,1},{1,9},{25,17},{17,25},{10,2},{2,... | collective-permute-start | bytes 786440 | tf_op jit(solution)/shard_map/ppermute | solution.py:156
  91.6 7.2 %collective-permute-done.14.refs_7_ = bf16[64,2048]{1,0:T(8,128)(2,1)S(1)} collective-permute-done((bf16[64,2048]{1,0:T(8,128)(2,1)S(1)}, bf16[64,2048]{1,0:T(8,128)(2,1)S(1)}, u32[]{:S(2)}, u32[]{:S(2)}) %collective-permute-start.14) | collective-permute-done | bytes 262176 | tf_op jit(solution)/shard_map/ppermute | solution.py:156
  99.3 4.6 %collective-permute-done.7.refs_7_ = bf16[64,2048]{1,0:T(8,128)(2,1)S(1)} collective-permute-done((bf16[64,2048]{1,0:T(8,128)(2,1)S(1)}, bf16[64,2048]{1,0:T(8,128)(2,1)S(1)}, u32[]{:S(2)}, u32[]{:S(2)}) %collective-permute-start.7) | collective-permute-done | bytes 262176 | tf_op jit(solution)/shard_map/ppermute | solution.py:156
  103.8 1.6 %shard_map.61.refs_9_ = f32[128,2048]{1,0:T(8,128)S(1)} custom-call(f32[4]{0:T(128)S(1)} %copy-done.11, f32[256,128]{1,0:T(8,128)S(1)} %copy-done.1, f32[8,128]{1,0:T(8,128)S(1)} %copy-done.10, bf16[128,2048]{1,0:T(8,128)(2,1)S(1)} %bitcast.17, bf16[128,2048]{1,0:T(8,128)(2,1)S(1)} %collective-permute-done.1.refs_12_.refs_18_.refs_7_.refs_4_, ...), custom_call_target="tpu_custom_call" | custom-call | flops 201326592 | bytes 1048576 | tf_op jit(solution)/shard_map/pallas_call | solution.py:267
  105.5 2.1 %shard_map.62 = f32[128,2048]{1,0:T(8,128)} custom-call(f32[4]{0:T(128)S(1)} %copy-done.11, f32[256,128]{1,0:T(8,128)S(1)} %copy-done.1, f32[8,128]{1,0:T(8,128)S(1)} %copy-done.10, bf16[128,2048]{1,0:T(8,128)(2,1)S(1)} %bitcast.18, bf16[128,2048]{1,0:T(8,128)(2,1)S(1)} %collective-permute-done.1.refs_12_.refs_18_.refs_7_.refs_4_, ...), custom_call_target="tpu_custom_call" | custom-call | flops 201326592 | bytes 1048576 | tf_op jit(solution)/shard_map/pallas_call | solution.py:267
  (60 shorter events, 5.3 us)
Async XLA Ops:
  0.0 22.3 %collective-permute-start.20 = (bf16[128,2048]{1,0:T(8,128)(2,1)}, bf16[128,2048]{1,0:T(8,128)(2,1)S(1)}, u32[]{:S(2)}, u32[]{:S(2)}) collective-permute-start(bf16[128,2048]{1,0:T(8,128)(2,1)} %bitcast.3), channel_id=1, source_target_pairs={{8,0},{0,8},{24,16},{16,24},{9,1},{1,9},{25,17},{17,25},{10,2},{2,... | collective-permute-start | bytes 1572872 | tf_op jit(solution)/shard_map/ppermute | solution.py:156
  3.1 19.3 %collective-permute-start.9 = (bf16[128,2048]{1,0:T(8,128)(2,1)}, bf16[128,2048]{1,0:T(8,128)(2,1)S(1)}, u32[]{:S(2)}, u32[]{:S(2)}) collective-permute-start(bf16[128,2048]{1,0:T(8,128)(2,1)} %bitcast.4), channel_id=1, source_target_pairs={{2,0},{3,1},{0,2},{1,3},{6,4},{7,5},{4,6},{5,7},{10,8},{11,9},{8,1... | collective-permute-start | bytes 1572872 | tf_op jit(solution)/shard_map/ppermute | solution.py:150
  4.6 20.4 %collective-permute-start.2 = (bf16[128,2048]{1,0:T(8,128)(2,1)}, bf16[128,2048]{1,0:T(8,128)(2,1)S(1)}, u32[]{:S(2)}, u32[]{:S(2)}) collective-permute-start(bf16[128,2048]{1,0:T(8,128)(2,1)} %bitcast.5), channel_id=1, source_target_pairs={{4,0},{0,4},{5,1},{1,5},{6,2},{2,6},{7,3},{3,7},{12,8},{8,12},{13,... | collective-permute-start | bytes 1572872 | tf_op jit(solution)/shard_map/ppermute | solution.py:146
  6.1 19.0 %collective-permute-start.16 = (bf16[128,2048]{1,0:T(8,128)(2,1)}, bf16[128,2048]{1,0:T(8,128)(2,1)S(1)}, u32[]{:S(2)}, u32[]{:S(2)}) collective-permute-start(bf16[128,2048]{1,0:T(8,128)(2,1)} %bitcast.6), channel_id=1, source_target_pairs={{1,0},{0,1},{3,2},{2,3},{5,4},{4,5},{7,6},{6,7},{9,8},{8,9},{11,10... | collective-permute-start | bytes 1572872 | tf_op jit(solution)/shard_map/ppermute | solution.py:153
  6.1 26.7 %collective-permute-start = (bf16[128,2048]{1,0:T(8,128)(2,1)}, bf16[128,2048]{1,0:T(8,128)(2,1)S(1)}, u32[]{:S(2)}, u32[]{:S(2)}) collective-permute-start(bf16[128,2048]{1,0:T(8,128)(2,1)} %bitcast.7), channel_id=1, source_target_pairs={{16,0},{24,8},{0,16},{8,24},{17,1},{25,9},{1,17},{9,25},{18,2},{26... | collective-permute-start | bytes 1572872 | tf_op jit(solution)/shard_map/ppermute | solution.py:156
  22.3 23.5 %collective-permute-start.21 = (bf16[128,2048]{1,0:T(8,128)(2,1)S(1)}, bf16[128,2048]{1,0:T(8,128)(2,1)S(1)}, u32[]{:S(2)}, u32[]{:S(2)}) collective-permute-start(bf16[128,2048]{1,0:T(8,128)(2,1)S(1)} %collective-permute-done.20.refs_8_.refs_10_), channel_id=1, source_target_pairs={{1,0},{0,1},{3,2},{2,3},{5,4},{4,5},{7,6},{6,7},{9,8},{8,9},{11,10... | collective-permute-start | bytes 1572872 | tf_op jit(solution)/shard_map/ppermute | solution.py:153
  22.3 24.3 %collective-permute-start.25 = (bf16[128,2048]{1,0:T(8,128)(2,1)S(1)}, bf16[128,2048]{1,0:T(8,128)(2,1)S(1)}, u32[]{:S(2)}, u32[]{:S(2)}) collective-permute-start(bf16[128,2048]{1,0:T(8,128)(2,1)S(1)} %collective-permute-done.20.refs_8_.refs_10_), channel_id=1, source_target_pairs={{4,0},{0,4},{5,1},{1,5},{6,2},{2,6},{7,3},{3,7},{12,8},{8,12},{13,... | collective-permute-start | bytes 1572872 | tf_op jit(solution)/shard_map/ppermute | solution.py:146
  25.0 18.3 %collective-permute-start.10 = (bf16[64,2048]{1,0:T(8,128)(2,1)S(1)}, bf16[64,2048]{1,0:T(8,128)(2,1)}, u32[]{:S(2)}, u32[]{:S(2)}) collective-permute-start(bf16[64,2048]{1,0:T(8,128)(2,1)S(1)} %slice.18), channel_id=1, source_target_pairs={{4,0},{0,4},{5,1},{1,5},{6,2},{2,6},{7,3},{3,7},{12,8},{8,12},{13,... | collective-permute-start | bytes 786440 | tf_op jit(solution)/shard_map/ppermute | solution.py:146
  25.1 20.7 %collective-permute-start.3 = (bf16[64,2048]{1,0:T(8,128)(2,1)S(1)}, bf16[64,2048]{1,0:T(8,128)(2,1)S(1)}, u32[]{:S(2)}, u32[]{:S(2)}) collective-permute-start(bf16[64,2048]{1,0:T(8,128)(2,1)S(1)} %slice.16), channel_id=1, source_target_pairs={{2,0},{3,1},{0,2},{1,3},{6,4},{7,5},{4,6},{5,7},{10,8},{11,9},{8,1... | collective-permute-start | bytes 786440 | tf_op jit(solution)/shard_map/ppermute | solution.py:150
  32.8 16.4 %collective-permute-start.26 = (bf16[128,2048]{1,0:T(8,128)(2,1)S(1)}, bf16[128,2048]{1,0:T(8,128)(2,1)S(1)}, u32[]{:S(2)}, u32[]{:S(2)}) collective-permute-start(bf16[128,2048]{1,0:T(8,128)(2,1)S(1)} %collective-permute-done.20.refs_8_.refs_10_), channel_id=1, source_target_pairs={{2,0},{3,1},{0,2},{1,3},{6,4},{7,5},{4,6},{5,7},{10,8},{11,9},{8,1... | collective-permute-start | bytes 1572872 | tf_op jit(solution)/shard_map/ppermute | solution.py:150
  43.3 14.7 %collective-permute-start.12 = (bf16[128,2048]{1,0:T(8,128)(2,1)S(1)}, bf16[128,2048]{1,0:T(8,128)(2,1)}, u32[]{:S(2)}, u32[]{:S(2)}) collective-permute-start(bf16[128,2048]{1,0:T(8,128)(2,1)S(1)} %collective-permute-done.refs_8_.refs_10_), channel_id=1, source_target_pairs={{2,0},{3,1},{0,2},{1,3},{6,4},{7,5},{4,6},{5,7},{10,8},{11,9},{8,1... | collective-permute-start | bytes 1572872 | tf_op jit(solution)/shard_map/ppermute | solution.py:150
  45.8 14.8 %collective-permute-start.1 = (bf16[128,2048]{1,0:T(8,128)(2,1)S(1)}, bf16[128,2048]{1,0:T(8,128)(2,1)S(1)}, u32[]{:S(2)}, u32[]{:S(2)}) collective-permute-start(bf16[128,2048]{1,0:T(8,128)(2,1)S(1)} %collective-permute-done.refs_8_.refs_10_), channel_id=1, source_target_pairs={{8,0},{0,8},{24,16},{16,24},{9,1},{1,9},{25,17},{17,25},{10,2},{2,... | collective-permute-start | bytes 1572872 | tf_op jit(solution)/shard_map/ppermute | solution.py:156
  46.6 14.0 %collective-permute-start.22 = (bf16[128,2048]{1,0:T(8,128)(2,1)S(1)}, bf16[128,2048]{1,0:T(8,128)(2,1)S(1)}, u32[]{:S(2)}, u32[]{:S(2)}) collective-permute-start(bf16[128,2048]{1,0:T(8,128)(2,1)S(1)} %collective-permute-done.refs_8_.refs_10_), channel_id=1, source_target_pairs={{1,0},{0,1},{3,2},{2,3},{5,4},{4,5},{7,6},{6,7},{9,8},{8,9},{11,10... | collective-permute-start | bytes 1572872 | tf_op jit(solution)/shard_map/ppermute | solution.py:153
  47.4 15.7 %collective-permute-start.5 = (bf16[128,2048]{1,0:T(8,128)(2,1)S(1)}, bf16[128,2048]{1,0:T(8,128)(2,1)}, u32[]{:S(2)}, u32[]{:S(2)}) collective-permute-start(bf16[128,2048]{1,0:T(8,128)(2,1)S(1)} %collective-permute-done.refs_8_.refs_10_), channel_id=1, source_target_pairs={{4,0},{0,4},{5,1},{1,5},{6,2},{2,6},{7,3},{3,7},{12,8},{8,12},{13,... | collective-permute-start | bytes 1572872 | tf_op jit(solution)/shard_map/ppermute | solution.py:146
  50.0 17.7 %collective-permute-start.23 = (bf16[64,2048]{1,0:T(8,128)(2,1)}, bf16[64,2048]{1,0:T(8,128)(2,1)}, u32[]{:S(2)}, u32[]{:S(2)}) collective-permute-start(bf16[64,2048]{1,0:T(8,128)(2,1)} %collective-permute-done.10.refs_8_.refs_6_.refs_5_), channel_id=1, source_target_pairs={{8,0},{0,8},{24,16},{16,24},{9,1},{1,9},{25,17},{17,25},{10,2},{2,... | collective-permute-start | bytes 786440 | tf_op jit(solution)/shard_map/ppermute | solution.py:156
  57.9 12.7 %collective-permute-start.24 = (bf16[64,2048]{1,0:T(8,128)(2,1)S(1)}, bf16[64,2048]{1,0:T(8,128)(2,1)}, u32[]{:S(2)}, u32[]{:S(2)}) collective-permute-start(bf16[64,2048]{1,0:T(8,128)(2,1)S(1)} %collective-permute-done.3.refs_9_.refs_7_.refs_5_), channel_id=1, source_target_pairs={{8,0},{0,8},{24,16},{16,24},{9,1},{1,9},{25,17},{17,25},{10,2},{2,... | collective-permute-start | bytes 786440 | tf_op jit(solution)/shard_map/ppermute | solution.py:156
  60.6 22.2 %collective-permute-start.17 = (bf16[128,2048]{1,0:T(8,128)(2,1)S(1)}, bf16[128,2048]{1,0:T(8,128)(2,1)}, u32[]{:S(2)}, u32[]{:S(2)}) collective-permute-start(bf16[128,2048]{1,0:T(8,128)(2,1)S(1)} %collective-permute-done.1.refs_12_.refs_18_.refs_7_.refs_4_), channel_id=1, source_target_pairs={{1,0},{0,1},{3,2},{2,3},{5,4},{4,5},{7,6},{6,7},{9,8},{8,9},{11,10... | collective-permute-start | bytes 1572872 | tf_op jit(solution)/shard_map/ppermute | solution.py:153
  61.4 25.4 %collective-permute-start.18 = (bf16[128,2048]{1,0:T(8,128)(2,1)S(1)}, bf16[128,2048]{1,0:T(8,128)(2,1)}, u32[]{:S(2)}, u32[]{:S(2)}) collective-permute-start(bf16[128,2048]{1,0:T(8,128)(2,1)S(1)} %collective-permute-done.1.refs_12_.refs_18_.refs_7_.refs_4_), channel_id=1, source_target_pairs={{4,0},{0,4},{5,1},{1,5},{6,2},{2,6},{7,3},{3,7},{12,8},{8,12},{13,... | collective-permute-start | bytes 1572872 | tf_op jit(solution)/shard_map/ppermute | solution.py:146
  63.2 23.6 %collective-permute-start.19 = (bf16[128,2048]{1,0:T(8,128)(2,1)S(1)}, bf16[128,2048]{1,0:T(8,128)(2,1)}, u32[]{:S(2)}, u32[]{:S(2)}) collective-permute-start(bf16[128,2048]{1,0:T(8,128)(2,1)S(1)} %collective-permute-done.1.refs_12_.refs_18_.refs_7_.refs_4_), channel_id=1, source_target_pairs={{2,0},{3,1},{0,2},{1,3},{6,4},{7,5},{4,6},{5,7},{10,8},{11,9},{8,1... | collective-permute-start | bytes 1572872 | tf_op jit(solution)/shard_map/ppermute | solution.py:150
  65.6 5.3 %copy-start = (bf16[1,128,2048]{2,1,0:T(8,128)(2,1)S(1)}, bf16[1,128,2048]{2,1,0:T(8,128)(2,1)}, u32[]{:S(2)}) copy-start(bf16[1,128,2048]{2,1,0:T(8,128)(2,1)} %param.5) | copy-start | bytes 1572868
  66.7 4.2 %copy-start.1 = (f32[256,128]{1,0:T(8,128)S(1)}, f32[256,128]{1,0:T(8,128)}, u32[]{:S(2)}) copy-start(f32[256,128]{1,0:T(8,128)} %get-tuple-element.19.refs_1_) | copy-start | bytes 393220
  67.7 3.2 %copy-start.10 = (f32[8,128]{1,0:T(8,128)S(1)}, f32[8,128]{1,0:T(8,128)}, u32[]{:S(2)}) copy-start(f32[8,128]{1,0:T(8,128)} %get-tuple-element.20.refs_2_) | copy-start | bytes 12292
  67.7 13.6 %collective-permute-start.13 = (bf16[64,2048]{1,0:T(8,128)(2,1)S(1)}, bf16[64,2048]{1,0:T(8,128)(2,1)S(1)}, u32[]{:S(2)}, u32[]{:S(2)}) collective-permute-start(bf16[64,2048]{1,0:T(8,128)(2,1)S(1)} %slice.19), channel_id=1, source_target_pairs={{4,0},{0,4},{5,1},{1,5},{6,2},{2,6},{7,3},{3,7},{12,8},{8,12},{13,... | collective-permute-start | bytes 786440 | tf_op jit(solution)/shard_map/ppermute | solution.py:146
  70.6 12.2 %collective-permute-start.6 = (bf16[64,2048]{1,0:T(8,128)(2,1)S(1)}, bf16[64,2048]{1,0:T(8,128)(2,1)S(1)}, u32[]{:S(2)}, u32[]{:S(2)}) collective-permute-start(bf16[64,2048]{1,0:T(8,128)(2,1)S(1)} %slice.17), channel_id=1, source_target_pairs={{2,0},{3,1},{0,2},{1,3},{6,4},{7,5},{4,6},{5,7},{10,8},{11,9},{8,1... | collective-permute-start | bytes 786440 | tf_op jit(solution)/shard_map/ppermute | solution.py:150
  74.0 2.7 %copy-start.5 = (bf16[128,2048]{1,0:T(8,128)(2,1)S(1)}, bf16[128,2048]{1,0:T(8,128)(2,1)}, u32[]{:S(2)}) copy-start(bf16[128,2048]{1,0:T(8,128)(2,1)} %copy-done.4) | copy-start | bytes 1572868
  89.4 16.1 %collective-permute-start.27 = (f32[128,2048]{1,0:T(8,128)S(1)}, f32[128,2048]{1,0:T(8,128)S(1)}, u32[]{:S(2)}, u32[]{:S(2)}) collective-permute-start(f32[128,2048]{1,0:T(8,128)S(1)} %get-tuple-element.30), channel_id=1, source_target_pairs={{1,0},{0,1},{3,2},{2,3},{5,4},{4,5},{7,6},{6,7},{9,8},{8,9},{11,10... | collective-permute-start | bytes 3145736 | tf_op jit(solution)/shard_map/ppermute | solution.py:153
  89.5 9.2 %collective-permute-start.14 = (bf16[64,2048]{1,0:T(8,128)(2,1)S(1)}, bf16[64,2048]{1,0:T(8,128)(2,1)S(1)}, u32[]{:S(2)}, u32[]{:S(2)}) collective-permute-start(bf16[64,2048]{1,0:T(8,128)(2,1)S(1)} %collective-permute-done.13.refs_16_), channel_id=1, source_target_pairs={{8,0},{0,8},{24,16},{16,24},{9,1},{1,9},{25,17},{17,25},{10,2},{2,... | collective-permute-start | bytes 786440 | tf_op jit(solution)/shard_map/ppermute | solution.py:156
  89.7 14.1 %collective-permute-start.7 = (bf16[64,2048]{1,0:T(8,128)(2,1)S(1)}, bf16[64,2048]{1,0:T(8,128)(2,1)S(1)}, u32[]{:S(2)}, u32[]{:S(2)}) collective-permute-start(bf16[64,2048]{1,0:T(8,128)(2,1)S(1)} %collective-permute-done.6.refs_17_), channel_id=1, source_target_pairs={{8,0},{0,8},{24,16},{16,24},{9,1},{1,9},{25,17},{17,25},{10,2},{2,... | collective-permute-start | bytes 786440 | tf_op jit(solution)/shard_map/ppermute | solution.py:156
  91.6 12.2 %collective-permute-start.11 = (bf16[64,2048]{1,0:T(8,128)(2,1)}, bf16[64,2048]{1,0:T(8,128)(2,1)S(1)}, u32[]{:S(2)}, u32[]{:S(2)}) collective-permute-start(bf16[64,2048]{1,0:T(8,128)(2,1)} %collective-permute-done.10.refs_8_.refs_6_.refs_5_), channel_id=1, source_target_pairs={{1,0},{0,1},{3,2},{2,3},{5,4},{4,5},{7,6},{6,7},{9,8},{8,9},{11,10... | collective-permute-start | bytes 786440 | tf_op jit(solution)/shard_map/ppermute | solution.py:153
  98.8 5.1 %collective-permute-start.15 = (bf16[64,2048]{1,0:T(8,128)(2,1)S(1)}, bf16[64,2048]{1,0:T(8,128)(2,1)S(1)}, u32[]{:S(2)}, u32[]{:S(2)}) collective-permute-start(bf16[64,2048]{1,0:T(8,128)(2,1)S(1)} %collective-permute-done.14.refs_7_), channel_id=1, source_target_pairs={{1,0},{0,1},{3,2},{2,3},{5,4},{4,5},{7,6},{6,7},{9,8},{8,9},{11,10... | collective-permute-start | bytes 786440 | tf_op jit(solution)/shard_map/ppermute | solution.py:153
  98.8 6.7 %collective-permute-start.4 = (bf16[64,2048]{1,0:T(8,128)(2,1)S(1)}, bf16[64,2048]{1,0:T(8,128)(2,1)S(1)}, u32[]{:S(2)}, u32[]{:S(2)}) collective-permute-start(bf16[64,2048]{1,0:T(8,128)(2,1)S(1)} %collective-permute-done.3.refs_9_.refs_7_.refs_5_), channel_id=1, source_target_pairs={{1,0},{0,1},{3,2},{2,3},{5,4},{4,5},{7,6},{6,7},{9,8},{8,9},{11,10... | collective-permute-start | bytes 786440 | tf_op jit(solution)/shard_map/ppermute | solution.py:153
  103.8 1.7 %collective-permute-start.8 = (bf16[64,2048]{1,0:T(8,128)(2,1)S(1)}, bf16[64,2048]{1,0:T(8,128)(2,1)S(1)}, u32[]{:S(2)}, u32[]{:S(2)}) collective-permute-start(bf16[64,2048]{1,0:T(8,128)(2,1)S(1)} %collective-permute-done.7.refs_7_), channel_id=1, source_target_pairs={{1,0},{0,1},{3,2},{2,3},{5,4},{4,5},{7,6},{6,7},{9,8},{8,9},{11,10... | collective-permute-start | bytes 786440 | tf_op jit(solution)/shard_map/ppermute | solution.py:153
  (8 other events, 11.2 us)

commit v2 on v1

--- a/solution.py
+++ b/solution.py
@@ -164,25 +164,28 @@
         line[d] = from_occ(line[d - low], low)
     other = {d: from_core(line[d]) for d in range(STEPS)}
     plane_of = {(dx, dy): dx * chip_count + dy for dx in range(va_count) for dy in range(chip_count)}
+    half = width // 2
     held = {}
     for d in range(STEPS):
+        blocks = {"": line[d]}
+        if d == 2:
+            blocks = {"a": line[d][:half], "b": line[d][half:]}
         for (dx, dy), p in plane_of.items():
             if dx == 0 and dy == 0:
-                held[d, p] = line[d]
+                held[d, p] = [line[d]]
             elif dy == 0:
-                held[d, p] = from_va(line[d], dx)
+                held[d, p] = [from_va(b, dx) for b in blocks.values()]
             elif dx == 0:
-                held[d, p] = from_vb(line[d], dy)
-    held = {key: [block] for key, block in held.items()}
+                held[d, p] = [from_vb(b, dy) for b in blocks.values()]
     for d in range(STEPS):
         for (dx, dy), p in plane_of.items():
             if dx > 0 and dy > 0 and d % 2 == 1:
                 first, second = held[d - 1, p]
                 held[d, p] = [from_occ(first, 1), from_occ(second, 1)]
             elif dx > 0 and dy > 0:
-                first = held[d, plane_of[0, dy]][0][: width // 2]
-                second = held[d, plane_of[dx, 0]][0][width // 2 :]
-                held[d, p] = [from_va(first, dx), from_vb(second, dy)]
+                first = held[d, plane_of[0, dy]][0]
+                second = held[d, plane_of[dx, 0]][-1]
+                held[d, p] = [from_va(first[:half], dx), from_vb(second[-half:], dy)]
 
     whole = pl.BlockSpec(memory_space=pltpu.VMEM)
     scalar = pl.BlockSpec(memory_space=pltpu.SMEM)

time: 108 us -> 103 us (0.954)
  waiting for transfers between devices: 54.2 us -> 47.5 us
  local copies, waits for them, and re-layouts: 5.85 us -> 7.92 us
  Pallas kernels: 21.3 us -> 20.1 us
    ppermute x7, waiting for transfers between devices: 35.5 us -> 25.8 us  [from_occ(): lax.ppermute(block, 'occ', [(partner(i, step, occ_count), i) for i in ran...]
    ppermute x6 -> x7, waiting for transfers between devices: 7.41 us -> 11.7 us  [from_vb(): lax.ppermute(block, 'vb', [((i - move) % vb_count, i) for i in range(vb_c...]
    unnamed x24 -> x42, local copies, waits for them, and re-layouts: 3.79 us -> 7.85 us
    ppermute x6 -> x7, starting transfers between devices: 7.45 us -> 10.7 us  [from_vb(): lax.ppermute(block, 'vb', [((i - move) % vb_count, i) for i in range(vb_c...]
    slice x4 -> x3, local copies, waits for them, and re-layouts: 2.07 us -> 0.07 us  [the longest x2 0.04 us: per_device(): held[d, p] = [from_va(first[:half], dx), from_vb(second[-half:], dy)]]
    ppermute x6 -> x7, starting transfers between devices: 8.22 us -> 6.36 us  [from_va(): lax.ppermute(block, 'va', [((i - step) % va_count, i) for i in range(va_c...]
    ppermute x6 -> x7, waiting for transfers between devices: 11.2 us -> 9.77 us  [from_va(): lax.ppermute(block, 'va', [((i - step) % va_count, i) for i in range(va_c...]
  transfers between devices with their start and end apart: 28 -> 30, of which waited for: 10 -> 10; matrix products, arithmetic and copies ran while one was open for 2% -> 0% of each run, Pallas kernels for 15% -> 15%
where the time goes in v2:
time: 103 us
  waiting for transfers between devices  47.5 us (46%)
  starting transfers between devices  26.8 us (26%)
  Pallas kernels  20.1 us (20%)
  local copies, waits for them, and re-layouts  7.92 us (8%)
    ppermute x7, waiting for transfers between devices, from_occ(): lax.ppermute(block, 'occ', [(partner(i, step, occ_count), i) for i in ran...  25.8 us
    pallas_call x5, Pallas kernels, add(): pl.pallas_call(functools.partial(contract, blocks, parts, sums is None),...  14.3 us
    ppermute x7, waiting for transfers between devices, from_vb(): lax.ppermute(block, 'vb', [((i - move) % vb_count, i) for i in range(vb_c...  11.7 us
    ppermute x7, starting transfers between devices, from_vb(): lax.ppermute(block, 'vb', [((i - move) % vb_count, i) for i in range(vb_c...  10.7 us
    ppermute x7, waiting for transfers between devices, from_va(): lax.ppermute(block, 'va', [((i - step) % va_count, i) for i in range(va_c...  9.77 us
    ppermute x7, starting transfers between devices, from_occ(): lax.ppermute(block, 'occ', [(partner(i, step, occ_count), i) for i in ran...  9.05 us
    unnamed x42, local copies, waits for them, and re-layouts  7.85 us
    ppermute x7, starting transfers between devices, from_va(): lax.ppermute(block, 'va', [((i - step) % va_count, i) for i in range(va_c...  6.36 us
  transfers between devices with their start and end apart: 30, of which 10 were waited for; matrix products, arithmetic and copies ran while one was open for 0% of the time, Pallas kernels for 15%

profile of v2, /device:TPU:0, one launch (start us, length us, event | category | flops | bytes accessed | tf_op | source)
XLA Modules:
  0.0 102.6 jit_solution(3249216071215933491)
XLA Ops:
  0.0 3.0 %collective-permute-start.9 = (bf16[128,2048]{1,0:T(8,128)(2,1)}, bf16[128,2048]{1,0:T(8,128)(2,1)S(1)}, u32[]{:S(2)}, u32[]{:S(2)}) collective-permute-start(bf16[128,2048]{1,0:T(8,128)(2,1)} %bitcast.3), channel_id=1, source_target_pairs={{2,0},{3,1},{0,2},{1,3},{6,4},{7,5},{4,6},{5,7},{10,8},{11,9},{8,1... | collective-permute-start | bytes 1572872 | tf_op jit(solution)/shard_map/ppermute | solution.py:150
  3.0 1.5 %collective-permute-start.2 = (bf16[128,2048]{1,0:T(8,128)(2,1)}, bf16[128,2048]{1,0:T(8,128)(2,1)S(1)}, u32[]{:S(2)}, u32[]{:S(2)}) collective-permute-start(bf16[128,2048]{1,0:T(8,128)(2,1)} %bitcast.4), channel_id=1, source_target_pairs={{4,0},{0,4},{5,1},{1,5},{6,2},{2,6},{7,3},{3,7},{12,8},{8,12},{13,... | collective-permute-start | bytes 1572872 | tf_op jit(solution)/shard_map/ppermute | solution.py:146
  4.5 2.6 %collective-permute-start = (bf16[128,2048]{1,0:T(8,128)(2,1)}, bf16[128,2048]{1,0:T(8,128)(2,1)S(1)}, u32[]{:S(2)}, u32[]{:S(2)}) collective-permute-start(bf16[128,2048]{1,0:T(8,128)(2,1)} %bitcast.5), channel_id=1, source_target_pairs={{16,0},{24,8},{0,16},{8,24},{17,1},{25,9},{1,17},{9,25},{18,2},{26... | collective-permute-start | bytes 1572872 | tf_op jit(solution)/shard_map/ppermute | solution.py:156
  7.1 1.6 %collective-permute-start.20 = (bf16[128,2048]{1,0:T(8,128)(2,1)}, bf16[128,2048]{1,0:T(8,128)(2,1)S(1)}, u32[]{:S(2)}, u32[]{:S(2)}) collective-permute-start(bf16[128,2048]{1,0:T(8,128)(2,1)} %bitcast.7), channel_id=1, source_target_pairs={{8,0},{0,8},{24,16},{16,24},{9,1},{1,9},{25,17},{17,25},{10,2},{2,... | collective-permute-start | bytes 1572872 | tf_op jit(solution)/shard_map/ppermute | solution.py:156
  8.7 6.5 %collective-permute-done.9.refs_7_.refs_6_.refs_5_ = bf16[128,2048]{1,0:T(8,128)(2,1)S(1)} collective-permute-done((bf16[128,2048]{1,0:T(8,128)(2,1)}, bf16[128,2048]{1,0:T(8,128)(2,1)S(1)}, u32[]{:S(2)}, u32[]{:S(2)}) %collective-permute-start.9) | collective-permute-done | bytes 524320 | tf_op jit(solution)/shard_map/ppermute | solution.py:150
  15.1 1.8 %collective-permute-start.10 = (bf16[64,2048]{1,0:T(8,128)(2,1)S(1)}, bf16[64,2048]{1,0:T(8,128)(2,1)S(1)}, u32[]{:S(2)}, u32[]{:S(2)}) collective-permute-start(bf16[64,2048]{1,0:T(8,128)(2,1)S(1)} %slice.18), channel_id=1, source_target_pairs={{4,0},{0,4},{5,1},{1,5},{6,2},{2,6},{7,3},{3,7},{12,8},{8,12},{13,... | collective-permute-start | bytes 786440 | tf_op jit(solution)/shard_map/ppermute | solution.py:146
  17.0 1.6 %collective-permute-start.3 = (bf16[64,2048]{1,0:T(8,128)(2,1)S(1)}, bf16[64,2048]{1,0:T(8,128)(2,1)S(1)}, u32[]{:S(2)}, u32[]{:S(2)}) collective-permute-start(bf16[64,2048]{1,0:T(8,128)(2,1)S(1)} %slice.16), channel_id=1, source_target_pairs={{2,0},{3,1},{0,2},{1,3},{6,4},{7,5},{4,6},{5,7},{10,8},{11,9},{8,1... | collective-permute-start | bytes 786440 | tf_op jit(solution)/shard_map/ppermute | solution.py:150
  18.6 11.5 %collective-permute-done.refs_8_.refs_10_ = bf16[128,2048]{1,0:T(8,128)(2,1)S(1)} collective-permute-done((bf16[128,2048]{1,0:T(8,128)(2,1)}, bf16[128,2048]{1,0:T(8,128)(2,1)S(1)}, u32[]{:S(2)}, u32[]{:S(2)}) %collective-permute-start) | collective-permute-done | bytes 524320 | tf_op jit(solution)/shard_map/ppermute | solution.py:156
  31.7 0.9 collective-permute-start.25
  32.7 1.5 %collective-permute-start.26 = (bf16[64,2048]{1,0:T(8,128)(2,1)S(1)}, bf16[64,2048]{1,0:T(8,128)(2,1)S(1)}, u32[]{:S(2)}, u32[]{:S(2)}) collective-permute-start(bf16[64,2048]{1,0:T(8,128)(2,1)S(1)} %get-tuple-element.32), channel_id=1, source_target_pairs={{2,0},{3,1},{0,2},{1,3},{6,4},{7,5},{4,6},{5,7},{10,8},{11,9},{8,1... | collective-permute-start | bytes 786440 | tf_op jit(solution)/shard_map/ppermute | solution.py:150
  34.2 5.2 %collective-permute-done.12.refs_13_ = bf16[64,2048]{1,0:T(8,128)(2,1)} collective-permute-done((bf16[64,2048]{1,0:T(8,128)(2,1)S(1)}, bf16[64,2048]{1,0:T(8,128)(2,1)}, u32[]{:S(2)}, u32[]{:S(2)}) %collective-permute-start.12) | collective-permute-done | bytes 262176 | tf_op jit(solution)/shard_map/ppermute | solution.py:150
  40.7 4.8 %collective-permute-done.25.refs_11_ = bf16[64,2048]{1,0:T(8,128)(2,1)S(1)} collective-permute-done((bf16[64,2048]{1,0:T(8,128)(2,1)S(1)}, bf16[64,2048]{1,0:T(8,128)(2,1)S(1)}, u32[]{:S(2)}, u32[]{:S(2)}) %collective-permute-start.25) | collective-permute-done | bytes 262176 | tf_op jit(solution)/shard_map/ppermute | solution.py:146
  46.2 1.5 %collective-permute-start.28 = (bf16[128,2048]{1,0:T(8,128)(2,1)S(1)}, bf16[128,2048]{1,0:T(8,128)(2,1)S(1)}, u32[]{:S(2)}, u32[]{:S(2)}) collective-permute-start(bf16[128,2048]{1,0:T(8,128)(2,1)S(1)} %collective-permute-done.20.refs_8_.refs_10_), channel_id=1, source_target_pairs={{2,0},{3,1},{0,2},{1,3},{6,4},{7,5},{4,6},{5,7},{10,8},{11,9},{8,1... | collective-permute-start | bytes 1572872 | tf_op jit(solution)/shard_map/ppermute | solution.py:150
  50.5 5.0 %collective-permute-done.27.refs_11_ = bf16[128,2048]{1,0:T(8,128)(2,1)S(1)} collective-permute-done((bf16[128,2048]{1,0:T(8,128)(2,1)S(1)}, bf16[128,2048]{1,0:T(8,128)(2,1)S(1)}, u32[]{:S(2)}, u32[]{:S(2)}) %collective-permute-start.27) | collective-permute-done | bytes 524320 | tf_op jit(solution)/shard_map/ppermute | solution.py:146
  55.5 0.8 copy-done.11
  56.3 2.5 %collective-permute-start.6 = (bf16[64,2048]{1,0:T(8,128)(2,1)}, bf16[64,2048]{1,0:T(8,128)(2,1)}, u32[]{:S(2)}, u32[]{:S(2)}) collective-permute-start(bf16[64,2048]{1,0:T(8,128)(2,1)} %collective-permute-done.5.refs_12_), channel_id=1, source_target_pairs={{2,0},{3,1},{0,2},{1,3},{6,4},{7,5},{4,6},{5,7},{10,8},{11,9},{8,1... | collective-permute-start | bytes 786440 | tf_op jit(solution)/shard_map/ppermute | solution.py:150
  61.0 2.5 %shard_map.55 = (f32[4]{0:T(128)}, f32[256,128]{1,0:T(8,128)}, f32[8,128]{1,0:T(8,128)}) custom-call(s32[8,128]{1,0:T(8,128)} %bitcast.19, f32[1024]{0:T(1024)} %vir_ref.1, s32[4]{0:T(128)} %occ_index_ref.1, f32[4]{0:T(128)} %occ_ref.1), custom_call_target="tpu_custom_call" | custom-call | flops 3145728 | bytes 262144 | tf_op jit(solution)/shard_map/pallas_call | solution.py:195
  63.5 1.4 %collective-permute-start.23 = (bf16[64,2048]{1,0:T(8,128)(2,1)}, bf16[64,2048]{1,0:T(8,128)(2,1)S(1)}, u32[]{:S(2)}, u32[]{:S(2)}) collective-permute-start(bf16[64,2048]{1,0:T(8,128)(2,1)} %copy-done.8), channel_id=1, source_target_pairs={{8,0},{0,8},{24,16},{16,24},{9,1},{1,9},{25,17},{17,25},{10,2},{2,... | collective-permute-start | bytes 786440 | tf_op jit(solution)/shard_map/ppermute | solution.py:156
  66.2 0.9 copy-done.1
  67.1 0.9 copy-done.9
  68.1 1.9 %shard_map.56 = (f32[128,2048]{1,0:T(8,128)S(1)}, f32[128,2048]{1,0:T(8,128)S(1)}) custom-call(f32[4]{0:T(128)S(1)} %copy-done.20, f32[256,128]{1,0:T(8,128)S(1)} %copy-done.1, f32[8,128]{1,0:T(8,128)S(1)} %copy-done.19, bf16[128,2048]{1,0:T(8,128)(2,1)S(1)} %bitcast.8, bf16[128,2048]{1,0:T(8,128)(2,1)S(1)} %collective-permute-done.16.refs_4_, ...), custom_call_target="tpu_custom_call" | custom-call | flops 1610612736 | bytes 4194304 | tf_op jit(solution)/shard_map/pallas_call | solution.py:224
  70.1 2.7 %shard_map.57 = (f32[128,2048]{1,0:T(8,128)S(1)}, f32[128,2048]{1,0:T(8,128)S(1)}) custom-call(f32[4]{0:T(128)S(1)} %copy-done.20, f32[256,128]{1,0:T(8,128)S(1)} %copy-done.1, f32[8,128]{1,0:T(8,128)S(1)} %copy-done.19, bf16[128,2048]{1,0:T(8,128)(2,1)S(1)} %bitcast.10, ...), custom_call_target="tpu_custom_call", output_to_operand_aliasing={{0}: (13, {}), {1}: (14, {})} | custom-call | flops 1207959552 | bytes 3145728 | tf_op jit(solution)/shard_map/pallas_call | solution.py:224
  72.8 3.2 %shard_map.58 = (f32[128,2048]{1,0:T(8,128)S(1)}, f32[128,2048]{1,0:T(8,128)S(1)}) custom-call(f32[4]{0:T(128)S(1)} %copy-done.20, f32[256,128]{1,0:T(8,128)S(1)} %copy-done.1, f32[8,128]{1,0:T(8,128)S(1)} %copy-done.19, bf16[128,2048]{1,0:T(8,128)(2,1)S(1)} %bitcast.12, ...), custom_call_target="tpu_custom_call", output_to_operand_aliasing={{0}: (15, {}), {1}: (16, {})} | custom-call | flops 1207959552 | bytes 3145728 | tf_op jit(solution)/shard_map/pallas_call | solution.py:224
  76.1 1.8 %collective-permute-done.24.refs_15_ = bf16[64,2048]{1,0:T(8,128)(2,1)S(1)} collective-permute-done((bf16[64,2048]{1,0:T(8,128)(2,1)S(1)}, bf16[64,2048]{1,0:T(8,128)(2,1)S(1)}, u32[]{:S(2)}, u32[]{:S(2)}) %collective-permute-start.24) | collective-permute-done | bytes 262176 | tf_op jit(solution)/shard_map/ppermute | solution.py:156
  77.8 3.8 %shard_map.59 = (f32[128,2048]{1,0:T(8,128)S(1)}, f32[128,2048]{1,0:T(8,128)S(1)}) custom-call(f32[4]{0:T(128)S(1)} %copy-done.20, f32[256,128]{1,0:T(8,128)S(1)} %copy-done.1, f32[8,128]{1,0:T(8,128)S(1)} %copy-done.19, bf16[128,2048]{1,0:T(8,128)(2,1)S(1)} %bitcast.14, ...), custom_call_target="tpu_custom_call", output_to_operand_aliasing={{0}: (19, {}), {1}: (20, {})} | custom-call | flops 1207959552 | bytes 3145728 | tf_op jit(solution)/shard_map/pallas_call | solution.py:224
  81.7 2.6 %shard_map.60 = (f32[128,2048]{1,0:T(8,128)S(1)}, f32[128,2048]{1,0:T(8,128)S(1)}) custom-call(f32[4]{0:T(128)S(1)} %copy-done.20, f32[256,128]{1,0:T(8,128)S(1)} %copy-done.1, f32[8,128]{1,0:T(8,128)S(1)} %copy-done.19, bf16[128,2048]{1,0:T(8,128)(2,1)S(1)} %bitcast.16, ...), custom_call_target="tpu_custom_call", output_to_operand_aliasing={{0}: (11, {}), {1}: (12, {})} | custom-call | flops 805306368 | bytes 2097152 | tf_op jit(solution)/shard_map/pallas_call | solution.py:224
  84.4 1.1 %collective-permute-start.14 = (bf16[64,2048]{1,0:T(8,128)(2,1)}, bf16[64,2048]{1,0:T(8,128)(2,1)S(1)}, u32[]{:S(2)}, u32[]{:S(2)}) collective-permute-start(bf16[64,2048]{1,0:T(8,128)(2,1)} %collective-permute-done.13.refs_16_), channel_id=1, source_target_pairs={{8,0},{0,8},{24,16},{16,24},{9,1},{1,9},{25,17},{17,25},{10,2},{2,... | collective-permute-start | bytes 786440 | tf_op jit(solution)/shard_map/ppermute | solution.py:156
  85.5 1.0 collective-permute-start.7
  86.5 7.4 %collective-permute-done.14.refs_7_ = bf16[64,2048]{1,0:T(8,128)(2,1)S(1)} collective-permute-done((bf16[64,2048]{1,0:T(8,128)(2,1)}, bf16[64,2048]{1,0:T(8,128)(2,1)S(1)}, u32[]{:S(2)}, u32[]{:S(2)}) %collective-permute-start.14) | collective-permute-done | bytes 262176 | tf_op jit(solution)/shard_map/ppermute | solution.py:156
  94.4 4.6 %collective-permute-done.7.refs_7_ = bf16[64,2048]{1,0:T(8,128)(2,1)S(1)} collective-permute-done((bf16[64,2048]{1,0:T(8,128)(2,1)}, bf16[64,2048]{1,0:T(8,128)(2,1)S(1)}, u32[]{:S(2)}, u32[]{:S(2)}) %collective-permute-start.7) | collective-permute-done | bytes 262176 | tf_op jit(solution)/shard_map/ppermute | solution.py:156
  98.9 1.2 %shard_map.61.refs_9_ = f32[128,2048]{1,0:T(8,128)S(1)} custom-call(f32[4]{0:T(128)S(1)} %copy-done.20, f32[256,128]{1,0:T(8,128)S(1)} %copy-done.1, f32[8,128]{1,0:T(8,128)S(1)} %copy-done.19, bf16[128,2048]{1,0:T(8,128)(2,1)S(1)} %bitcast.17, bf16[128,2048]{1,0:T(8,128)(2,1)S(1)} %collective-permute-done.1.refs_12_.refs_18_.refs_7_.refs_4_, ...), custom_call_target="tpu_custom_call" | custom-call | flops 201326592 | bytes 1048576 | tf_op jit(solution)/shard_map/pallas_call | solution.py:270
  100.5 2.1 %shard_map.62 = f32[128,2048]{1,0:T(8,128)} custom-call(f32[4]{0:T(128)S(1)} %copy-done.20, f32[256,128]{1,0:T(8,128)S(1)} %copy-done.1, f32[8,128]{1,0:T(8,128)S(1)} %copy-done.19, bf16[128,2048]{1,0:T(8,128)(2,1)S(1)} %bitcast.18, bf16[128,2048]{1,0:T(8,128)(2,1)S(1)} %collective-permute-done.1.refs_12_.refs_18_.refs_7_.refs_4_, ...), custom_call_target="tpu_custom_call" | custom-call | flops 201326592 | bytes 1048576 | tf_op jit(solution)/shard_map/pallas_call | solution.py:270
  (81 shorter events, 10.9 us)
Async XLA Ops:
  0.0 15.1 %collective-permute-start.9 = (bf16[128,2048]{1,0:T(8,128)(2,1)}, bf16[128,2048]{1,0:T(8,128)(2,1)S(1)}, u32[]{:S(2)}, u32[]{:S(2)}) collective-permute-start(bf16[128,2048]{1,0:T(8,128)(2,1)} %bitcast.3), channel_id=1, source_target_pairs={{2,0},{3,1},{0,2},{1,3},{6,4},{7,5},{4,6},{5,7},{10,8},{11,9},{8,1... | collective-permute-start | bytes 1572872 | tf_op jit(solution)/shard_map/ppermute | solution.py:150
  3.0 13.9 %collective-permute-start.2 = (bf16[128,2048]{1,0:T(8,128)(2,1)}, bf16[128,2048]{1,0:T(8,128)(2,1)S(1)}, u32[]{:S(2)}, u32[]{:S(2)}) collective-permute-start(bf16[128,2048]{1,0:T(8,128)(2,1)} %bitcast.4), channel_id=1, source_target_pairs={{4,0},{0,4},{5,1},{1,5},{6,2},{2,6},{7,3},{3,7},{12,8},{8,12},{13,... | collective-permute-start | bytes 1572872 | tf_op jit(solution)/shard_map/ppermute | solution.py:146
  4.5 25.6 %collective-permute-start = (bf16[128,2048]{1,0:T(8,128)(2,1)}, bf16[128,2048]{1,0:T(8,128)(2,1)S(1)}, u32[]{:S(2)}, u32[]{:S(2)}) collective-permute-start(bf16[128,2048]{1,0:T(8,128)(2,1)} %bitcast.5), channel_id=1, source_target_pairs={{16,0},{24,8},{0,16},{8,24},{17,1},{25,9},{1,17},{9,25},{18,2},{26... | collective-permute-start | bytes 1572872 | tf_op jit(solution)/shard_map/ppermute | solution.py:156
  7.1 23.6 %collective-permute-start.16 = (bf16[128,2048]{1,0:T(8,128)(2,1)}, bf16[128,2048]{1,0:T(8,128)(2,1)S(1)}, u32[]{:S(2)}, u32[]{:S(2)}) collective-permute-start(bf16[128,2048]{1,0:T(8,128)(2,1)} %bitcast.6), channel_id=1, source_target_pairs={{1,0},{0,1},{3,2},{2,3},{5,4},{4,5},{7,6},{6,7},{9,8},{8,9},{11,10... | collective-permute-start | bytes 1572872 | tf_op jit(solution)/shard_map/ppermute | solution.py:153
  7.1 24.7 %collective-permute-start.20 = (bf16[128,2048]{1,0:T(8,128)(2,1)}, bf16[128,2048]{1,0:T(8,128)(2,1)S(1)}, u32[]{:S(2)}, u32[]{:S(2)}) collective-permute-start(bf16[128,2048]{1,0:T(8,128)(2,1)} %bitcast.7), channel_id=1, source_target_pairs={{8,0},{0,8},{24,16},{16,24},{9,1},{1,9},{25,17},{17,25},{10,2},{2,... | collective-permute-start | bytes 1572872 | tf_op jit(solution)/shard_map/ppermute | solution.py:156
  15.1 17.6 %collective-permute-start.10 = (bf16[64,2048]{1,0:T(8,128)(2,1)S(1)}, bf16[64,2048]{1,0:T(8,128)(2,1)S(1)}, u32[]{:S(2)}, u32[]{:S(2)}) collective-permute-start(bf16[64,2048]{1,0:T(8,128)(2,1)S(1)} %slice.18), channel_id=1, source_target_pairs={{4,0},{0,4},{5,1},{1,5},{6,2},{2,6},{7,3},{3,7},{12,8},{8,12},{13,... | collective-permute-start | bytes 786440 | tf_op jit(solution)/shard_map/ppermute | solution.py:146
  17.0 48.7 %copy-start = (bf16[1,128,2048]{2,1,0:T(8,128)(2,1)S(1)}, bf16[1,128,2048]{2,1,0:T(8,128)(2,1)}, u32[]{:S(2)}) copy-start(bf16[1,128,2048]{2,1,0:T(8,128)(2,1)} %param.5) | copy-start | bytes 1572868
  17.0 17.3 %collective-permute-start.3 = (bf16[64,2048]{1,0:T(8,128)(2,1)S(1)}, bf16[64,2048]{1,0:T(8,128)(2,1)S(1)}, u32[]{:S(2)}, u32[]{:S(2)}) collective-permute-start(bf16[64,2048]{1,0:T(8,128)(2,1)S(1)} %slice.16), channel_id=1, source_target_pairs={{2,0},{3,1},{0,2},{1,3},{6,4},{7,5},{4,6},{5,7},{10,8},{11,9},{8,1... | collective-permute-start | bytes 786440 | tf_op jit(solution)/shard_map/ppermute | solution.py:150
  30.1 9.3 %collective-permute-start.12 = (bf16[64,2048]{1,0:T(8,128)(2,1)S(1)}, bf16[64,2048]{1,0:T(8,128)(2,1)}, u32[]{:S(2)}, u32[]{:S(2)}) collective-permute-start(bf16[64,2048]{1,0:T(8,128)(2,1)S(1)} %get-tuple-element.31), channel_id=1, source_target_pairs={{2,0},{3,1},{0,2},{1,3},{6,4},{7,5},{4,6},{5,7},{10,8},{11,9},{8,1... | collective-permute-start | bytes 786440 | tf_op jit(solution)/shard_map/ppermute | solution.py:150
  30.7 9.3 %collective-permute-start.5 = (bf16[64,2048]{1,0:T(8,128)(2,1)S(1)}, bf16[64,2048]{1,0:T(8,128)(2,1)}, u32[]{:S(2)}, u32[]{:S(2)}) collective-permute-start(bf16[64,2048]{1,0:T(8,128)(2,1)S(1)} %get-tuple-element.32), channel_id=1, source_target_pairs={{4,0},{0,4},{5,1},{1,5},{6,2},{2,6},{7,3},{3,7},{12,8},{8,12},{13,... | collective-permute-start | bytes 786440 | tf_op jit(solution)/shard_map/ppermute | solution.py:146
  31.7 13.7 %collective-permute-start.25 = (bf16[64,2048]{1,0:T(8,128)(2,1)S(1)}, bf16[64,2048]{1,0:T(8,128)(2,1)S(1)}, u32[]{:S(2)}, u32[]{:S(2)}) collective-permute-start(bf16[64,2048]{1,0:T(8,128)(2,1)S(1)} %get-tuple-element.31), channel_id=1, source_target_pairs={{4,0},{0,4},{5,1},{1,5},{6,2},{2,6},{7,3},{3,7},{12,8},{8,12},{13,... | collective-permute-start | bytes 786440 | tf_op jit(solution)/shard_map/ppermute | solution.py:146
  32.7 7.3 %copy-start.8 = (bf16[64,2048]{1,0:T(8,128)(2,1)}, bf16[64,2048]{1,0:T(8,128)(2,1)S(1)}, u32[]{:S(2)}) copy-start(bf16[64,2048]{1,0:T(8,128)(2,1)S(1)} %collective-permute-done.10.refs_8_.refs_6_.refs_5_) | copy-start | bytes 786436
  32.7 15.8 %collective-permute-start.26 = (bf16[64,2048]{1,0:T(8,128)(2,1)S(1)}, bf16[64,2048]{1,0:T(8,128)(2,1)S(1)}, u32[]{:S(2)}, u32[]{:S(2)}) collective-permute-start(bf16[64,2048]{1,0:T(8,128)(2,1)S(1)} %get-tuple-element.32), channel_id=1, source_target_pairs={{2,0},{3,1},{0,2},{1,3},{6,4},{7,5},{4,6},{5,7},{10,8},{11,9},{8,1... | collective-permute-start | bytes 786440 | tf_op jit(solution)/shard_map/ppermute | solution.py:150
  34.2 15.0 %collective-permute-start.21 = (bf16[128,2048]{1,0:T(8,128)(2,1)S(1)}, bf16[128,2048]{1,0:T(8,128)(2,1)S(1)}, u32[]{:S(2)}, u32[]{:S(2)}) collective-permute-start(bf16[128,2048]{1,0:T(8,128)(2,1)S(1)} %collective-permute-done.20.refs_8_.refs_10_), channel_id=1, source_target_pairs={{1,0},{0,1},{3,2},{2,3},{5,4},{4,5},{7,6},{6,7},{9,8},{8,9},{11,10... | collective-permute-start | bytes 1572872 | tf_op jit(solution)/shard_map/ppermute | solution.py:153
  39.4 16.1 %collective-permute-start.27 = (bf16[128,2048]{1,0:T(8,128)(2,1)S(1)}, bf16[128,2048]{1,0:T(8,128)(2,1)S(1)}, u32[]{:S(2)}, u32[]{:S(2)}) collective-permute-start(bf16[128,2048]{1,0:T(8,128)(2,1)S(1)} %collective-permute-done.20.refs_8_.refs_10_), channel_id=1, source_target_pairs={{4,0},{0,4},{5,1},{1,5},{6,2},{2,6},{7,3},{3,7},{12,8},{8,12},{13,... | collective-permute-start | bytes 1572872 | tf_op jit(solution)/shard_map/ppermute | solution.py:146
  40.0 18.9 %collective-permute-start.1 = (bf16[128,2048]{1,0:T(8,128)(2,1)S(1)}, bf16[128,2048]{1,0:T(8,128)(2,1)S(1)}, u32[]{:S(2)}, u32[]{:S(2)}) collective-permute-start(bf16[128,2048]{1,0:T(8,128)(2,1)S(1)} %collective-permute-done.refs_8_.refs_10_), channel_id=1, source_target_pairs={{8,0},{0,8},{24,16},{16,24},{9,1},{1,9},{25,17},{17,25},{10,2},{2,... | collective-permute-start | bytes 1572872 | tf_op jit(solution)/shard_map/ppermute | solution.py:156
  46.2 12.7 %collective-permute-start.28 = (bf16[128,2048]{1,0:T(8,128)(2,1)S(1)}, bf16[128,2048]{1,0:T(8,128)(2,1)S(1)}, u32[]{:S(2)}, u32[]{:S(2)}) collective-permute-start(bf16[128,2048]{1,0:T(8,128)(2,1)S(1)} %collective-permute-done.20.refs_8_.refs_10_), channel_id=1, source_target_pairs={{2,0},{3,1},{0,2},{1,3},{6,4},{7,5},{4,6},{5,7},{10,8},{11,9},{8,1... | collective-permute-start | bytes 1572872 | tf_op jit(solution)/shard_map/ppermute | solution.py:150
  49.2 11.0 %collective-permute-start.22 = (bf16[128,2048]{1,0:T(8,128)(2,1)S(1)}, bf16[128,2048]{1,0:T(8,128)(2,1)S(1)}, u32[]{:S(2)}, u32[]{:S(2)}) collective-permute-start(bf16[128,2048]{1,0:T(8,128)(2,1)S(1)} %collective-permute-done.refs_8_.refs_10_), channel_id=1, source_target_pairs={{1,0},{0,1},{3,2},{2,3},{5,4},{4,5},{7,6},{6,7},{9,8},{8,9},{11,10... | collective-permute-start | bytes 1572872 | tf_op jit(solution)/shard_map/ppermute | solution.py:153
  50.0 13.5 %collective-permute-start.13 = (bf16[64,2048]{1,0:T(8,128)(2,1)}, bf16[64,2048]{1,0:T(8,128)(2,1)}, u32[]{:S(2)}, u32[]{:S(2)}) collective-permute-start(bf16[64,2048]{1,0:T(8,128)(2,1)} %collective-permute-done.12.refs_13_), channel_id=1, source_target_pairs={{4,0},{0,4},{5,1},{1,5},{6,2},{2,6},{7,3},{3,7},{12,8},{8,12},{13,... | collective-permute-start | bytes 786440 | tf_op jit(solution)/shard_map/ppermute | solution.py:146
  56.3 8.6 %collective-permute-start.6 = (bf16[64,2048]{1,0:T(8,128)(2,1)}, bf16[64,2048]{1,0:T(8,128)(2,1)}, u32[]{:S(2)}, u32[]{:S(2)}) collective-permute-start(bf16[64,2048]{1,0:T(8,128)(2,1)} %collective-permute-done.5.refs_12_), channel_id=1, source_target_pairs={{2,0},{3,1},{0,2},{1,3},{6,4},{7,5},{4,6},{5,7},{10,8},{11,9},{8,1... | collective-permute-start | bytes 786440 | tf_op jit(solution)/shard_map/ppermute | solution.py:150
  58.8 19.0 %collective-permute-start.17 = (bf16[128,2048]{1,0:T(8,128)(2,1)S(1)}, bf16[128,2048]{1,0:T(8,128)(2,1)}, u32[]{:S(2)}, u32[]{:S(2)}) collective-permute-start(bf16[128,2048]{1,0:T(8,128)(2,1)S(1)} %collective-permute-done.1.refs_12_.refs_18_.refs_7_.refs_4_), channel_id=1, source_target_pairs={{1,0},{0,1},{3,2},{2,3},{5,4},{4,5},{7,6},{6,7},{9,8},{8,9},{11,10... | collective-permute-start | bytes 1572872 | tf_op jit(solution)/shard_map/ppermute | solution.py:153
  59.6 22.0 %collective-permute-start.18 = (bf16[128,2048]{1,0:T(8,128)(2,1)S(1)}, bf16[128,2048]{1,0:T(8,128)(2,1)}, u32[]{:S(2)}, u32[]{:S(2)}) collective-permute-start(bf16[128,2048]{1,0:T(8,128)(2,1)S(1)} %collective-permute-done.1.refs_12_.refs_18_.refs_7_.refs_4_), channel_id=1, source_target_pairs={{4,0},{0,4},{5,1},{1,5},{6,2},{2,6},{7,3},{3,7},{12,8},{8,12},{13,... | collective-permute-start | bytes 1572872 | tf_op jit(solution)/shard_map/ppermute | solution.py:146
  61.0 20.7 %collective-permute-start.19 = (bf16[128,2048]{1,0:T(8,128)(2,1)S(1)}, bf16[128,2048]{1,0:T(8,128)(2,1)}, u32[]{:S(2)}, u32[]{:S(2)}) collective-permute-start(bf16[128,2048]{1,0:T(8,128)(2,1)S(1)} %collective-permute-done.1.refs_12_.refs_18_.refs_7_.refs_4_), channel_id=1, source_target_pairs={{2,0},{3,1},{0,2},{1,3},{6,4},{7,5},{4,6},{5,7},{10,8},{11,9},{8,1... | collective-permute-start | bytes 1572872 | tf_op jit(solution)/shard_map/ppermute | solution.py:150
  63.5 12.6 %collective-permute-start.23 = (bf16[64,2048]{1,0:T(8,128)(2,1)}, bf16[64,2048]{1,0:T(8,128)(2,1)S(1)}, u32[]{:S(2)}, u32[]{:S(2)}) collective-permute-start(bf16[64,2048]{1,0:T(8,128)(2,1)} %copy-done.8), channel_id=1, source_target_pairs={{8,0},{0,8},{24,16},{16,24},{9,1},{1,9},{25,17},{17,25},{10,2},{2,... | collective-permute-start | bytes 786440 | tf_op jit(solution)/shard_map/ppermute | solution.py:156
  64.9 12.9 %collective-permute-start.24 = (bf16[64,2048]{1,0:T(8,128)(2,1)S(1)}, bf16[64,2048]{1,0:T(8,128)(2,1)S(1)}, u32[]{:S(2)}, u32[]{:S(2)}) collective-permute-start(bf16[64,2048]{1,0:T(8,128)(2,1)S(1)} %collective-permute-done.3.refs_9_.refs_7_.refs_5_), channel_id=1, source_target_pairs={{8,0},{0,8},{24,16},{16,24},{9,1},{1,9},{25,17},{17,25},{10,2},{2,... | collective-permute-start | bytes 786440 | tf_op jit(solution)/shard_map/ppermute | solution.py:156
  84.3 16.2 %collective-permute-start.29 = (f32[128,2048]{1,0:T(8,128)S(1)}, f32[128,2048]{1,0:T(8,128)S(1)}, u32[]{:S(2)}, u32[]{:S(2)}) collective-permute-start(f32[128,2048]{1,0:T(8,128)S(1)} %get-tuple-element.30), channel_id=1, source_target_pairs={{1,0},{0,1},{3,2},{2,3},{5,4},{4,5},{7,6},{6,7},{9,8},{8,9},{11,10... | collective-permute-start | bytes 3145736 | tf_op jit(solution)/shard_map/ppermute | solution.py:153
  84.4 9.5 %collective-permute-start.14 = (bf16[64,2048]{1,0:T(8,128)(2,1)}, bf16[64,2048]{1,0:T(8,128)(2,1)S(1)}, u32[]{:S(2)}, u32[]{:S(2)}) collective-permute-start(bf16[64,2048]{1,0:T(8,128)(2,1)} %collective-permute-done.13.refs_16_), channel_id=1, source_target_pairs={{8,0},{0,8},{24,16},{16,24},{9,1},{1,9},{25,17},{17,25},{10,2},{2,... | collective-permute-start | bytes 786440 | tf_op jit(solution)/shard_map/ppermute | solution.py:156
  85.5 13.4 %collective-permute-start.7 = (bf16[64,2048]{1,0:T(8,128)(2,1)}, bf16[64,2048]{1,0:T(8,128)(2,1)S(1)}, u32[]{:S(2)}, u32[]{:S(2)}) collective-permute-start(bf16[64,2048]{1,0:T(8,128)(2,1)} %collective-permute-done.6.refs_17_), channel_id=1, source_target_pairs={{8,0},{0,8},{24,16},{16,24},{9,1},{1,9},{25,17},{17,25},{10,2},{2,... | collective-permute-start | bytes 786440 | tf_op jit(solution)/shard_map/ppermute | solution.py:156
  86.5 12.5 %collective-permute-start.11 = (bf16[64,2048]{1,0:T(8,128)(2,1)S(1)}, bf16[64,2048]{1,0:T(8,128)(2,1)S(1)}, u32[]{:S(2)}, u32[]{:S(2)}) collective-permute-start(bf16[64,2048]{1,0:T(8,128)(2,1)S(1)} %copy-done.10), channel_id=1, source_target_pairs={{1,0},{0,1},{3,2},{2,3},{5,4},{4,5},{7,6},{6,7},{9,8},{8,9},{11,10... | collective-permute-start | bytes 786440 | tf_op jit(solution)/shard_map/ppermute | solution.py:153
  93.9 5.1 %collective-permute-start.15 = (bf16[64,2048]{1,0:T(8,128)(2,1)S(1)}, bf16[64,2048]{1,0:T(8,128)(2,1)S(1)}, u32[]{:S(2)}, u32[]{:S(2)}) collective-permute-start(bf16[64,2048]{1,0:T(8,128)(2,1)S(1)} %collective-permute-done.14.refs_7_), channel_id=1, source_target_pairs={{1,0},{0,1},{3,2},{2,3},{5,4},{4,5},{7,6},{6,7},{9,8},{8,9},{11,10... | collective-permute-start | bytes 786440 | tf_op jit(solution)/shard_map/ppermute | solution.py:153
  93.9 6.3 %collective-permute-start.4 = (bf16[64,2048]{1,0:T(8,128)(2,1)S(1)}, bf16[64,2048]{1,0:T(8,128)(2,1)S(1)}, u32[]{:S(2)}, u32[]{:S(2)}) collective-permute-start(bf16[64,2048]{1,0:T(8,128)(2,1)S(1)} %collective-permute-done.3.refs_9_.refs_7_.refs_5_), channel_id=1, source_target_pairs={{1,0},{0,1},{3,2},{2,3},{5,4},{4,5},{7,6},{6,7},{9,8},{8,9},{11,10... | collective-permute-start | bytes 786440 | tf_op jit(solution)/shard_map/ppermute | solution.py:153
  98.9 1.5 %collective-permute-start.8 = (bf16[64,2048]{1,0:T(8,128)(2,1)S(1)}, bf16[64,2048]{1,0:T(8,128)(2,1)S(1)}, u32[]{:S(2)}, u32[]{:S(2)}) collective-permute-start(bf16[64,2048]{1,0:T(8,128)(2,1)S(1)} %collective-permute-done.7.refs_7_), channel_id=1, source_target_pairs={{1,0},{0,1},{3,2},{2,3},{5,4},{4,5},{7,6},{6,7},{9,8},{8,9},{11,10... | collective-permute-start | bytes 786440 | tf_op jit(solution)/shard_map/ppermute | solution.py:153
  (19 other events, 31.0 us)

commit v3 on v2

--- a/solution.py
+++ b/solution.py
@@ -21,7 +21,7 @@
     index = index_ref[...]
     width = index.shape[1]
 
-    lanes = 8
+    lanes = 16
     share = vir_ref.shape[0] // lanes
 
     def step(k, found):
@@ -31,7 +31,7 @@
         )
 
     zero = jnp.zeros(index.shape, jnp.float32)
-    found = lax.fori_loop(0, share, step, (zero,) * lanes, unroll=4)
+    found = lax.fori_loop(0, share, step, (zero,) * lanes, unroll=2)
     energy = sum(found[1:], found[0])
 
     def block(dx, dy, flip):
@@ -50,7 +50,8 @@
                 col_ref[p : p + 1, :] = block(dx, dy, flip)
     for d in range(STEPS):
         far = partner(occ, d, occ_count)
-        pair_ref[d] = occ_ref[occ_index_ref[occ]] + occ_ref[occ_index_ref[far]]
+        pair = occ_ref[occ_index_ref[occ]] + occ_ref[occ_index_ref[far]]
+        pair_ref[d : d + 1, :] = jnp.full((1, width), pair, jnp.float32)
 
 
 def needed(blocks):
@@ -86,7 +87,7 @@
             swapped = direct
         for k, p in enumerate(ps):
             cut = slice(k * count, (k + 1) * count)
-            gap = pair_energy[d] - row_energy[...] - col_energy[p : p + 1, :]
+            gap = pair_energy[d : d + 1, :] - row_energy[...] - col_energy[p : p + 1, :]
             weights.append(((2.0 * direct[:, cut] - swapped[:, cut]) / gap).astype(jnp.bfloat16))
     weights = jnp.concatenate(weights, axis=1)
     columns = stack([r for d, ps in blocks for p in ps for r in far[d, p]])
@@ -111,7 +112,8 @@
     )
     table = jnp.concatenate([col_energy[p : p + 1, cut] for p, cut in cuts], axis=1)
     row = jnp.concatenate([row_energy[:count, cut] for _, cut in cuts], axis=1)
-    gap = pair_energy[label] - row - table
+    pair = jnp.concatenate([pair_energy[label : label + 1, cut] for _, cut in cuts], axis=1)
+    gap = pair - row - table
     weights = ((2.0 * direct - swapped) / gap).astype(jnp.bfloat16)
     if not final:
         sums, out = refs
@@ -195,12 +197,12 @@
         return pl.pallas_call(
             functools.partial(prepare, (va_count, chip_count, occ_count), partner),
             out_shape=(
-                jax.ShapeDtypeStruct((STEPS,), f32),
+                jax.ShapeDtypeStruct((STEPS, width), f32),
                 jax.ShapeDtypeStruct((CORES * width, width), f32),
                 jax.ShapeDtypeStruct((CORES * len(plane_of), width), f32),
             ),
             in_specs=[whole, scalar, scalar, scalar],
-            out_specs=(scalar, whole, whole),
+            out_specs=(whole, whole, whole),
             cost_estimate=pl.CostEstimate(
                 flops=3 * vir_index.shape[0] ** 2, bytes_accessed=1 << 18, transcendentals=0
             ),
@@ -224,7 +226,7 @@
         return pl.pallas_call(
             functools.partial(contract, blocks, parts, sums is None),
             out_shape=(total, total),
-            in_specs=[scalar] + [whole] * (len(operands) - 1),
+            in_specs=[whole] * len(operands),
             out_specs=(whole, whole),
             input_output_aliases=aliases,
             cost_estimate=pl.CostEstimate(
@@ -270,7 +272,7 @@
         return pl.pallas_call(
             functools.partial(finish, 3, [(row, cut) for row in rows], final),
             out_shape=total,
-            in_specs=[scalar] + [whole] * (len(operands) - 1),
+            in_specs=[whole] * len(operands),
             out_specs=pl.BlockSpec(memory_space=pl.ANY) if final else whole,
             scratch_shapes=[pltpu.VMEM(total.shape, f32), pltpu.SemaphoreType.DMA((4,))]
             if final

time: 103 us -> 102 us (level)
  Pallas kernels: 20.1 us -> 18 us
    pallas_call x5, Pallas kernels: 14.3 us -> 13.2 us  [add(): pl.pallas_call(functools.partial(contract, blocks, parts, sums is None),...]
    pallas_call x2, Pallas kernels: 3.32 us -> 2.25 us  [late(): pl.pallas_call(functools.partial(finish, 3, [(row, cut) for row in rows],...]
    unnamed x42 -> x44, local copies, waits for them, and re-layouts: 7.85 us -> 8.57 us
  transfers between devices with their start and end apart: 30 -> 30, of which waited for: 10 -> 10; matrix products, arithmetic and copies ran while one was open for 0% -> 0% of each run, Pallas kernels for 15% -> 13%
where the time goes in v3:
time: 102 us
  waiting for transfers between devices  48.5 us (48%)
  starting transfers between devices  26.7 us (26%)
  Pallas kernels  18 us (18%)
  local copies, waits for them, and re-layouts  8.64 us (8%)
    ppermute x7, waiting for transfers between devices, from_occ(): lax.ppermute(block, 'occ', [(partner(i, step, occ_count), i) for i in ran...  26.2 us
    pallas_call x5, Pallas kernels, add(): pl.pallas_call(functools.partial(contract, blocks, parts, sums is None),...  13.2 us
    ppermute x7, waiting for transfers between devices, from_vb(): lax.ppermute(block, 'vb', [((i - move) % vb_count, i) for i in range(vb_c...  11.7 us
    ppermute x7, starting transfers between devices, from_vb(): lax.ppermute(block, 'vb', [((i - move) % vb_count, i) for i in range(vb_c...  10.7 us
    ppermute x7, waiting for transfers between devices, from_va(): lax.ppermute(block, 'va', [((i - step) % va_count, i) for i in range(va_c...  9.73 us
    ppermute x7, starting transfers between devices, from_occ(): lax.ppermute(block, 'occ', [(partner(i, step, occ_count), i) for i in ran...  9 us
    unnamed x44, local copies, waits for them, and re-layouts  8.57 us
    ppermute x7, starting transfers between devices, from_va(): lax.ppermute(block, 'va', [((i - step) % va_count, i) for i in range(va_c...  6.36 us
  transfers between devices with their start and end apart: 30, of which 10 were waited for; matrix products, arithmetic and copies ran while one was open for 0% of the time, Pallas kernels for 13%

profile of v3, /device:TPU:0, one launch (start us, length us, event | category | flops | bytes accessed | tf_op | source)
XLA Modules:
  0.0 102.0 jit_solution(17013225629569242646)
XLA Ops:
  0.0 3.0 %collective-permute-start.9 = (bf16[128,2048]{1,0:T(8,128)(2,1)}, bf16[128,2048]{1,0:T(8,128)(2,1)S(1)}, u32[]{:S(2)}, u32[]{:S(2)}) collective-permute-start(bf16[128,2048]{1,0:T(8,128)(2,1)} %bitcast.3), channel_id=1, source_target_pairs={{2,0},{3,1},{0,2},{1,3},{6,4},{7,5},{4,6},{5,7},{10,8},{11,9},{8,1... | collective-permute-start | bytes 1572872 | tf_op jit(solution)/shard_map/ppermute | solution.py:152
  3.0 1.5 %collective-permute-start.2 = (bf16[128,2048]{1,0:T(8,128)(2,1)}, bf16[128,2048]{1,0:T(8,128)(2,1)S(1)}, u32[]{:S(2)}, u32[]{:S(2)}) collective-permute-start(bf16[128,2048]{1,0:T(8,128)(2,1)} %bitcast.4), channel_id=1, source_target_pairs={{4,0},{0,4},{5,1},{1,5},{6,2},{2,6},{7,3},{3,7},{12,8},{8,12},{13,... | collective-permute-start | bytes 1572872 | tf_op jit(solution)/shard_map/ppermute | solution.py:148
  4.5 2.6 %collective-permute-start = (bf16[128,2048]{1,0:T(8,128)(2,1)}, bf16[128,2048]{1,0:T(8,128)(2,1)S(1)}, u32[]{:S(2)}, u32[]{:S(2)}) collective-permute-start(bf16[128,2048]{1,0:T(8,128)(2,1)} %bitcast.5), channel_id=1, source_target_pairs={{16,0},{24,8},{0,16},{8,24},{17,1},{25,9},{1,17},{9,25},{18,2},{26... | collective-permute-start | bytes 1572872 | tf_op jit(solution)/shard_map/ppermute | solution.py:158
  7.1 1.6 %collective-permute-start.20 = (bf16[128,2048]{1,0:T(8,128)(2,1)}, bf16[128,2048]{1,0:T(8,128)(2,1)S(1)}, u32[]{:S(2)}, u32[]{:S(2)}) collective-permute-start(bf16[128,2048]{1,0:T(8,128)(2,1)} %bitcast.7), channel_id=1, source_target_pairs={{8,0},{0,8},{24,16},{16,24},{9,1},{1,9},{25,17},{17,25},{10,2},{2,... | collective-permute-start | bytes 1572872 | tf_op jit(solution)/shard_map/ppermute | solution.py:158
  8.7 6.5 %collective-permute-done.9.refs_7_.refs_6_.refs_5_ = bf16[128,2048]{1,0:T(8,128)(2,1)S(1)} collective-permute-done((bf16[128,2048]{1,0:T(8,128)(2,1)}, bf16[128,2048]{1,0:T(8,128)(2,1)S(1)}, u32[]{:S(2)}, u32[]{:S(2)}) %collective-permute-start.9) | collective-permute-done | bytes 524320 | tf_op jit(solution)/shard_map/ppermute | solution.py:152
  15.1 1.8 %collective-permute-start.10 = (bf16[64,2048]{1,0:T(8,128)(2,1)S(1)}, bf16[64,2048]{1,0:T(8,128)(2,1)S(1)}, u32[]{:S(2)}, u32[]{:S(2)}) collective-permute-start(bf16[64,2048]{1,0:T(8,128)(2,1)S(1)} %slice.18), channel_id=1, source_target_pairs={{4,0},{0,4},{5,1},{1,5},{6,2},{2,6},{7,3},{3,7},{12,8},{8,12},{13,... | collective-permute-start | bytes 786440 | tf_op jit(solution)/shard_map/ppermute | solution.py:148
  17.0 1.6 %collective-permute-start.3 = (bf16[64,2048]{1,0:T(8,128)(2,1)S(1)}, bf16[64,2048]{1,0:T(8,128)(2,1)S(1)}, u32[]{:S(2)}, u32[]{:S(2)}) collective-permute-start(bf16[64,2048]{1,0:T(8,128)(2,1)S(1)} %slice.16), channel_id=1, source_target_pairs={{2,0},{3,1},{0,2},{1,3},{6,4},{7,5},{4,6},{5,7},{10,8},{11,9},{8,1... | collective-permute-start | bytes 786440 | tf_op jit(solution)/shard_map/ppermute | solution.py:152
  18.6 11.5 %collective-permute-done.refs_8_.refs_10_ = bf16[128,2048]{1,0:T(8,128)(2,1)S(1)} collective-permute-done((bf16[128,2048]{1,0:T(8,128)(2,1)}, bf16[128,2048]{1,0:T(8,128)(2,1)S(1)}, u32[]{:S(2)}, u32[]{:S(2)}) %collective-permute-start) | collective-permute-done | bytes 524320 | tf_op jit(solution)/shard_map/ppermute | solution.py:158
  31.7 0.9 collective-permute-start.25
  32.7 1.5 %collective-permute-start.26 = (bf16[64,2048]{1,0:T(8,128)(2,1)S(1)}, bf16[64,2048]{1,0:T(8,128)(2,1)S(1)}, u32[]{:S(2)}, u32[]{:S(2)}) collective-permute-start(bf16[64,2048]{1,0:T(8,128)(2,1)S(1)} %get-tuple-element.32), channel_id=1, source_target_pairs={{2,0},{3,1},{0,2},{1,3},{6,4},{7,5},{4,6},{5,7},{10,8},{11,9},{8,1... | collective-permute-start | bytes 786440 | tf_op jit(solution)/shard_map/ppermute | solution.py:152
  34.2 5.2 %collective-permute-done.12.refs_13_ = bf16[64,2048]{1,0:T(8,128)(2,1)} collective-permute-done((bf16[64,2048]{1,0:T(8,128)(2,1)S(1)}, bf16[64,2048]{1,0:T(8,128)(2,1)}, u32[]{:S(2)}, u32[]{:S(2)}) %collective-permute-start.12) | collective-permute-done | bytes 262176 | tf_op jit(solution)/shard_map/ppermute | solution.py:152
  40.7 4.8 %collective-permute-done.25.refs_11_ = bf16[64,2048]{1,0:T(8,128)(2,1)S(1)} collective-permute-done((bf16[64,2048]{1,0:T(8,128)(2,1)S(1)}, bf16[64,2048]{1,0:T(8,128)(2,1)S(1)}, u32[]{:S(2)}, u32[]{:S(2)}) %collective-permute-start.25) | collective-permute-done | bytes 262176 | tf_op jit(solution)/shard_map/ppermute | solution.py:148
  46.2 1.5 %collective-permute-start.28 = (bf16[128,2048]{1,0:T(8,128)(2,1)S(1)}, bf16[128,2048]{1,0:T(8,128)(2,1)S(1)}, u32[]{:S(2)}, u32[]{:S(2)}) collective-permute-start(bf16[128,2048]{1,0:T(8,128)(2,1)S(1)} %collective-permute-done.20.refs_8_.refs_10_), channel_id=1, source_target_pairs={{2,0},{3,1},{0,2},{1,3},{6,4},{7,5},{4,6},{5,7},{10,8},{11,9},{8,1... | collective-permute-start | bytes 1572872 | tf_op jit(solution)/shard_map/ppermute | solution.py:152
  49.2 0.8 copy-done.4
  50.5 4.9 %collective-permute-done.27.refs_11_ = bf16[128,2048]{1,0:T(8,128)(2,1)S(1)} collective-permute-done((bf16[128,2048]{1,0:T(8,128)(2,1)S(1)}, bf16[128,2048]{1,0:T(8,128)(2,1)S(1)}, u32[]{:S(2)}, u32[]{:S(2)}) %collective-permute-start.27) | collective-permute-done | bytes 524320 | tf_op jit(solution)/shard_map/ppermute | solution.py:148
  56.3 2.5 %collective-permute-start.6 = (bf16[64,2048]{1,0:T(8,128)(2,1)}, bf16[64,2048]{1,0:T(8,128)(2,1)}, u32[]{:S(2)}, u32[]{:S(2)}) collective-permute-start(bf16[64,2048]{1,0:T(8,128)(2,1)} %collective-permute-done.5.refs_12_), channel_id=1, source_target_pairs={{2,0},{3,1},{0,2},{1,3},{6,4},{7,5},{4,6},{5,7},{10,8},{11,9},{8,1... | collective-permute-start | bytes 786440 | tf_op jit(solution)/shard_map/ppermute | solution.py:152
  61.0 2.5 %shard_map.55 = (f32[4,128]{1,0:T(4,128)}, f32[256,128]{1,0:T(8,128)}, f32[8,128]{1,0:T(8,128)}) custom-call(s32[8,128]{1,0:T(8,128)} %bitcast.19, f32[1024]{0:T(1024)} %vir_ref.1, s32[4]{0:T(128)} %occ_index_ref.1, f32[4]{0:T(128)} %occ_ref.1), custom_call_target="tpu_custom_call" | custom-call | flops 3145728 | bytes 262144 | tf_op jit(solution)/shard_map/pallas_call | solution.py:197
  63.5 1.4 %collective-permute-start.23 = (bf16[64,2048]{1,0:T(8,128)(2,1)}, bf16[64,2048]{1,0:T(8,128)(2,1)S(1)}, u32[]{:S(2)}, u32[]{:S(2)}) collective-permute-start(bf16[64,2048]{1,0:T(8,128)(2,1)} %copy-done.8), channel_id=1, source_target_pairs={{8,0},{0,8},{24,16},{16,24},{9,1},{1,9},{25,17},{17,25},{10,2},{2,... | collective-permute-start | bytes 786440 | tf_op jit(solution)/shard_map/ppermute | solution.py:158
  65.6 0.9 copy-done.1
  66.5 0.9 copy-done.9
  68.1 1.4 %shard_map.56 = (f32[128,2048]{1,0:T(8,128)S(1)}, f32[128,2048]{1,0:T(8,128)S(1)}) custom-call(f32[4,128]{1,0:T(4,128)S(1)} %copy-done.20, f32[256,128]{1,0:T(8,128)S(1)} %copy-done.1, f32[8,128]{1,0:T(8,128)S(1)} %copy-done.19, bf16[128,2048]{1,0:T(8,128)(2,1)S(1)} %bitcast.8, bf16[128,2048]{1,0:T(8,128)(2,1)S(1)} %collective-permute-done.16.refs_4_, ...), custom_call_target="tpu_custom_call" | custom-call | flops 1610612736 | bytes 4194304 | tf_op jit(solution)/shard_map/pallas_call | solution.py:226
  70.2 2.1 %shard_map.57 = (f32[128,2048]{1,0:T(8,128)S(1)}, f32[128,2048]{1,0:T(8,128)S(1)}) custom-call(f32[4,128]{1,0:T(4,128)S(1)} %copy-done.21, f32[256,128]{1,0:T(8,128)S(1)} %copy-done.1, f32[8,128]{1,0:T(8,128)S(1)} %copy-done.19, bf16[128,2048]{1,0:T(8,128)(2,1)S(1)} %bitcast.10, ...), custom_call_target="tpu_custom_call", output_to_operand_aliasing={{0}: (13, {}), {1}: (14, {})} | custom-call | flops 1207959552 | bytes 3145728 | tf_op jit(solution)/shard_map/pallas_call | solution.py:226
  72.4 3.2 %shard_map.58 = (f32[128,2048]{1,0:T(8,128)S(1)}, f32[128,2048]{1,0:T(8,128)S(1)}) custom-call(f32[4,128]{1,0:T(4,128)S(1)} %copy-done.21, f32[256,128]{1,0:T(8,128)S(1)} %copy-done.1, f32[8,128]{1,0:T(8,128)S(1)} %copy-done.19, bf16[128,2048]{1,0:T(8,128)(2,1)S(1)} %bitcast.12, ...), custom_call_target="tpu_custom_call", output_to_operand_aliasing={{0}: (15, {}), {1}: (16, {})} | custom-call | flops 1207959552 | bytes 3145728 | tf_op jit(solution)/shard_map/pallas_call | solution.py:226
  75.6 2.2 %collective-permute-done.24.refs_15_ = bf16[64,2048]{1,0:T(8,128)(2,1)S(1)} collective-permute-done((bf16[64,2048]{1,0:T(8,128)(2,1)S(1)}, bf16[64,2048]{1,0:T(8,128)(2,1)S(1)}, u32[]{:S(2)}, u32[]{:S(2)}) %collective-permute-start.24) | collective-permute-done | bytes 262176 | tf_op jit(solution)/shard_map/ppermute | solution.py:158
  77.8 3.8 %shard_map.59 = (f32[128,2048]{1,0:T(8,128)S(1)}, f32[128,2048]{1,0:T(8,128)S(1)}) custom-call(f32[4,128]{1,0:T(4,128)S(1)} %copy-done.21, f32[256,128]{1,0:T(8,128)S(1)} %copy-done.1, f32[8,128]{1,0:T(8,128)S(1)} %copy-done.19, bf16[128,2048]{1,0:T(8,128)(2,1)S(1)} %bitcast.14, ...), custom_call_target="tpu_custom_call", output_to_operand_aliasing={{0}: (19, {}), {1}: (20, {})} | custom-call | flops 1207959552 | bytes 3145728 | tf_op jit(solution)/shard_map/pallas_call | solution.py:226
  81.7 2.6 %shard_map.60 = (f32[128,2048]{1,0:T(8,128)S(1)}, f32[128,2048]{1,0:T(8,128)S(1)}) custom-call(f32[4,128]{1,0:T(4,128)S(1)} %copy-done.21, f32[256,128]{1,0:T(8,128)S(1)} %copy-done.1, f32[8,128]{1,0:T(8,128)S(1)} %copy-done.19, bf16[128,2048]{1,0:T(8,128)(2,1)S(1)} %bitcast.16, ...), custom_call_target="tpu_custom_call", output_to_operand_aliasing={{0}: (11, {}), {1}: (12, {})} | custom-call | flops 805306368 | bytes 2097152 | tf_op jit(solution)/shard_map/pallas_call | solution.py:226
  84.4 1.2 %collective-permute-start.14 = (bf16[64,2048]{1,0:T(8,128)(2,1)}, bf16[64,2048]{1,0:T(8,128)(2,1)S(1)}, u32[]{:S(2)}, u32[]{:S(2)}) collective-permute-start(bf16[64,2048]{1,0:T(8,128)(2,1)} %collective-permute-done.13.refs_16_), channel_id=1, source_target_pairs={{8,0},{0,8},{24,16},{16,24},{9,1},{1,9},{25,17},{17,25},{10,2},{2,... | collective-permute-start | bytes 786440 | tf_op jit(solution)/shard_map/ppermute | solution.py:158
  85.5 0.9 collective-permute-start.7
  86.5 7.4 %collective-permute-done.14.refs_7_ = bf16[64,2048]{1,0:T(8,128)(2,1)S(1)} collective-permute-done((bf16[64,2048]{1,0:T(8,128)(2,1)}, bf16[64,2048]{1,0:T(8,128)(2,1)S(1)}, u32[]{:S(2)}, u32[]{:S(2)}) %collective-permute-start.14) | collective-permute-done | bytes 262176 | tf_op jit(solution)/shard_map/ppermute | solution.py:158
  94.3 4.6 %collective-permute-done.7.refs_7_ = bf16[64,2048]{1,0:T(8,128)(2,1)S(1)} collective-permute-done((bf16[64,2048]{1,0:T(8,128)(2,1)}, bf16[64,2048]{1,0:T(8,128)(2,1)S(1)}, u32[]{:S(2)}, u32[]{:S(2)}) %collective-permute-start.7) | collective-permute-done | bytes 262176 | tf_op jit(solution)/shard_map/ppermute | solution.py:158
  99.6 0.8 collective-permute-done.8.refs_8_
  100.4 1.6 %shard_map.62 = f32[128,2048]{1,0:T(8,128)} custom-call(f32[4,128]{1,0:T(4,128)S(1)} %copy-done.21, f32[256,128]{1,0:T(8,128)S(1)} %copy-done.1, f32[8,128]{1,0:T(8,128)S(1)} %copy-done.19, bf16[128,2048]{1,0:T(8,128)(2,1)S(1)} %bitcast.18, bf16[128,2048]{1,0:T(8,128)(2,1)S(1)} %collective-permute-done.1.refs_12_.refs_18_.refs_7_.refs_4_, ...), custom_call_target="tpu_custom_call" | custom-call | flops 201326592 | bytes 1048576 | tf_op jit(solution)/shard_map/pallas_call | solution.py:272
  (83 shorter events, 12.0 us)
Async XLA Ops:
  0.0 15.1 %collective-permute-start.9 = (bf16[128,2048]{1,0:T(8,128)(2,1)}, bf16[128,2048]{1,0:T(8,128)(2,1)S(1)}, u32[]{:S(2)}, u32[]{:S(2)}) collective-permute-start(bf16[128,2048]{1,0:T(8,128)(2,1)} %bitcast.3), channel_id=1, source_target_pairs={{2,0},{3,1},{0,2},{1,3},{6,4},{7,5},{4,6},{5,7},{10,8},{11,9},{8,1... | collective-permute-start | bytes 1572872 | tf_op jit(solution)/shard_map/ppermute | solution.py:152
  3.0 13.9 %collective-permute-start.2 = (bf16[128,2048]{1,0:T(8,128)(2,1)}, bf16[128,2048]{1,0:T(8,128)(2,1)S(1)}, u32[]{:S(2)}, u32[]{:S(2)}) collective-permute-start(bf16[128,2048]{1,0:T(8,128)(2,1)} %bitcast.4), channel_id=1, source_target_pairs={{4,0},{0,4},{5,1},{1,5},{6,2},{2,6},{7,3},{3,7},{12,8},{8,12},{13,... | collective-permute-start | bytes 1572872 | tf_op jit(solution)/shard_map/ppermute | solution.py:148
  4.5 25.6 %collective-permute-start = (bf16[128,2048]{1,0:T(8,128)(2,1)}, bf16[128,2048]{1,0:T(8,128)(2,1)S(1)}, u32[]{:S(2)}, u32[]{:S(2)}) collective-permute-start(bf16[128,2048]{1,0:T(8,128)(2,1)} %bitcast.5), channel_id=1, source_target_pairs={{16,0},{24,8},{0,16},{8,24},{17,1},{25,9},{1,17},{9,25},{18,2},{26... | collective-permute-start | bytes 1572872 | tf_op jit(solution)/shard_map/ppermute | solution.py:158
  7.1 23.6 %collective-permute-start.16 = (bf16[128,2048]{1,0:T(8,128)(2,1)}, bf16[128,2048]{1,0:T(8,128)(2,1)S(1)}, u32[]{:S(2)}, u32[]{:S(2)}) collective-permute-start(bf16[128,2048]{1,0:T(8,128)(2,1)} %bitcast.6), channel_id=1, source_target_pairs={{1,0},{0,1},{3,2},{2,3},{5,4},{4,5},{7,6},{6,7},{9,8},{8,9},{11,10... | collective-permute-start | bytes 1572872 | tf_op jit(solution)/shard_map/ppermute | solution.py:155
  7.1 24.7 %collective-permute-start.20 = (bf16[128,2048]{1,0:T(8,128)(2,1)}, bf16[128,2048]{1,0:T(8,128)(2,1)S(1)}, u32[]{:S(2)}, u32[]{:S(2)}) collective-permute-start(bf16[128,2048]{1,0:T(8,128)(2,1)} %bitcast.7), channel_id=1, source_target_pairs={{8,0},{0,8},{24,16},{16,24},{9,1},{1,9},{25,17},{17,25},{10,2},{2,... | collective-permute-start | bytes 1572872 | tf_op jit(solution)/shard_map/ppermute | solution.py:158
  15.1 17.6 %collective-permute-start.10 = (bf16[64,2048]{1,0:T(8,128)(2,1)S(1)}, bf16[64,2048]{1,0:T(8,128)(2,1)S(1)}, u32[]{:S(2)}, u32[]{:S(2)}) collective-permute-start(bf16[64,2048]{1,0:T(8,128)(2,1)S(1)} %slice.18), channel_id=1, source_target_pairs={{4,0},{0,4},{5,1},{1,5},{6,2},{2,6},{7,3},{3,7},{12,8},{8,12},{13,... | collective-permute-start | bytes 786440 | tf_op jit(solution)/shard_map/ppermute | solution.py:148
  17.0 48.6 %copy-start = (bf16[1,128,2048]{2,1,0:T(8,128)(2,1)S(1)}, bf16[1,128,2048]{2,1,0:T(8,128)(2,1)}, u32[]{:S(2)}) copy-start(bf16[1,128,2048]{2,1,0:T(8,128)(2,1)} %param.5) | copy-start | bytes 1572868
  17.0 17.3 %collective-permute-start.3 = (bf16[64,2048]{1,0:T(8,128)(2,1)S(1)}, bf16[64,2048]{1,0:T(8,128)(2,1)S(1)}, u32[]{:S(2)}, u32[]{:S(2)}) collective-permute-start(bf16[64,2048]{1,0:T(8,128)(2,1)S(1)} %slice.16), channel_id=1, source_target_pairs={{2,0},{3,1},{0,2},{1,3},{6,4},{7,5},{4,6},{5,7},{10,8},{11,9},{8,1... | collective-permute-start | bytes 786440 | tf_op jit(solution)/shard_map/ppermute | solution.py:152
  30.1 9.3 %collective-permute-start.12 = (bf16[64,2048]{1,0:T(8,128)(2,1)S(1)}, bf16[64,2048]{1,0:T(8,128)(2,1)}, u32[]{:S(2)}, u32[]{:S(2)}) collective-permute-start(bf16[64,2048]{1,0:T(8,128)(2,1)S(1)} %get-tuple-element.31), channel_id=1, source_target_pairs={{2,0},{3,1},{0,2},{1,3},{6,4},{7,5},{4,6},{5,7},{10,8},{11,9},{8,1... | collective-permute-start | bytes 786440 | tf_op jit(solution)/shard_map/ppermute | solution.py:152
  30.7 9.3 %collective-permute-start.5 = (bf16[64,2048]{1,0:T(8,128)(2,1)S(1)}, bf16[64,2048]{1,0:T(8,128)(2,1)}, u32[]{:S(2)}, u32[]{:S(2)}) collective-permute-start(bf16[64,2048]{1,0:T(8,128)(2,1)S(1)} %get-tuple-element.32), channel_id=1, source_target_pairs={{4,0},{0,4},{5,1},{1,5},{6,2},{2,6},{7,3},{3,7},{12,8},{8,12},{13,... | collective-permute-start | bytes 786440 | tf_op jit(solution)/shard_map/ppermute | solution.py:148
  31.7 13.7 %collective-permute-start.25 = (bf16[64,2048]{1,0:T(8,128)(2,1)S(1)}, bf16[64,2048]{1,0:T(8,128)(2,1)S(1)}, u32[]{:S(2)}, u32[]{:S(2)}) collective-permute-start(bf16[64,2048]{1,0:T(8,128)(2,1)S(1)} %get-tuple-element.31), channel_id=1, source_target_pairs={{4,0},{0,4},{5,1},{1,5},{6,2},{2,6},{7,3},{3,7},{12,8},{8,12},{13,... | collective-permute-start | bytes 786440 | tf_op jit(solution)/shard_map/ppermute | solution.py:148
  32.7 7.3 %copy-start.8 = (bf16[64,2048]{1,0:T(8,128)(2,1)}, bf16[64,2048]{1,0:T(8,128)(2,1)S(1)}, u32[]{:S(2)}) copy-start(bf16[64,2048]{1,0:T(8,128)(2,1)S(1)} %collective-permute-done.10.refs_8_.refs_6_.refs_5_) | copy-start | bytes 786436
  32.7 15.8 %collective-permute-start.26 = (bf16[64,2048]{1,0:T(8,128)(2,1)S(1)}, bf16[64,2048]{1,0:T(8,128)(2,1)S(1)}, u32[]{:S(2)}, u32[]{:S(2)}) collective-permute-start(bf16[64,2048]{1,0:T(8,128)(2,1)S(1)} %get-tuple-element.32), channel_id=1, source_target_pairs={{2,0},{3,1},{0,2},{1,3},{6,4},{7,5},{4,6},{5,7},{10,8},{11,9},{8,1... | collective-permute-start | bytes 786440 | tf_op jit(solution)/shard_map/ppermute | solution.py:152
  34.2 15.0 %collective-permute-start.21 = (bf16[128,2048]{1,0:T(8,128)(2,1)S(1)}, bf16[128,2048]{1,0:T(8,128)(2,1)S(1)}, u32[]{:S(2)}, u32[]{:S(2)}) collective-permute-start(bf16[128,2048]{1,0:T(8,128)(2,1)S(1)} %collective-permute-done.20.refs_8_.refs_10_), channel_id=1, source_target_pairs={{1,0},{0,1},{3,2},{2,3},{5,4},{4,5},{7,6},{6,7},{9,8},{8,9},{11,10... | collective-permute-start | bytes 1572872 | tf_op jit(solution)/shard_map/ppermute | solution.py:155
  39.4 16.0 %collective-permute-start.27 = (bf16[128,2048]{1,0:T(8,128)(2,1)S(1)}, bf16[128,2048]{1,0:T(8,128)(2,1)S(1)}, u32[]{:S(2)}, u32[]{:S(2)}) collective-permute-start(bf16[128,2048]{1,0:T(8,128)(2,1)S(1)} %collective-permute-done.20.refs_8_.refs_10_), channel_id=1, source_target_pairs={{4,0},{0,4},{5,1},{1,5},{6,2},{2,6},{7,3},{3,7},{12,8},{8,12},{13,... | collective-permute-start | bytes 1572872 | tf_op jit(solution)/shard_map/ppermute | solution.py:148
  40.0 18.8 %collective-permute-start.1 = (bf16[128,2048]{1,0:T(8,128)(2,1)S(1)}, bf16[128,2048]{1,0:T(8,128)(2,1)S(1)}, u32[]{:S(2)}, u32[]{:S(2)}) collective-permute-start(bf16[128,2048]{1,0:T(8,128)(2,1)S(1)} %collective-permute-done.refs_8_.refs_10_), channel_id=1, source_target_pairs={{8,0},{0,8},{24,16},{16,24},{9,1},{1,9},{25,17},{17,25},{10,2},{2,... | collective-permute-start | bytes 1572872 | tf_op jit(solution)/shard_map/ppermute | solution.py:158
  46.2 12.6 %collective-permute-start.28 = (bf16[128,2048]{1,0:T(8,128)(2,1)S(1)}, bf16[128,2048]{1,0:T(8,128)(2,1)S(1)}, u32[]{:S(2)}, u32[]{:S(2)}) collective-permute-start(bf16[128,2048]{1,0:T(8,128)(2,1)S(1)} %collective-permute-done.20.refs_8_.refs_10_), channel_id=1, source_target_pairs={{2,0},{3,1},{0,2},{1,3},{6,4},{7,5},{4,6},{5,7},{10,8},{11,9},{8,1... | collective-permute-start | bytes 1572872 | tf_op jit(solution)/shard_map/ppermute | solution.py:152
  49.2 11.0 %collective-permute-start.22 = (bf16[128,2048]{1,0:T(8,128)(2,1)S(1)}, bf16[128,2048]{1,0:T(8,128)(2,1)S(1)}, u32[]{:S(2)}, u32[]{:S(2)}) collective-permute-start(bf16[128,2048]{1,0:T(8,128)(2,1)S(1)} %collective-permute-done.refs_8_.refs_10_), channel_id=1, source_target_pairs={{1,0},{0,1},{3,2},{2,3},{5,4},{4,5},{7,6},{6,7},{9,8},{8,9},{11,10... | collective-permute-start | bytes 1572872 | tf_op jit(solution)/shard_map/ppermute | solution.py:155
  50.0 13.5 %collective-permute-start.13 = (bf16[64,2048]{1,0:T(8,128)(2,1)}, bf16[64,2048]{1,0:T(8,128)(2,1)}, u32[]{:S(2)}, u32[]{:S(2)}) collective-permute-start(bf16[64,2048]{1,0:T(8,128)(2,1)} %collective-permute-done.12.refs_13_), channel_id=1, source_target_pairs={{4,0},{0,4},{5,1},{1,5},{6,2},{2,6},{7,3},{3,7},{12,8},{8,12},{13,... | collective-permute-start | bytes 786440 | tf_op jit(solution)/shard_map/ppermute | solution.py:148
  56.3 8.6 %collective-permute-start.6 = (bf16[64,2048]{1,0:T(8,128)(2,1)}, bf16[64,2048]{1,0:T(8,128)(2,1)}, u32[]{:S(2)}, u32[]{:S(2)}) collective-permute-start(bf16[64,2048]{1,0:T(8,128)(2,1)} %collective-permute-done.5.refs_12_), channel_id=1, source_target_pairs={{2,0},{3,1},{0,2},{1,3},{6,4},{7,5},{4,6},{5,7},{10,8},{11,9},{8,1... | collective-permute-start | bytes 786440 | tf_op jit(solution)/shard_map/ppermute | solution.py:152
  58.8 19.0 %collective-permute-start.17 = (bf16[128,2048]{1,0:T(8,128)(2,1)S(1)}, bf16[128,2048]{1,0:T(8,128)(2,1)}, u32[]{:S(2)}, u32[]{:S(2)}) collective-permute-start(bf16[128,2048]{1,0:T(8,128)(2,1)S(1)} %collective-permute-done.1.refs_12_.refs_18_.refs_7_.refs_4_), channel_id=1, source_target_pairs={{1,0},{0,1},{3,2},{2,3},{5,4},{4,5},{7,6},{6,7},{9,8},{8,9},{11,10... | collective-permute-start | bytes 1572872 | tf_op jit(solution)/shard_map/ppermute | solution.py:155
  59.6 22.0 %collective-permute-start.18 = (bf16[128,2048]{1,0:T(8,128)(2,1)S(1)}, bf16[128,2048]{1,0:T(8,128)(2,1)}, u32[]{:S(2)}, u32[]{:S(2)}) collective-permute-start(bf16[128,2048]{1,0:T(8,128)(2,1)S(1)} %collective-permute-done.1.refs_12_.refs_18_.refs_7_.refs_4_), channel_id=1, source_target_pairs={{4,0},{0,4},{5,1},{1,5},{6,2},{2,6},{7,3},{3,7},{12,8},{8,12},{13,... | collective-permute-start | bytes 1572872 | tf_op jit(solution)/shard_map/ppermute | solution.py:148
  61.0 20.7 %collective-permute-start.19 = (bf16[128,2048]{1,0:T(8,128)(2,1)S(1)}, bf16[128,2048]{1,0:T(8,128)(2,1)}, u32[]{:S(2)}, u32[]{:S(2)}) collective-permute-start(bf16[128,2048]{1,0:T(8,128)(2,1)S(1)} %collective-permute-done.1.refs_12_.refs_18_.refs_7_.refs_4_), channel_id=1, source_target_pairs={{2,0},{3,1},{0,2},{1,3},{6,4},{7,5},{4,6},{5,7},{10,8},{11,9},{8,1... | collective-permute-start | bytes 1572872 | tf_op jit(solution)/shard_map/ppermute | solution.py:152
  63.5 12.1 %collective-permute-start.23 = (bf16[64,2048]{1,0:T(8,128)(2,1)}, bf16[64,2048]{1,0:T(8,128)(2,1)S(1)}, u32[]{:S(2)}, u32[]{:S(2)}) collective-permute-start(bf16[64,2048]{1,0:T(8,128)(2,1)} %copy-done.8), channel_id=1, source_target_pairs={{8,0},{0,8},{24,16},{16,24},{9,1},{1,9},{25,17},{17,25},{10,2},{2,... | collective-permute-start | bytes 786440 | tf_op jit(solution)/shard_map/ppermute | solution.py:158
  64.9 12.9 %collective-permute-start.24 = (bf16[64,2048]{1,0:T(8,128)(2,1)S(1)}, bf16[64,2048]{1,0:T(8,128)(2,1)S(1)}, u32[]{:S(2)}, u32[]{:S(2)}) collective-permute-start(bf16[64,2048]{1,0:T(8,128)(2,1)S(1)} %collective-permute-done.3.refs_9_.refs_7_.refs_5_), channel_id=1, source_target_pairs={{8,0},{0,8},{24,16},{16,24},{9,1},{1,9},{25,17},{17,25},{10,2},{2,... | collective-permute-start | bytes 786440 | tf_op jit(solution)/shard_map/ppermute | solution.py:158
  84.3 16.2 %collective-permute-start.29 = (f32[128,2048]{1,0:T(8,128)S(1)}, f32[128,2048]{1,0:T(8,128)S(1)}, u32[]{:S(2)}, u32[]{:S(2)}) collective-permute-start(f32[128,2048]{1,0:T(8,128)S(1)} %get-tuple-element.30), channel_id=1, source_target_pairs={{1,0},{0,1},{3,2},{2,3},{5,4},{4,5},{7,6},{6,7},{9,8},{8,9},{11,10... | collective-permute-start | bytes 3145736 | tf_op jit(solution)/shard_map/ppermute | solution.py:155
  84.4 9.5 %collective-permute-start.14 = (bf16[64,2048]{1,0:T(8,128)(2,1)}, bf16[64,2048]{1,0:T(8,128)(2,1)S(1)}, u32[]{:S(2)}, u32[]{:S(2)}) collective-permute-start(bf16[64,2048]{1,0:T(8,128)(2,1)} %collective-permute-done.13.refs_16_), channel_id=1, source_target_pairs={{8,0},{0,8},{24,16},{16,24},{9,1},{1,9},{25,17},{17,25},{10,2},{2,... | collective-permute-start | bytes 786440 | tf_op jit(solution)/shard_map/ppermute | solution.py:158
  85.5 13.4 %collective-permute-start.7 = (bf16[64,2048]{1,0:T(8,128)(2,1)}, bf16[64,2048]{1,0:T(8,128)(2,1)S(1)}, u32[]{:S(2)}, u32[]{:S(2)}) collective-permute-start(bf16[64,2048]{1,0:T(8,128)(2,1)} %collective-permute-done.6.refs_17_), channel_id=1, source_target_pairs={{8,0},{0,8},{24,16},{16,24},{9,1},{1,9},{25,17},{17,25},{10,2},{2,... | collective-permute-start | bytes 786440 | tf_op jit(solution)/shard_map/ppermute | solution.py:158
  86.5 12.5 %collective-permute-start.11 = (bf16[64,2048]{1,0:T(8,128)(2,1)S(1)}, bf16[64,2048]{1,0:T(8,128)(2,1)S(1)}, u32[]{:S(2)}, u32[]{:S(2)}) collective-permute-start(bf16[64,2048]{1,0:T(8,128)(2,1)S(1)} %copy-done.10), channel_id=1, source_target_pairs={{1,0},{0,1},{3,2},{2,3},{5,4},{4,5},{7,6},{6,7},{9,8},{8,9},{11,10... | collective-permute-start | bytes 786440 | tf_op jit(solution)/shard_map/ppermute | solution.py:155
  93.8 5.1 %collective-permute-start.15 = (bf16[64,2048]{1,0:T(8,128)(2,1)S(1)}, bf16[64,2048]{1,0:T(8,128)(2,1)S(1)}, u32[]{:S(2)}, u32[]{:S(2)}) collective-permute-start(bf16[64,2048]{1,0:T(8,128)(2,1)S(1)} %collective-permute-done.14.refs_7_), channel_id=1, source_target_pairs={{1,0},{0,1},{3,2},{2,3},{5,4},{4,5},{7,6},{6,7},{9,8},{8,9},{11,10... | collective-permute-start | bytes 786440 | tf_op jit(solution)/shard_map/ppermute | solution.py:155
  93.8 5.8 %collective-permute-start.4 = (bf16[64,2048]{1,0:T(8,128)(2,1)S(1)}, bf16[64,2048]{1,0:T(8,128)(2,1)S(1)}, u32[]{:S(2)}, u32[]{:S(2)}) collective-permute-start(bf16[64,2048]{1,0:T(8,128)(2,1)S(1)} %collective-permute-done.3.refs_9_.refs_7_.refs_5_), channel_id=1, source_target_pairs={{1,0},{0,1},{3,2},{2,3},{5,4},{4,5},{7,6},{6,7},{9,8},{8,9},{11,10... | collective-permute-start | bytes 786440 | tf_op jit(solution)/shard_map/ppermute | solution.py:155
  98.9 1.5 %collective-permute-start.8 = (bf16[64,2048]{1,0:T(8,128)(2,1)S(1)}, bf16[64,2048]{1,0:T(8,128)(2,1)S(1)}, u32[]{:S(2)}, u32[]{:S(2)}) collective-permute-start(bf16[64,2048]{1,0:T(8,128)(2,1)S(1)} %collective-permute-done.7.refs_7_), channel_id=1, source_target_pairs={{1,0},{0,1},{3,2},{2,3},{5,4},{4,5},{7,6},{6,7},{9,8},{8,9},{11,10... | collective-permute-start | bytes 786440 | tf_op jit(solution)/shard_map/ppermute | solution.py:155
  (20 other events, 28.4 us)

commit v4 on v3

--- a/solution.py
+++ b/solution.py
@@ -58,14 +58,14 @@
     return sorted({p for d, ps in blocks for p in ps if d > 0})
 
 
-def contract(blocks, parts, first, *refs):
+def contract(blocks, parts, first, halves, *refs):
     refs = list(refs)
     pair_energy, row_energy, col_energy = (refs.pop(0) for _ in range(3))
-    rows = [refs.pop(0), refs.pop(0)]
+    rows = [refs.pop(0) for _ in halves]
     near = {p: [refs.pop(0) for _ in range(parts[0, p])] for p in needed(blocks)}
-    far_rows = {d: [refs.pop(0), refs.pop(0)] for d, _ in blocks if d > 0}
+    far_rows = {d: [refs.pop(0) for _ in halves] for d, _ in blocks if d > 0}
     far = {(d, p): [refs.pop(0) for _ in range(parts[d, p])] for d, ps in blocks for p in ps}
-    sums_in = None if first else [refs.pop(0), refs.pop(0)]
+    sums_in = None if first else [refs.pop(0) for _ in halves]
     sums_out = refs
     count = rows[0].shape[0]
 
@@ -73,6 +73,7 @@
         return jnp.concatenate([r[...] for r in parts], axis=0)
 
     own = stack(rows)
+    row = row_energy[halves[0] * count : (halves[-1] + 1) * count, :]
     weights = []
     for d, ps in blocks:
         direct = lax.dot_general(
@@ -87,11 +88,11 @@
             swapped = direct
         for k, p in enumerate(ps):
             cut = slice(k * count, (k + 1) * count)
-            gap = pair_energy[d : d + 1, :] - row_energy[...] - col_energy[p : p + 1, :]
+            gap = pair_energy[d : d + 1, :] - row - col_energy[p : p + 1, :]
             weights.append(((2.0 * direct[:, cut] - swapped[:, cut]) / gap).astype(jnp.bfloat16))
     weights = jnp.concatenate(weights, axis=1)
     columns = stack([r for d, ps in blocks for p in ps for r in far[d, p]])
-    for half in range(CORES):
+    for half in range(len(halves)):
         part = jnp.dot(
             weights[half * count : (half + 1) * count], columns, preferred_element_type=jnp.float32
         )
@@ -212,25 +213,25 @@
     tables = energies()
     total = jax.ShapeDtypeStruct((width, aux_width), f32)
 
-    def add(blocks, sums):
-        operands = [*tables, own, other[0]]
+    def add(blocks, sums, halves=tuple(range(CORES))):
+        operands = [*tables, *[(own, other[0])[h] for h in halves]]
         operands += [part for p in needed(blocks) for part in held[0, p]]
         for d, _ in blocks:
-            operands += [line[d], other[d]] if d > 0 else []
+            operands += [(line[d], other[d])[h] for h in halves] if d > 0 else []
         operands += [part for d, ps in blocks for p in ps for part in held[d, p]]
         aliases = {}
         if sums is not None:
-            aliases = {len(operands) + k: k for k in range(CORES)}
+            aliases = {len(operands) + k: k for k in range(len(halves))}
             operands += list(sums)
         count = sum(len(ps) for _, ps in blocks)
         return pl.pallas_call(
-            functools.partial(contract, blocks, parts, sums is None),
-            out_shape=(total, total),
+            functools.partial(contract, blocks, parts, sums is None, halves),
+            out_shape=(total,) * len(halves),
             in_specs=[whole] * len(operands),
-            out_specs=(whole, whole),
+            out_specs=(whole,) * len(halves),
             input_output_aliases=aliases,
             cost_estimate=pl.CostEstimate(
-                flops=2 * 3 * count * CORES * width * width * aux_width,
+                flops=2 * 3 * count * len(halves) * width * width * aux_width,
                 bytes_accessed=count * width * aux_width * 4,
                 transcendentals=0,
             ),
@@ -249,8 +250,11 @@
         ((3, xs + ys),),
     )
     sums = None
-    for blocks in groups:
+    for blocks in groups[:-1]:
         sums = add(blocks, sums)
+    (away,) = add(groups[-1], sums[1:], (1,))
+    (kept,) = add(groups[-1], sums[:1], (0,))
+    sums = [kept, away]
     sums = [sums[0], from_core(sums[1])]
 
     pieces = parts[0, cs[0]]

time: 102 us -> 106 us (1.039)
  Pallas kernels: 18 us -> 22.1 us
  waiting for transfers between devices: 48.5 us -> 47.4 us
    pallas_call x5 -> x6, Pallas kernels: 13.2 us -> 16.4 us  [add(): pl.pallas_call(functools.partial(contract, blocks, parts, sums is None, h...]
    ppermute x7, waiting for transfers between devices: 26.2 us -> 23.8 us  [from_occ(): lax.ppermute(block, 'occ', [(partner(i, step, occ_count), i) for i in ran...]
    ppermute x7, waiting for transfers between devices: 9.73 us -> 10.9 us  [from_va(): lax.ppermute(block, 'va', [((i - step) % va_count, i) for i in range(va_c...]
    unnamed x44 -> x42, local copies, waits for them, and re-layouts: 8.57 us -> 7.75 us
  transfers between devices with their start and end apart: 30 -> 30, of which waited for: 10 -> 10; matrix products, arithmetic and copies ran while one was open for 0% -> 0% of each run, Pallas kernels for 13% -> 17%
where the time goes in v4:
time: 106 us; the launch traced here: 105 us
  waiting for transfers between devices  47.4 us (45%)
  starting transfers between devices  27.6 us (26%)
  Pallas kernels  22.1 us (21%)
  local copies, waits for them, and re-layouts  7.82 us (7%)
    ppermute x7, waiting for transfers between devices, from_occ(): lax.ppermute(block, 'occ', [(partner(i, step, occ_count), i) for i in ran...  23.8 us
    pallas_call x6, Pallas kernels, add(): pl.pallas_call(functools.partial(contract, blocks, parts, sums is None, h...  16.4 us
    ppermute x7, waiting for transfers between devices, from_vb(): lax.ppermute(block, 'vb', [((i - move) % vb_count, i) for i in range(vb_c...  12.6 us
    ppermute x7, waiting for transfers between devices, from_va(): lax.ppermute(block, 'va', [((i - step) % va_count, i) for i in range(va_c...  10.9 us
    ppermute x7, starting transfers between devices, from_vb(): lax.ppermute(block, 'vb', [((i - move) % vb_count, i) for i in range(vb_c...  10.2 us
    ppermute x7, starting transfers between devices, from_occ(): lax.ppermute(block, 'occ', [(partner(i, step, occ_count), i) for i in ran...  9.44 us
    unnamed x42, local copies, waits for them, and re-layouts  7.75 us
    ppermute x7, starting transfers between devices, from_va(): lax.ppermute(block, 'va', [((i - step) % va_count, i) for i in range(va_c...  7.29 us
  transfers between devices with their start and end apart: 30, of which 10 were waited for; matrix products, arithmetic and copies ran while one was open for 0% of the time, Pallas kernels for 17%

profile of v4, /device:TPU:0, one launch (start us, length us, event | category | flops | bytes accessed | tf_op | source)
XLA Modules:
  0.0 105.1 jit_solution(3850200723218195783)
XLA Ops:
  0.0 3.0 %collective-permute-start.9 = (bf16[128,2048]{1,0:T(8,128)(2,1)}, bf16[128,2048]{1,0:T(8,128)(2,1)S(1)}, u32[]{:S(2)}, u32[]{:S(2)}) collective-permute-start(bf16[128,2048]{1,0:T(8,128)(2,1)} %bitcast.3), channel_id=1, source_target_pairs={{2,0},{3,1},{0,2},{1,3},{6,4},{7,5},{4,6},{5,7},{10,8},{11,9},{8,1... | collective-permute-start | bytes 1572872 | tf_op jit(solution)/shard_map/ppermute | solution.py:153
  3.0 1.5 %collective-permute-start.2 = (bf16[128,2048]{1,0:T(8,128)(2,1)}, bf16[128,2048]{1,0:T(8,128)(2,1)S(1)}, u32[]{:S(2)}, u32[]{:S(2)}) collective-permute-start(bf16[128,2048]{1,0:T(8,128)(2,1)} %bitcast.4), channel_id=1, source_target_pairs={{4,0},{0,4},{5,1},{1,5},{6,2},{2,6},{7,3},{3,7},{12,8},{8,12},{13,... | collective-permute-start | bytes 1572872 | tf_op jit(solution)/shard_map/ppermute | solution.py:149
  4.5 2.6 %collective-permute-start = (bf16[128,2048]{1,0:T(8,128)(2,1)}, bf16[128,2048]{1,0:T(8,128)(2,1)S(1)}, u32[]{:S(2)}, u32[]{:S(2)}) collective-permute-start(bf16[128,2048]{1,0:T(8,128)(2,1)} %bitcast.5), channel_id=1, source_target_pairs={{16,0},{24,8},{0,16},{8,24},{17,1},{25,9},{1,17},{9,25},{18,2},{26... | collective-permute-start | bytes 1572872 | tf_op jit(solution)/shard_map/ppermute | solution.py:159
  7.1 1.6 %collective-permute-start.19 = (bf16[128,2048]{1,0:T(8,128)(2,1)}, bf16[128,2048]{1,0:T(8,128)(2,1)S(1)}, u32[]{:S(2)}, u32[]{:S(2)}) collective-permute-start(bf16[128,2048]{1,0:T(8,128)(2,1)} %bitcast.7), channel_id=1, source_target_pairs={{8,0},{0,8},{24,16},{16,24},{9,1},{1,9},{25,17},{17,25},{10,2},{2,... | collective-permute-start | bytes 1572872 | tf_op jit(solution)/shard_map/ppermute | solution.py:159
  8.7 6.5 %collective-permute-done.9.refs_7_.refs_6_.refs_4_ = bf16[128,2048]{1,0:T(8,128)(2,1)S(1)} collective-permute-done((bf16[128,2048]{1,0:T(8,128)(2,1)}, bf16[128,2048]{1,0:T(8,128)(2,1)S(1)}, u32[]{:S(2)}, u32[]{:S(2)}) %collective-permute-start.9) | collective-permute-done | bytes 524320 | tf_op jit(solution)/shard_map/ppermute | solution.py:153
  15.1 1.8 %collective-permute-start.10 = (bf16[64,2048]{1,0:T(8,128)(2,1)S(1)}, bf16[64,2048]{1,0:T(8,128)(2,1)}, u32[]{:S(2)}, u32[]{:S(2)}) collective-permute-start(bf16[64,2048]{1,0:T(8,128)(2,1)S(1)} %slice.18), channel_id=1, source_target_pairs={{4,0},{0,4},{5,1},{1,5},{6,2},{2,6},{7,3},{3,7},{12,8},{8,12},{13,... | collective-permute-start | bytes 786440 | tf_op jit(solution)/shard_map/ppermute | solution.py:149
  17.0 1.6 %collective-permute-start.3 = (bf16[64,2048]{1,0:T(8,128)(2,1)S(1)}, bf16[64,2048]{1,0:T(8,128)(2,1)S(1)}, u32[]{:S(2)}, u32[]{:S(2)}) collective-permute-start(bf16[64,2048]{1,0:T(8,128)(2,1)S(1)} %slice.16), channel_id=1, source_target_pairs={{2,0},{3,1},{0,2},{1,3},{6,4},{7,5},{4,6},{5,7},{10,8},{11,9},{8,1... | collective-permute-start | bytes 786440 | tf_op jit(solution)/shard_map/ppermute | solution.py:153
  18.6 11.5 %collective-permute-done.refs_8_.refs_10_ = bf16[128,2048]{1,0:T(8,128)(2,1)S(1)} collective-permute-done((bf16[128,2048]{1,0:T(8,128)(2,1)}, bf16[128,2048]{1,0:T(8,128)(2,1)S(1)}, u32[]{:S(2)}, u32[]{:S(2)}) %collective-permute-start) | collective-permute-done | bytes 524320 | tf_op jit(solution)/shard_map/ppermute | solution.py:159
  31.7 0.9 collective-permute-start.25
  32.7 1.5 %collective-permute-start.26 = (bf16[64,2048]{1,0:T(8,128)(2,1)S(1)}, bf16[64,2048]{1,0:T(8,128)(2,1)S(1)}, u32[]{:S(2)}, u32[]{:S(2)}) collective-permute-start(bf16[64,2048]{1,0:T(8,128)(2,1)S(1)} %get-tuple-element.28), channel_id=1, source_target_pairs={{2,0},{3,1},{0,2},{1,3},{6,4},{7,5},{4,6},{5,7},{10,8},{11,9},{8,1... | collective-permute-start | bytes 786440 | tf_op jit(solution)/shard_map/ppermute | solution.py:153
  34.2 5.1 %collective-permute-done.12.refs_13_ = bf16[64,2048]{1,0:T(8,128)(2,1)S(1)} collective-permute-done((bf16[64,2048]{1,0:T(8,128)(2,1)S(1)}, bf16[64,2048]{1,0:T(8,128)(2,1)S(1)}, u32[]{:S(2)}, u32[]{:S(2)}) %collective-permute-start.12) | collective-permute-done | bytes 262176 | tf_op jit(solution)/shard_map/ppermute | solution.py:153
  40.7 4.7 %collective-permute-done.25.refs_11_ = bf16[64,2048]{1,0:T(8,128)(2,1)S(1)} collective-permute-done((bf16[64,2048]{1,0:T(8,128)(2,1)S(1)}, bf16[64,2048]{1,0:T(8,128)(2,1)S(1)}, u32[]{:S(2)}, u32[]{:S(2)}) %collective-permute-start.25) | collective-permute-done | bytes 262176 | tf_op jit(solution)/shard_map/ppermute | solution.py:149
  46.2 1.5 %collective-permute-start.28 = (bf16[128,2048]{1,0:T(8,128)(2,1)S(1)}, bf16[128,2048]{1,0:T(8,128)(2,1)S(1)}, u32[]{:S(2)}, u32[]{:S(2)}) collective-permute-start(bf16[128,2048]{1,0:T(8,128)(2,1)S(1)} %collective-permute-done.19.refs_8_.refs_10_), channel_id=1, source_target_pairs={{2,0},{3,1},{0,2},{1,3},{6,4},{7,5},{4,6},{5,7},{10,8},{11,9},{8,1... | collective-permute-start | bytes 1572872 | tf_op jit(solution)/shard_map/ppermute | solution.py:153
  50.7 3.7 %collective-permute-done.27.refs_11_ = bf16[128,2048]{1,0:T(8,128)(2,1)S(1)} collective-permute-done((bf16[128,2048]{1,0:T(8,128)(2,1)S(1)}, bf16[128,2048]{1,0:T(8,128)(2,1)S(1)}, u32[]{:S(2)}, u32[]{:S(2)}) %collective-permute-start.27) | collective-permute-done | bytes 524320 | tf_op jit(solution)/shard_map/ppermute | solution.py:149
  55.2 1.8 %collective-permute-start.24 = (bf16[64,2048]{1,0:T(8,128)(2,1)S(1)}, bf16[64,2048]{1,0:T(8,128)(2,1)}, u32[]{:S(2)}, u32[]{:S(2)}) collective-permute-start(bf16[64,2048]{1,0:T(8,128)(2,1)S(1)} %collective-permute-done.3.refs_9_.refs_7_.refs_5_), channel_id=1, source_target_pairs={{8,0},{0,8},{24,16},{16,24},{9,1},{1,9},{25,17},{17,25},{10,2},{2,... | collective-permute-start | bytes 786440 | tf_op jit(solution)/shard_map/ppermute | solution.py:159
  59.1 1.5 %collective-permute-start.17 = (bf16[128,2048]{1,0:T(8,128)(2,1)S(1)}, bf16[128,2048]{1,0:T(8,128)(2,1)}, u32[]{:S(2)}, u32[]{:S(2)}) collective-permute-start(bf16[128,2048]{1,0:T(8,128)(2,1)S(1)} %collective-permute-done.1.refs_12_.refs_18_.refs_6_.refs_4_), channel_id=1, source_target_pairs={{2,0},{3,1},{0,2},{1,3},{6,4},{7,5},{4,6},{5,7},{10,8},{11,9},{8,1... | collective-permute-start | bytes 1572872 | tf_op jit(solution)/shard_map/ppermute | solution.py:153
  60.6 2.5 %shard_map.55 = (f32[4,128]{1,0:T(4,128)}, f32[256,128]{1,0:T(8,128)}, f32[8,128]{1,0:T(8,128)}) custom-call(s32[8,128]{1,0:T(8,128)} %bitcast.19, f32[1024]{0:T(1024)} %vir_ref.1, s32[4]{0:T(128)} %occ_index_ref.1, f32[4]{0:T(128)} %occ_ref.1), custom_call_target="tpu_custom_call" | custom-call | flops 3145728 | bytes 262144 | tf_op jit(solution)/shard_map/pallas_call | solution.py:198
  63.2 1.5 %collective-permute-start.13 = (bf16[64,2048]{1,0:T(8,128)(2,1)}, bf16[64,2048]{1,0:T(8,128)(2,1)S(1)}, u32[]{:S(2)}, u32[]{:S(2)}) collective-permute-start(bf16[64,2048]{1,0:T(8,128)(2,1)} %copy-done.12), channel_id=1, source_target_pairs={{4,0},{0,4},{5,1},{1,5},{6,2},{2,6},{7,3},{3,7},{12,8},{8,12},{13,... | collective-permute-start | bytes 786440 | tf_op jit(solution)/shard_map/ppermute | solution.py:149
  65.2 0.9 copy-done.1
  66.8 2.5 %shard_map.56 = (f32[128,2048]{1,0:T(8,128)S(1)}, f32[128,2048]{1,0:T(8,128)S(1)}) custom-call(f32[4,128]{1,0:T(4,128)S(1)} %copy-done.19, f32[256,128]{1,0:T(8,128)S(1)} %copy-done.1, f32[8,128]{1,0:T(8,128)S(1)} %copy-done.18, bf16[128,2048]{1,0:T(8,128)(2,1)S(1)} %bitcast.8, bf16[128,2048]{1,0:T(8,128)(2,1)S(1)} %collective-permute-done.18.refs_4_.refs_3_, ...), custom_call_target="tpu_custom_call" | custom-call | flops 1610612736 | bytes 4194304 | tf_op jit(solution)/shard_map/pallas_call | solution.py:227
  70.0 2.1 %shard_map.57 = (f32[128,2048]{1,0:T(8,128)S(1)}, f32[128,2048]{1,0:T(8,128)S(1)}) custom-call(f32[4,128]{1,0:T(4,128)S(1)} %copy-done.20, f32[256,128]{1,0:T(8,128)S(1)} %copy-done.1, f32[8,128]{1,0:T(8,128)S(1)} %copy-done.18, bf16[128,2048]{1,0:T(8,128)(2,1)S(1)} %bitcast.10, ...), custom_call_target="tpu_custom_call", output_to_operand_aliasing={{0}: (13, {}), {1}: (14, {})} | custom-call | flops 1207959552 | bytes 3145728 | tf_op jit(solution)/shard_map/pallas_call | solution.py:227
  72.2 3.1 %shard_map.58 = (f32[128,2048]{1,0:T(8,128)S(1)}, f32[128,2048]{1,0:T(8,128)S(1)}) custom-call(f32[4,128]{1,0:T(4,128)S(1)} %copy-done.20, f32[256,128]{1,0:T(8,128)S(1)} %copy-done.1, f32[8,128]{1,0:T(8,128)S(1)} %copy-done.18, bf16[128,2048]{1,0:T(8,128)(2,1)S(1)} %bitcast.12, ...), custom_call_target="tpu_custom_call", output_to_operand_aliasing={{0}: (15, {}), {1}: (16, {})} | custom-call | flops 1207959552 | bytes 3145728 | tf_op jit(solution)/shard_map/pallas_call | solution.py:227
  75.3 2.5 %collective-permute-done.13.refs_16_ = bf16[64,2048]{1,0:T(8,128)(2,1)S(1)} collective-permute-done((bf16[64,2048]{1,0:T(8,128)(2,1)}, bf16[64,2048]{1,0:T(8,128)(2,1)S(1)}, u32[]{:S(2)}, u32[]{:S(2)}) %collective-permute-start.13) | collective-permute-done | bytes 262176 | tf_op jit(solution)/shard_map/ppermute | solution.py:149
  77.7 1.1 %collective-permute-done.6.refs_17_ = bf16[64,2048]{1,0:T(8,128)(2,1)S(1)} collective-permute-done((bf16[64,2048]{1,0:T(8,128)(2,1)}, bf16[64,2048]{1,0:T(8,128)(2,1)S(1)}, u32[]{:S(2)}, u32[]{:S(2)}) %collective-permute-start.6) | collective-permute-done | bytes 262176 | tf_op jit(solution)/shard_map/ppermute | solution.py:153
  78.8 3.9 %shard_map.59 = (f32[128,2048]{1,0:T(8,128)S(1)}, f32[128,2048]{1,0:T(8,128)S(1)}) custom-call(f32[4,128]{1,0:T(4,128)S(1)} %copy-done.20, f32[256,128]{1,0:T(8,128)S(1)} %copy-done.1, f32[8,128]{1,0:T(8,128)S(1)} %copy-done.18, bf16[128,2048]{1,0:T(8,128)(2,1)S(1)} %bitcast.14, ...), custom_call_target="tpu_custom_call", output_to_operand_aliasing={{0}: (19, {}), {1}: (20, {})} | custom-call | flops 1207959552 | bytes 3145728 | tf_op jit(solution)/shard_map/pallas_call | solution.py:227
  82.7 2.4 %shard_map.62 = f32[128,2048]{1,0:T(8,128)S(1)} custom-call(f32[4,128]{1,0:T(4,128)S(1)} %copy-done.20, f32[256,128]{1,0:T(8,128)S(1)} %copy-done.1, f32[8,128]{1,0:T(8,128)S(1)} %copy-done.18, bf16[128,2048]{1,0:T(8,128)(2,1)S(1)} %collective-permute-done.18.refs_4_.refs_3_, ...), custom_call_target="tpu_custom_call", output_to_operand_aliasing={{}: (9, {})} | custom-call | flops 402653184 | bytes 2097152 | tf_op jit(solution)/shard_map/pallas_call | solution.py:227
  85.5 1.8 %collective-permute-start.7 = (bf16[64,2048]{1,0:T(8,128)(2,1)S(1)}, bf16[64,2048]{1,0:T(8,128)(2,1)S(1)}, u32[]{:S(2)}, u32[]{:S(2)}) collective-permute-start(bf16[64,2048]{1,0:T(8,128)(2,1)S(1)} %collective-permute-done.6.refs_17_), channel_id=1, source_target_pairs={{8,0},{0,8},{24,16},{16,24},{9,1},{1,9},{25,17},{17,25},{10,2},{2,... | collective-permute-start | bytes 786440 | tf_op jit(solution)/shard_map/ppermute | solution.py:159
  87.3 7.2 %collective-permute-done.14.refs_7_ = bf16[64,2048]{1,0:T(8,128)(2,1)S(1)} collective-permute-done((bf16[64,2048]{1,0:T(8,128)(2,1)S(1)}, bf16[64,2048]{1,0:T(8,128)(2,1)S(1)}, u32[]{:S(2)}, u32[]{:S(2)}) %collective-permute-start.14) | collective-permute-done | bytes 262176 | tf_op jit(solution)/shard_map/ppermute | solution.py:159
  95.0 4.6 %collective-permute-done.7.refs_7_ = bf16[64,2048]{1,0:T(8,128)(2,1)S(1)} collective-permute-done((bf16[64,2048]{1,0:T(8,128)(2,1)S(1)}, bf16[64,2048]{1,0:T(8,128)(2,1)S(1)}, u32[]{:S(2)}, u32[]{:S(2)}) %collective-permute-start.7) | collective-permute-done | bytes 262176 | tf_op jit(solution)/shard_map/ppermute | solution.py:159
  99.6 2.3 %shard_map.60.refs_9_ = f32[128,2048]{1,0:T(8,128)S(1)} custom-call(f32[4,128]{1,0:T(4,128)S(1)} %copy-done.20, f32[256,128]{1,0:T(8,128)S(1)} %copy-done.1, f32[8,128]{1,0:T(8,128)S(1)} %copy-done.18, bf16[128,2048]{1,0:T(8,128)(2,1)S(1)} %bitcast.16, ...), custom_call_target="tpu_custom_call", output_to_operand_aliasing={{}: (9, {})} | custom-call | flops 402653184 | bytes 2097152 | tf_op jit(solution)/shard_map/pallas_call | solution.py:227
  101.9 1.6 %shard_map.61.refs_9_ = f32[128,2048]{1,0:T(8,128)S(1)} custom-call(f32[4,128]{1,0:T(4,128)S(1)} %copy-done.20, f32[256,128]{1,0:T(8,128)S(1)} %copy-done.1, f32[8,128]{1,0:T(8,128)S(1)} %copy-done.18, bf16[128,2048]{1,0:T(8,128)(2,1)S(1)} %bitcast.17, bf16[128,2048]{1,0:T(8,128)(2,1)S(1)} %collective-permute-done.1.refs_12_.refs_18_.refs_6_.refs_4_, ...), custom_call_target="tpu_custom_call" | custom-call | flops 201326592 | bytes 1048576 | tf_op jit(solution)/shard_map/pallas_call | solution.py:276
  103.5 1.6 %shard_map.63 = f32[128,2048]{1,0:T(8,128)} custom-call(f32[4,128]{1,0:T(4,128)S(1)} %copy-done.20, f32[256,128]{1,0:T(8,128)S(1)} %copy-done.1, f32[8,128]{1,0:T(8,128)S(1)} %copy-done.18, bf16[128,2048]{1,0:T(8,128)(2,1)S(1)} %bitcast.18, bf16[128,2048]{1,0:T(8,128)(2,1)S(1)} %collective-permute-done.1.refs_12_.refs_18_.refs_6_.refs_4_, ...), custom_call_target="tpu_custom_call" | custom-call | flops 201326592 | bytes 1048576 | tf_op jit(solution)/shard_map/pallas_call | solution.py:276
  (82 shorter events, 12.5 us)
Async XLA Ops:
  0.0 15.1 %collective-permute-start.9 = (bf16[128,2048]{1,0:T(8,128)(2,1)}, bf16[128,2048]{1,0:T(8,128)(2,1)S(1)}, u32[]{:S(2)}, u32[]{:S(2)}) collective-permute-start(bf16[128,2048]{1,0:T(8,128)(2,1)} %bitcast.3), channel_id=1, source_target_pairs={{2,0},{3,1},{0,2},{1,3},{6,4},{7,5},{4,6},{5,7},{10,8},{11,9},{8,1... | collective-permute-start | bytes 1572872 | tf_op jit(solution)/shard_map/ppermute | solution.py:153
  3.0 13.9 %collective-permute-start.2 = (bf16[128,2048]{1,0:T(8,128)(2,1)}, bf16[128,2048]{1,0:T(8,128)(2,1)S(1)}, u32[]{:S(2)}, u32[]{:S(2)}) collective-permute-start(bf16[128,2048]{1,0:T(8,128)(2,1)} %bitcast.4), channel_id=1, source_target_pairs={{4,0},{0,4},{5,1},{1,5},{6,2},{2,6},{7,3},{3,7},{12,8},{8,12},{13,... | collective-permute-start | bytes 1572872 | tf_op jit(solution)/shard_map/ppermute | solution.py:149
  4.5 25.6 %collective-permute-start = (bf16[128,2048]{1,0:T(8,128)(2,1)}, bf16[128,2048]{1,0:T(8,128)(2,1)S(1)}, u32[]{:S(2)}, u32[]{:S(2)}) collective-permute-start(bf16[128,2048]{1,0:T(8,128)(2,1)} %bitcast.5), channel_id=1, source_target_pairs={{16,0},{24,8},{0,16},{8,24},{17,1},{25,9},{1,17},{9,25},{18,2},{26... | collective-permute-start | bytes 1572872 | tf_op jit(solution)/shard_map/ppermute | solution.py:159
  7.1 23.6 %collective-permute-start.18 = (bf16[128,2048]{1,0:T(8,128)(2,1)}, bf16[128,2048]{1,0:T(8,128)(2,1)S(1)}, u32[]{:S(2)}, u32[]{:S(2)}) collective-permute-start(bf16[128,2048]{1,0:T(8,128)(2,1)} %bitcast.6), channel_id=1, source_target_pairs={{1,0},{0,1},{3,2},{2,3},{5,4},{4,5},{7,6},{6,7},{9,8},{8,9},{11,10... | collective-permute-start | bytes 1572872 | tf_op jit(solution)/shard_map/ppermute | solution.py:156
  7.1 24.7 %collective-permute-start.19 = (bf16[128,2048]{1,0:T(8,128)(2,1)}, bf16[128,2048]{1,0:T(8,128)(2,1)S(1)}, u32[]{:S(2)}, u32[]{:S(2)}) collective-permute-start(bf16[128,2048]{1,0:T(8,128)(2,1)} %bitcast.7), channel_id=1, source_target_pairs={{8,0},{0,8},{24,16},{16,24},{9,1},{1,9},{25,17},{17,25},{10,2},{2,... | collective-permute-start | bytes 1572872 | tf_op jit(solution)/shard_map/ppermute | solution.py:159
  15.1 17.6 %collective-permute-start.10 = (bf16[64,2048]{1,0:T(8,128)(2,1)S(1)}, bf16[64,2048]{1,0:T(8,128)(2,1)}, u32[]{:S(2)}, u32[]{:S(2)}) collective-permute-start(bf16[64,2048]{1,0:T(8,128)(2,1)S(1)} %slice.18), channel_id=1, source_target_pairs={{4,0},{0,4},{5,1},{1,5},{6,2},{2,6},{7,3},{3,7},{12,8},{8,12},{13,... | collective-permute-start | bytes 786440 | tf_op jit(solution)/shard_map/ppermute | solution.py:149
  17.0 48.2 %copy-start = (bf16[1,128,2048]{2,1,0:T(8,128)(2,1)S(1)}, bf16[1,128,2048]{2,1,0:T(8,128)(2,1)}, u32[]{:S(2)}) copy-start(bf16[1,128,2048]{2,1,0:T(8,128)(2,1)} %param.5) | copy-start | bytes 1572868
  17.0 17.3 %collective-permute-start.3 = (bf16[64,2048]{1,0:T(8,128)(2,1)S(1)}, bf16[64,2048]{1,0:T(8,128)(2,1)S(1)}, u32[]{:S(2)}, u32[]{:S(2)}) collective-permute-start(bf16[64,2048]{1,0:T(8,128)(2,1)S(1)} %slice.16), channel_id=1, source_target_pairs={{2,0},{3,1},{0,2},{1,3},{6,4},{7,5},{4,6},{5,7},{10,8},{11,9},{8,1... | collective-permute-start | bytes 786440 | tf_op jit(solution)/shard_map/ppermute | solution.py:153
  30.1 9.2 %collective-permute-start.12 = (bf16[64,2048]{1,0:T(8,128)(2,1)S(1)}, bf16[64,2048]{1,0:T(8,128)(2,1)S(1)}, u32[]{:S(2)}, u32[]{:S(2)}) collective-permute-start(bf16[64,2048]{1,0:T(8,128)(2,1)S(1)} %get-tuple-element.27), channel_id=1, source_target_pairs={{2,0},{3,1},{0,2},{1,3},{6,4},{7,5},{4,6},{5,7},{10,8},{11,9},{8,1... | collective-permute-start | bytes 786440 | tf_op jit(solution)/shard_map/ppermute | solution.py:153
  30.7 9.4 %collective-permute-start.5 = (bf16[64,2048]{1,0:T(8,128)(2,1)S(1)}, bf16[64,2048]{1,0:T(8,128)(2,1)}, u32[]{:S(2)}, u32[]{:S(2)}) collective-permute-start(bf16[64,2048]{1,0:T(8,128)(2,1)S(1)} %get-tuple-element.28), channel_id=1, source_target_pairs={{4,0},{0,4},{5,1},{1,5},{6,2},{2,6},{7,3},{3,7},{12,8},{8,12},{13,... | collective-permute-start | bytes 786440 | tf_op jit(solution)/shard_map/ppermute | solution.py:149
  31.7 13.7 %collective-permute-start.25 = (bf16[64,2048]{1,0:T(8,128)(2,1)S(1)}, bf16[64,2048]{1,0:T(8,128)(2,1)S(1)}, u32[]{:S(2)}, u32[]{:S(2)}) collective-permute-start(bf16[64,2048]{1,0:T(8,128)(2,1)S(1)} %get-tuple-element.27), channel_id=1, source_target_pairs={{4,0},{0,4},{5,1},{1,5},{6,2},{2,6},{7,3},{3,7},{12,8},{8,12},{13,... | collective-permute-start | bytes 786440 | tf_op jit(solution)/shard_map/ppermute | solution.py:149
  32.7 15.8 %collective-permute-start.26 = (bf16[64,2048]{1,0:T(8,128)(2,1)S(1)}, bf16[64,2048]{1,0:T(8,128)(2,1)S(1)}, u32[]{:S(2)}, u32[]{:S(2)}) collective-permute-start(bf16[64,2048]{1,0:T(8,128)(2,1)S(1)} %get-tuple-element.28), channel_id=1, source_target_pairs={{2,0},{3,1},{0,2},{1,3},{6,4},{7,5},{4,6},{5,7},{10,8},{11,9},{8,1... | collective-permute-start | bytes 786440 | tf_op jit(solution)/shard_map/ppermute | solution.py:153
  34.2 14.9 %collective-permute-start.20 = (bf16[128,2048]{1,0:T(8,128)(2,1)S(1)}, bf16[128,2048]{1,0:T(8,128)(2,1)S(1)}, u32[]{:S(2)}, u32[]{:S(2)}) collective-permute-start(bf16[128,2048]{1,0:T(8,128)(2,1)S(1)} %collective-permute-done.19.refs_8_.refs_10_), channel_id=1, source_target_pairs={{1,0},{0,1},{3,2},{2,3},{5,4},{4,5},{7,6},{6,7},{9,8},{8,9},{11,10... | collective-permute-start | bytes 1572872 | tf_op jit(solution)/shard_map/ppermute | solution.py:156
  39.3 15.1 %collective-permute-start.27 = (bf16[128,2048]{1,0:T(8,128)(2,1)S(1)}, bf16[128,2048]{1,0:T(8,128)(2,1)S(1)}, u32[]{:S(2)}, u32[]{:S(2)}) collective-permute-start(bf16[128,2048]{1,0:T(8,128)(2,1)S(1)} %collective-permute-done.19.refs_8_.refs_10_), channel_id=1, source_target_pairs={{4,0},{0,4},{5,1},{1,5},{6,2},{2,6},{7,3},{3,7},{12,8},{8,12},{13,... | collective-permute-start | bytes 1572872 | tf_op jit(solution)/shard_map/ppermute | solution.py:149
  40.0 16.9 %collective-permute-start.1 = (bf16[128,2048]{1,0:T(8,128)(2,1)S(1)}, bf16[128,2048]{1,0:T(8,128)(2,1)S(1)}, u32[]{:S(2)}, u32[]{:S(2)}) collective-permute-start(bf16[128,2048]{1,0:T(8,128)(2,1)S(1)} %collective-permute-done.refs_8_.refs_10_), channel_id=1, source_target_pairs={{8,0},{0,8},{24,16},{16,24},{9,1},{1,9},{25,17},{17,25},{10,2},{2,... | collective-permute-start | bytes 1572872 | tf_op jit(solution)/shard_map/ppermute | solution.py:159
  46.2 10.8 %collective-permute-start.28 = (bf16[128,2048]{1,0:T(8,128)(2,1)S(1)}, bf16[128,2048]{1,0:T(8,128)(2,1)S(1)}, u32[]{:S(2)}, u32[]{:S(2)}) collective-permute-start(bf16[128,2048]{1,0:T(8,128)(2,1)S(1)} %collective-permute-done.19.refs_8_.refs_10_), channel_id=1, source_target_pairs={{2,0},{3,1},{0,2},{1,3},{6,4},{7,5},{4,6},{5,7},{10,8},{11,9},{8,1... | collective-permute-start | bytes 1572872 | tf_op jit(solution)/shard_map/ppermute | solution.py:153
  49.2 9.1 %collective-permute-start.21 = (bf16[128,2048]{1,0:T(8,128)(2,1)S(1)}, bf16[128,2048]{1,0:T(8,128)(2,1)S(1)}, u32[]{:S(2)}, u32[]{:S(2)}) collective-permute-start(bf16[128,2048]{1,0:T(8,128)(2,1)S(1)} %collective-permute-done.refs_8_.refs_10_), channel_id=1, source_target_pairs={{1,0},{0,1},{3,2},{2,3},{5,4},{4,5},{7,6},{6,7},{9,8},{8,9},{11,10... | collective-permute-start | bytes 1572872 | tf_op jit(solution)/shard_map/ppermute | solution.py:156
  50.0 13.2 %collective-permute-start.23 = (bf16[64,2048]{1,0:T(8,128)(2,1)}, bf16[64,2048]{1,0:T(8,128)(2,1)}, u32[]{:S(2)}, u32[]{:S(2)}) collective-permute-start(bf16[64,2048]{1,0:T(8,128)(2,1)} %collective-permute-done.10.refs_8_.refs_6_.refs_5_), channel_id=1, source_target_pairs={{8,0},{0,8},{24,16},{16,24},{9,1},{1,9},{25,17},{17,25},{10,2},{2,... | collective-permute-start | bytes 786440 | tf_op jit(solution)/shard_map/ppermute | solution.py:159
  55.2 9.5 %collective-permute-start.24 = (bf16[64,2048]{1,0:T(8,128)(2,1)S(1)}, bf16[64,2048]{1,0:T(8,128)(2,1)}, u32[]{:S(2)}, u32[]{:S(2)}) collective-permute-start(bf16[64,2048]{1,0:T(8,128)(2,1)S(1)} %collective-permute-done.3.refs_9_.refs_7_.refs_5_), channel_id=1, source_target_pairs={{8,0},{0,8},{24,16},{16,24},{9,1},{1,9},{25,17},{17,25},{10,2},{2,... | collective-permute-start | bytes 786440 | tf_op jit(solution)/shard_map/ppermute | solution.py:159
  57.0 21.8 %collective-permute-start.22 = (bf16[128,2048]{1,0:T(8,128)(2,1)S(1)}, bf16[128,2048]{1,0:T(8,128)(2,1)}, u32[]{:S(2)}, u32[]{:S(2)}) collective-permute-start(bf16[128,2048]{1,0:T(8,128)(2,1)S(1)} %collective-permute-done.1.refs_12_.refs_18_.refs_6_.refs_4_), channel_id=1, source_target_pairs={{1,0},{0,1},{3,2},{2,3},{5,4},{4,5},{7,6},{6,7},{9,8},{8,9},{11,10... | collective-permute-start | bytes 1572872 | tf_op jit(solution)/shard_map/ppermute | solution.py:156
  57.8 24.9 %collective-permute-start.16 = (bf16[128,2048]{1,0:T(8,128)(2,1)S(1)}, bf16[128,2048]{1,0:T(8,128)(2,1)}, u32[]{:S(2)}, u32[]{:S(2)}) collective-permute-start(bf16[128,2048]{1,0:T(8,128)(2,1)S(1)} %collective-permute-done.1.refs_12_.refs_18_.refs_6_.refs_4_), channel_id=1, source_target_pairs={{4,0},{0,4},{5,1},{1,5},{6,2},{2,6},{7,3},{3,7},{12,8},{8,12},{13,... | collective-permute-start | bytes 1572872 | tf_op jit(solution)/shard_map/ppermute | solution.py:149
  59.1 23.6 %collective-permute-start.17 = (bf16[128,2048]{1,0:T(8,128)(2,1)S(1)}, bf16[128,2048]{1,0:T(8,128)(2,1)}, u32[]{:S(2)}, u32[]{:S(2)}) collective-permute-start(bf16[128,2048]{1,0:T(8,128)(2,1)S(1)} %collective-permute-done.1.refs_12_.refs_18_.refs_6_.refs_4_), channel_id=1, source_target_pairs={{2,0},{3,1},{0,2},{1,3},{6,4},{7,5},{4,6},{5,7},{10,8},{11,9},{8,1... | collective-permute-start | bytes 1572872 | tf_op jit(solution)/shard_map/ppermute | solution.py:153
  63.2 14.5 %collective-permute-start.13 = (bf16[64,2048]{1,0:T(8,128)(2,1)}, bf16[64,2048]{1,0:T(8,128)(2,1)S(1)}, u32[]{:S(2)}, u32[]{:S(2)}) collective-permute-start(bf16[64,2048]{1,0:T(8,128)(2,1)} %copy-done.12), channel_id=1, source_target_pairs={{4,0},{0,4},{5,1},{1,5},{6,2},{2,6},{7,3},{3,7},{12,8},{8,12},{13,... | collective-permute-start | bytes 786440 | tf_op jit(solution)/shard_map/ppermute | solution.py:149
  64.7 14.1 %collective-permute-start.6 = (bf16[64,2048]{1,0:T(8,128)(2,1)}, bf16[64,2048]{1,0:T(8,128)(2,1)S(1)}, u32[]{:S(2)}, u32[]{:S(2)}) collective-permute-start(bf16[64,2048]{1,0:T(8,128)(2,1)} %collective-permute-done.5.refs_12_), channel_id=1, source_target_pairs={{2,0},{3,1},{0,2},{1,3},{6,4},{7,5},{4,6},{5,7},{10,8},{11,9},{8,1... | collective-permute-start | bytes 786440 | tf_op jit(solution)/shard_map/ppermute | solution.py:153
  66.8 2.5 %copy-start.11 = (bf16[128,2048]{1,0:T(8,128)(2,1)S(1)}, bf16[128,2048]{1,0:T(8,128)(2,1)}, u32[]{:S(2)}) copy-start(bf16[128,2048]{1,0:T(8,128)(2,1)} %copy-done.10) | copy-start | bytes 1572868
  85.2 18.4 %collective-permute-start.29 = (f32[128,2048]{1,0:T(8,128)S(1)}, f32[128,2048]{1,0:T(8,128)S(1)}, u32[]{:S(2)}, u32[]{:S(2)}) collective-permute-start(f32[128,2048]{1,0:T(8,128)S(1)} %shard_map.62), channel_id=1, source_target_pairs={{1,0},{0,1},{3,2},{2,3},{5,4},{4,5},{7,6},{6,7},{9,8},{8,9},{11,10... | collective-permute-start | bytes 3145736 | tf_op jit(solution)/shard_map/ppermute | solution.py:156
  85.2 9.2 %collective-permute-start.14 = (bf16[64,2048]{1,0:T(8,128)(2,1)S(1)}, bf16[64,2048]{1,0:T(8,128)(2,1)S(1)}, u32[]{:S(2)}, u32[]{:S(2)}) collective-permute-start(bf16[64,2048]{1,0:T(8,128)(2,1)S(1)} %collective-permute-done.13.refs_16_), channel_id=1, source_target_pairs={{8,0},{0,8},{24,16},{16,24},{9,1},{1,9},{25,17},{17,25},{10,2},{2,... | collective-permute-start | bytes 786440 | tf_op jit(solution)/shard_map/ppermute | solution.py:159
  85.5 14.1 %collective-permute-start.7 = (bf16[64,2048]{1,0:T(8,128)(2,1)S(1)}, bf16[64,2048]{1,0:T(8,128)(2,1)S(1)}, u32[]{:S(2)}, u32[]{:S(2)}) collective-permute-start(bf16[64,2048]{1,0:T(8,128)(2,1)S(1)} %collective-permute-done.6.refs_17_), channel_id=1, source_target_pairs={{8,0},{0,8},{24,16},{16,24},{9,1},{1,9},{25,17},{17,25},{10,2},{2,... | collective-permute-start | bytes 786440 | tf_op jit(solution)/shard_map/ppermute | solution.py:159
  87.3 14.5 %collective-permute-start.11 = (bf16[64,2048]{1,0:T(8,128)(2,1)}, bf16[64,2048]{1,0:T(8,128)(2,1)S(1)}, u32[]{:S(2)}, u32[]{:S(2)}) collective-permute-start(bf16[64,2048]{1,0:T(8,128)(2,1)} %collective-permute-done.10.refs_8_.refs_6_.refs_5_), channel_id=1, source_target_pairs={{1,0},{0,1},{3,2},{2,3},{5,4},{4,5},{7,6},{6,7},{9,8},{8,9},{11,10... | collective-permute-start | bytes 786440 | tf_op jit(solution)/shard_map/ppermute | solution.py:156
  94.5 7.4 %collective-permute-start.15 = (bf16[64,2048]{1,0:T(8,128)(2,1)S(1)}, bf16[64,2048]{1,0:T(8,128)(2,1)S(1)}, u32[]{:S(2)}, u32[]{:S(2)}) collective-permute-start(bf16[64,2048]{1,0:T(8,128)(2,1)S(1)} %collective-permute-done.14.refs_7_), channel_id=1, source_target_pairs={{1,0},{0,1},{3,2},{2,3},{5,4},{4,5},{7,6},{6,7},{9,8},{8,9},{11,10... | collective-permute-start | bytes 786440 | tf_op jit(solution)/shard_map/ppermute | solution.py:156
  94.5 9.0 %collective-permute-start.4 = (bf16[64,2048]{1,0:T(8,128)(2,1)S(1)}, bf16[64,2048]{1,0:T(8,128)(2,1)S(1)}, u32[]{:S(2)}, u32[]{:S(2)}) collective-permute-start(bf16[64,2048]{1,0:T(8,128)(2,1)S(1)} %collective-permute-done.3.refs_9_.refs_7_.refs_5_), channel_id=1, source_target_pairs={{1,0},{0,1},{3,2},{2,3},{5,4},{4,5},{7,6},{6,7},{9,8},{8,9},{11,10... | collective-permute-start | bytes 786440 | tf_op jit(solution)/shard_map/ppermute | solution.py:156
  99.6 4.0 %collective-permute-start.8 = (bf16[64,2048]{1,0:T(8,128)(2,1)S(1)}, bf16[64,2048]{1,0:T(8,128)(2,1)S(1)}, u32[]{:S(2)}, u32[]{:S(2)}) collective-permute-start(bf16[64,2048]{1,0:T(8,128)(2,1)S(1)} %collective-permute-done.7.refs_7_), channel_id=1, source_target_pairs={{1,0},{0,1},{3,2},{2,3},{5,4},{4,5},{7,6},{6,7},{9,8},{8,9},{11,10... | collective-permute-start | bytes 786440 | tf_op jit(solution)/shard_map/ppermute | solution.py:156
  (19 other events, 26.6 us)
